TPU v7x, 32 devices: a whole 2x2x4 slice. The times are simulated.
32 devices in a mesh: dp: 16 (over z, y, x), mp: 2 (over core).
Axes of the slice: x: 2, y: 2, z: 4, core: 2. Of those that a mesh axis runs over, the one named last changes fastest.
Arguments:
- prompt_hidden: float32 [2048, 5120], P('dp'), may hold values from -6 to 6
- key_weight: float32 [5120, 1024], P('dp', 'mp'), may hold values from -0.078125 to 0.078125
- value_weight: float32 [5120, 1024], P('dp', 'mp'), may hold values from -0.078125 to 0.078125
- queries: float32 [4096, 5120], P('dp', 'mp'), may hold values from -21 to 21
- keys_resp: float32 [4096, 1024], P('dp', 'mp'), may hold values from -21 to 21
- response_value_rows: float32 [4096, 1024], P('dp', 'mp'), may hold values from -6 to 6
- grad_out: float32 [4096, 5120], P('dp', 'mp'), may hold values from -6 to 6
- resp_prompt: int32 [16], P('dp'), may hold values from 0 to 15, as said below
- resp_len: int32 [16], P('dp'), may hold values from 2 to 256
Outputs:
- attn_out: float32 [4096, 5120], P('dp', 'mp')
- grad_queries: float32 [4096, 5120], P('dp', 'mp')
- grad_keys_resp: float32 [4096, 1024], P('dp', 'mp')
- grad_values_resp: float32 [4096, 1024], P('dp', 'mp')
- grad_hidden: float32 [2048, 5120], P('dp', 'mp')
- grad_w_key: float32 [5120, 1024], P('dp', 'mp')
- grad_w_value: float32 [5120, 1024], P('dp', 'mp')
Inputs may be any that keep to these rules, and one draw needn't show every extreme that they name: `resp_prompt`: every one of the 16 prompts has exactly 1 responses.
All inputs are finite; a program needn't handle non-finite values.
Results may differ from a plain program's by a relative error of at most 0.0003.
Values sent between devices are 32-bit elements; how exact they have to be, the bound alone decides.
No kernel may reach another device: no remote copies, remote signals or barrier semaphores. Data moves between devices by JAX's collectives and lax.ppermute only.
A program may use at most 192 MiB of HBM per device.

v0:
```python
import math

import jax
import jax.numpy as jnp
from jax import lax
from jax.sharding import PartitionSpec as P

QUERY_HEADS = 40
KEY_VALUE_HEADS = 8
HEAD_SIZE = 128
PROMPT_COUNT = 16
RESPONSE_LENGTH = 256


masked_value = -1e30


def per_device(
    prompt_hidden,
    key_weight,
    value_weight,
    queries,
    keys_resp,
    response_value_rows,
    grad_out,
    resp_prompt,
    resp_len,
):
    highest_precision = lax.Precision.HIGHEST
    score_scale = 1.0 / math.sqrt(HEAD_SIZE)
    full_key, full_value = (
        lax.all_gather(key_weight, "dp", axis=0, tiled=True),
        lax.all_gather(value_weight, "dp", axis=0, tiled=True),
    )
    own_keys = jnp.dot(
        prompt_hidden, full_key, precision=highest_precision, preferred_element_type=jnp.float32
    )
    own_values = jnp.dot(
        prompt_hidden, full_value, precision=highest_precision, preferred_element_type=jnp.float32
    )
    all_keys, all_values = (
        lax.all_gather(own_keys, "dp", axis=0, tiled=True),
        lax.all_gather(own_values, "dp", axis=0, tiled=True),
    )
    width = key_weight.shape[1]
    groups = width // HEAD_SIZE
    queries_per_group = QUERY_HEADS // KEY_VALUE_HEADS
    plen = all_keys.shape[0] // PROMPT_COUNT
    number = queries.shape[0] // RESPONSE_LENGTH
    prompt_key_rows = all_keys.reshape(PROMPT_COUNT, plen, groups, HEAD_SIZE)[resp_prompt]
    prompt_value_rows = all_values.reshape(PROMPT_COUNT, plen, groups, HEAD_SIZE)[resp_prompt]
    query = queries.reshape(number, RESPONSE_LENGTH, groups, queries_per_group, HEAD_SIZE)
    key_cat = jnp.concatenate(
        [prompt_key_rows, keys_resp.reshape(number, RESPONSE_LENGTH, groups, HEAD_SIZE)], 1
    )
    value_cat = jnp.concatenate(
        [
            prompt_value_rows,
            response_value_rows.reshape(number, RESPONSE_LENGTH, groups, HEAD_SIZE),
        ],
        1,
    )
    rows = jnp.arange(RESPONSE_LENGTH, dtype=jnp.int32)[None, :, None]
    cols = jnp.arange(plen + RESPONSE_LENGTH, dtype=jnp.int32)[None, None, :]
    offset = cols - plen
    allowed = (cols < plen) | (offset <= rows) & (offset < resp_len[:, None, None])
    scores = (
        jnp.einsum("rigqd,rjgd->rgqij", query, key_cat, precision=highest_precision) * score_scale
    )
    scores = jnp.where(allowed[:, None, None], scores, masked_value)
    top = jnp.max(scores, axis=-1, keepdims=True)
    expo = jnp.exp(scores - top)
    attn_prob = expo / jnp.sum(expo, axis=-1, keepdims=True)
    result = jnp.einsum("rgqij,rjgd->rigqd", attn_prob, value_cat, precision=highest_precision)
    valid = (jnp.arange(RESPONSE_LENGTH, dtype=jnp.int32)[None, :] < resp_len[:, None])[
        :, :, None, None, None
    ]
    result = jnp.where(valid, result, 0.0)
    upstream = jnp.where(
        valid, grad_out.reshape(number, RESPONSE_LENGTH, groups, queries_per_group, HEAD_SIZE), 0.0
    )
    grad_prob = jnp.einsum("rigqd,rjgd->rgqij", upstream, value_cat, precision=highest_precision)
    inner = jnp.einsum("rigqd,rigqd->rgqi", upstream, result, precision=highest_precision)[
        ..., None
    ]
    grad_scores = attn_prob * (grad_prob - inner) * score_scale
    grad_query = jnp.einsum("rgqij,rjgd->rigqd", grad_scores, key_cat, precision=highest_precision)
    grad_keycat = jnp.einsum("rgqij,rigqd->rjgd", grad_scores, query, precision=highest_precision)
    grad_valuecat = jnp.einsum(
        "rgqij,rigqd->rjgd", attn_prob, upstream, precision=highest_precision
    )
    one_hot = (resp_prompt[:, None] == jnp.arange(PROMPT_COUNT, dtype=jnp.int32)[None, :]).astype(
        jnp.float32
    )
    key_terms = jnp.einsum(
        "rp,rx->px",
        one_hot,
        grad_keycat[:, :plen].reshape(number, plen * width),
        precision=highest_precision,
    ).reshape(PROMPT_COUNT * plen, width)
    value_terms = jnp.einsum(
        "rp,rx->px",
        one_hot,
        grad_valuecat[:, :plen].reshape(number, plen * width),
        precision=highest_precision,
    ).reshape(PROMPT_COUNT * plen, width)
    key_own, value_own = (
        lax.psum_scatter(key_terms, "dp", scatter_dimension=0, tiled=True),
        lax.psum_scatter(value_terms, "dp", scatter_dimension=0, tiled=True),
    )
    joined = jnp.concatenate([key_own, value_own], 1)
    summed = lax.psum_scatter(
        jnp.einsum(
            "tc,tk->ck",
            prompt_hidden,
            joined,
            precision=highest_precision,
            preferred_element_type=jnp.float32,
        ),
        "dp",
        scatter_dimension=0,
        tiled=True,
    )
    hidden_terms = jnp.einsum(
        "tk,ck->tc",
        key_own,
        full_key,
        precision=highest_precision,
        preferred_element_type=jnp.float32,
    )
    hidden_terms = hidden_terms + jnp.einsum(
        "tk,ck->tc",
        value_own,
        full_value,
        precision=highest_precision,
        preferred_element_type=jnp.float32,
    )
    grad_hidden = lax.psum_scatter(hidden_terms, "mp", scatter_dimension=1, tiled=True)
    out_width = groups * queries_per_group * HEAD_SIZE
    return (
        result.reshape(number * RESPONSE_LENGTH, out_width),
        grad_query.reshape(number * RESPONSE_LENGTH, out_width),
        grad_keycat[:, plen:].reshape(number * RESPONSE_LENGTH, width),
        grad_valuecat[:, plen:].reshape(number * RESPONSE_LENGTH, width),
        grad_hidden,
        summed[:, :width],
        summed[:, width:],
    )


def solution(mesh):
    in_specs = (
        P("dp", None),
        P("dp", "mp"),
        P("dp", "mp"),
        P("dp", "mp"),
        P("dp", "mp"),
        P("dp", "mp"),
        P("dp", "mp"),
        P("dp"),
        P("dp"),
    )
    out_specs = (
        P("dp", "mp"),
        P("dp", "mp"),
        P("dp", "mp"),
        P("dp", "mp"),
        P("dp", "mp"),
        P("dp", "mp"),
        P("dp", "mp"),
    )
    return jax.shard_map(
        per_device, mesh=mesh, in_specs=in_specs, out_specs=out_specs, check_vma=False
    )
```

profile of v0, /device:TPU:9, one launch (start us, length us, event | category | flops | bytes accessed | tf_op | source)
XLA Modules:
  0.0 1200.1 jit_solution(8724659214657297586)
XLA Ops:
  7.2 0.7 all-gather.5.cloned.1.call-update
  8.0 0.7 all-gather.9.cloned.1.call-update
  8.7 133.1 %all-gather.5.cloned.1.call-done = f32[5120,512]{1,0:T(8,128)} async-done(((f32[320,512]{1,0:T(8,128)}), f32[5120,512]{1,0:T(8,128)}) %all-gather.5.cloned.1.call-update) | async-done | bytes 10485776 | tf_op jit(solution)/shard_map/all_gather | solution.py:33
  141.8 9.2 fusion.46
  151.2 123.8 %all-gather.9.cloned.1.call-done = f32[5120,512]{1,0:T(8,128)} async-done(((f32[320,512]{1,0:T(8,128)}), f32[5120,512]{1,0:T(8,128)}) %all-gather.9.cloned.1.call-update) | async-done | bytes 10485776 | tf_op jit(solution)/shard_map/all_gather | solution.py:32
  275.0 9.2 fusion.47
  285.6 1.0 copy.61
  286.6 1.2 copy.62
  287.8 2.0 copy.59
  289.9 3.2 copy.63
  293.1 3.2 copy.66
  296.6 57.2 %all-gather.7.cloned.1.call-done = f32[2048,512]{1,0:T(8,128)} async-done(((f32[128,512]{1,0:T(8,128)}), f32[2048,512]{1,0:T(8,128)}) %all-gather.7.cloned.1.call-update) | async-done | bytes 4194320 | tf_op jit(solution)/shard_map/all_gather | solution.py:43
  353.7 5.3 reshape.253
  359.1 72.6 %all-gather.11.cloned.1.call-done = f32[2048,512]{1,0:T(8,128)} async-done(((f32[128,512]{1,0:T(8,128)}), f32[2048,512]{1,0:T(8,128)}) %all-gather.11.cloned.1.call-update) | async-done | bytes 4194320 | tf_op jit(solution)/shard_map/all_gather | solution.py:42
  431.6 5.5 reshape.256
  437.1 1.8 constant_dynamic-slice_fusion
  438.9 1.8 copy.105
  440.7 9.3 fusion.9
  450.0 1.7 fusion.8
  451.7 8.8 fusion.21
  460.6 0.9 copy-done.9
  461.5 0.7 slice.49
  462.2 1.8 copy.74
  464.0 12.8 %fusion.12 = (f32[4,5,256]{2,1,0:T(8,128)S(1)}, f32[1,4,128,5,256]{4,2,3,1,0:T(8,128)}) fusion(f32[256,4,5,128]{0,3,2,1:T(8,128)} %bitcast.144, pred[256]{0:T(512)(128)(4,1)S(1)} %iota_compare_fusion.2, f32[4,5,256]{2,1,0:T(8,128)} %copy-done.13, f32[4,5,256]{2,1,0:T(8,128)S(1)} %get-tuple-element.54, f32[4,384,256,5]{2,1,3,0:T(8,128)} %copy-done.2, ...), kind=kOutput, calls=%fused_computation.16 | convolution fusion | flops 3030576128 | bytes 14053632 | tf_op jit(solution)/shard_map/rgqij,rjgd->rigqd/dot_general | solution.py:74
  476.9 8.7 fusion.2
  485.6 3.0 copy-done.1
  488.6 7.3 convolution_bitcast_fusion.1
  496.0 0.9 copy-done.5
  496.8 0.7 slice.48
  497.6 1.8 copy.73
  499.3 4.9 broadcast_multiply_fusion
  504.3 3.9 reshape.272
  508.2 4.0 reshape.270
  512.3 88.6 %reduce-scatter.9.cloned.1.call-done = f32[128,512]{1,0:T(8,128)} async-done(((f32[2048,512]{1,0:T(8,128)}), f32[128,512]{1,0:T(8,128)}) %reduce-scatter.9.cloned.1.call-update) | async-done | bytes 262160 | tf_op jit(solution)/shard_map/reduce_scatter | solution.py:109
  600.8 96.8 %reduce-scatter.7.cloned.1.call-done = f32[128,512]{1,0:T(8,128)} async-done(((f32[2048,512]{1,0:T(8,128)}), f32[128,512]{1,0:T(8,128)}) %reduce-scatter.7.cloned.1.call-update) | async-done | bytes 262160 | tf_op jit(solution)/shard_map/reduce_scatter | solution.py:108
  697.7 20.6 %convolution_bitcast_fusion = f32[5120,1024]{0,1:T(8,128)} fusion(f32[128,5120]{1,0:T(8,128)S(1)} %copy-done, f32[128,512]{1,0:T(8,128)} %reduce-scatter.9.cloned.1.call-done, f32[128,512]{1,0:T(8,128)} %reduce-scatter.7.cloned.1.call-done), kind=kOutput, calls=%fused_computation | convolution fusion | flops 8053194752 | bytes 24117248 | tf_op jit(solution)/shard_map/tc,tk->ck/dot_general | solution.py:113
  718.3 21.3 %copy.103 = f32[5120,1024]{1,0:T(8,128)} copy(f32[5120,1024]{0,1:T(8,128)} %convolution_bitcast_fusion) | data formatting | bytes 41943040
  739.7 13.7 %fusion.48 = f32[128,5120]{1,0:T(8,128)S(1)} fusion(f32[128,512]{1,0:T(8,128)} %reduce-scatter.7.cloned.1.call-done, f32[5120,512]{1,0:T(8,128)} %all-gather.9.cloned.1.call-done), kind=kOutput, calls=%fused_computation.60 | convolution fusion | flops 4026531840 | bytes 13369344 | tf_op jit(solution)/shard_map/tk,ck->tc/dot_general | solution.py:124
  753.4 15.3 %convolution_add_fusion = f32[128,5120]{1,0:T(8,128)} fusion(f32[128,5120]{1,0:T(8,128)S(1)} %fusion.48, f32[128,512]{1,0:T(8,128)S(1)} %copy-done.8, f32[5120,512]{1,0:T(8,128)} %all-gather.5.cloned.1.call-done), kind=kOutput, calls=%fused_computation.13 | convolution fusion | flops 4027187200 | bytes 15990784 | tf_op jit(solution)/shard_map/tk,ck->tc/dot_general | solution.py:131
  768.7 1.9 slice.47
  770.6 2.0 copy.78
  772.6 8.9 fusion.26
  781.5 3.3 copy.76
  784.8 3.2 copy.75
  788.0 1.0 copy.77
  789.0 382.3 %reduce-scatter.13.cloned.1.call-done = f32[320,1024]{1,0:T(8,128)} async-done(((f32[5120,1024]{1,0:T(8,128)}), f32[320,1024]{1,0:T(8,128)}) %reduce-scatter.13.cloned.1.call-update) | async-done | bytes 1310736
  1171.3 2.4 fusion.45
  1173.8 19.1 %reduce-scatter.11.cloned.1.call-done = f32[128,2560]{1,0:T(8,128)} async-done(((f32[128,5120]{1,0:T(8,128)}), f32[128,2560]{1,0:T(8,128)}) %reduce-scatter.11.cloned.1.call-update) | async-done | bytes 1310736 | tf_op jit(solution)/shard_map/reduce_scatter | solution.py:138
  (49 shorter events, 0.7 us)
Async XLA Ops:
  7.2 134.7 %copy-start = (f32[128,5120]{1,0:T(8,128)S(1)}, f32[128,5120]{1,0:T(8,128)}, u32[]{:S(2)}) copy-start(f32[128,5120]{1,0:T(8,128)} %param.9) | copy-start | bytes 7864324
  7.2 134.7 %all-gather.5.cloned.1.call-start = ((), (), s32[]{:S(2)}) async-start(), calls=%async_computation.4 | async-start | bytes 11141120 | tf_op jit(solution)/shard_map/all_gather | solution.py:33
  7.9 267.0 %all-gather.9.cloned.1.call-start = ((), (), s32[]{:S(2)}) async-start(), calls=%async_computation.6 | async-start | bytes 11141120 | tf_op jit(solution)/shard_map/all_gather | solution.py:32
  8.7 345.1 %all-gather.7.cloned.1.call-start = ((), (), s32[]{:S(2)}) async-start(), calls=%async_computation.5 | async-start | bytes 4456448 | tf_op jit(solution)/shard_map/all_gather | solution.py:43
  151.1 134.5 %copy-start.10 = (f32[256,512]{1,0:T(8,128)S(1)}, f32[256,512]{1,0:T(8,128)}, u32[]{:S(2)}) copy-start(f32[256,512]{1,0:T(8,128)} %param.13) | copy-start | bytes 1572868
  151.1 280.5 %all-gather.11.cloned.1.call-start = ((), (), s32[]{:S(2)}) async-start(), calls=%async_computation.7 | async-start | bytes 4456448 | tf_op jit(solution)/shard_map/all_gather | solution.py:42
  284.2 316.6 %reduce-scatter.9.cloned.1.call-start = ((), (), s32[]{:S(2)}) async-start(), calls=%async_computation.9 | async-start | bytes 4456448 | tf_op jit(solution)/shard_map/reduce_scatter | solution.py:109
  440.7 11.0 copy-start.6
  450.0 10.6 copy-start.2
  451.7 8.9 copy-start.13
  460.6 0.9 copy-start.9
  464.0 12.9 %copy-start.3 = (f32[4,384,256,5]{2,1,3,0:T(8,128)S(1)}, f32[4,384,256,5]{2,1,3,0:T(8,128)}, u32[]{:S(2)}) copy-start(f32[4,384,256,5]{2,1,3,0:T(8,128)} %copy-done.2) | copy-start | bytes 23592964
  464.0 12.9 %copy-start.7 = (f32[256,2560]{0,1:T(8,128)S(1)}, f32[256,2560]{0,1:T(8,128)}, u32[]{:S(2)}) copy-start(f32[256,2560]{0,1:T(8,128)} %copy.66) | copy-start | bytes 7864324
  464.0 12.9 %copy-start.11 = (f32[256,512]{0,1:T(8,128)S(1)}, f32[256,512]{0,1:T(8,128)}, u32[]{:S(2)}) copy-start(f32[256,512]{0,1:T(8,128)} %copy.59) | copy-start | bytes 1572868
  464.0 12.9 %copy-start.12 = (f32[1,128,4,128]{1,3,2,0:T(8,128)S(1)}, f32[1,128,4,128]{1,3,2,0:T(8,128)}, u32[]{:S(2)}) copy-start(f32[1,128,4,128]{1,3,2,0:T(8,128)} %copy.105) | copy-start | bytes 786436
  464.0 12.9 %copy-start.14 = (f32[4,5,256]{2,1,0:T(8,128)S(1)}, f32[4,5,256]{2,1,0:T(8,128)}, u32[]{:S(2)}) copy-start(f32[4,5,256]{2,1,0:T(8,128)} %copy-done.13) | copy-start | bytes 61444
  476.9 11.8 copy-start.4
  485.6 3.1 copy-start.1
  495.9 0.9 copy-start.5
  508.2 189.5 %reduce-scatter.7.cloned.1.call-start = ((), (), s32[]{:S(2)}) async-start(), calls=%async_computation.8 | async-start | bytes 4456448 | tf_op jit(solution)/shard_map/reduce_scatter | solution.py:108
  512.2 659.1 %reduce-scatter.13.cloned.1.call-start = ((), (), s32[]{:S(2)}) async-start(), calls=%async_computation.11 | async-start | bytes 22282240
  739.7 453.1 %reduce-scatter.11.cloned.1.call-start = ((), (), s32[]{:S(2)}) async-start(), calls=%async_computation.10 | async-start | bytes 3932160 | tf_op jit(solution)/shard_map/reduce_scatter | solution.py:138
  739.7 13.7 %copy-start.8 = (f32[128,512]{1,0:T(8,128)S(1)}, f32[128,512]{1,0:T(8,128)}, u32[]{:S(2)}) copy-start(f32[128,512]{1,0:T(8,128)} %reduce-scatter.9.cloned.1.call-done) | copy-start | bytes 786436
  781.5 6.5 slice-start
Sparse Core Ops, SparseCore 0:
  10.7 131.0 all-gather.4
  144.5 130.3 all-gather.8
  278.3 75.3 all-gather.6
  356.9 74.6 all-gather.10
  508.3 92.4 reduce-scatter.8
  603.0 94.6 reduce-scatter.6
  739.8 431.4 reduce-scatter.12
  1174.1 18.6 reduce-scatter.10
where the time goes:
time: 1210 us; the launch traced here: 1200 us
  waiting for transfers between devices  975 us (81%)
  matrix products  124 us (10%)
  local copies, waits for them, and re-layouts  78 us (6%)
  between operations  16.1 us (1%)
    unnamed x9, waiting for transfers between devices  384 us
    all_gather x1, waiting for transfers between devices, per_device(): lax.all_gather(value_weight, 'dp', axis=0, tiled=True)  133 us
    all_gather x1, waiting for transfers between devices, per_device(): lax.all_gather(key_weight, 'dp', axis=0, tiled=True)  124 us
    reduce_scatter x1, waiting for transfers between devices, per_device(): lax.psum_scatter(key_terms, 'dp', scatter_dimension=0, tiled=True)  96.8 us
    reduce_scatter x1, waiting for transfers between devices, per_device(): lax.psum_scatter(value_terms, 'dp', scatter_dimension=0, tiled=True)  88.6 us
    all_gather x1, waiting for transfers between devices, per_device(): lax.all_gather(own_keys, 'dp', axis=0, tiled=True)  72.6 us
    all_gather x1, waiting for transfers between devices, per_device(): lax.all_gather(own_values, 'dp', axis=0, tiled=True)  57.2 us
    unnamed x41, local copies, waits for them, and re-layouts  47 us
  transfers between devices with their start and end apart: 8, of which 8 were waited for; matrix products, arithmetic and copies ran while one was open for 8% of the time, Pallas kernels for 0%

commit v1 on v0

v1 whole, which is shorter than its diff:
```python
import functools
import math

import jax
import jax.numpy as jnp
from jax import lax
from jax.experimental import pallas as pl
from jax.experimental.pallas import tpu as pltpu
from jax.sharding import PartitionSpec as P

QUERY_HEADS = 40
KEY_VALUE_HEADS = 8
HEAD_SIZE = 128
PROMPT_COUNT = 16
RESPONSE_LENGTH = 256

masked_value = -1e30
HIGH = lax.Precision.HIGH
BOTH = ("dp", "mp")


def pairs_of(target):
    return [
        (c * 2 + m, target(c, m) * 2 + m)
        for c in range(16)
        for m in range(2)
        if target(c, m) is not None
    ]


def along_z(moves):
    return pairs_of(lambda c, m: moves[c >> 2] << 2 | c & 3 if c >> 2 in moves else None)


SECOND = pairs_of(lambda c, m: c ^ (2, 1)[m])
THIRD = pairs_of(lambda c, m: c ^ (1, 2)[m])
ACROSS = [along_z({z: z ^ k for z in range(4)}) for k in range(4)]
MIDDLE = along_z({1: 2, 2: 1})
INWARD = along_z({0: 1, 3: 2})
OUTWARD = along_z({1: 0, 2: 3})
SWAP = [(0, 1), (1, 0)]


def permute(x, pairs):
    return lax.ppermute(x, BOTH, pairs)


def spread(block):
    second = permute(block, SECOND)
    return [block, second, permute(block, THIRD), permute(second, THIRD)]


def gather_blocks(block):
    out = spread(block)
    for k in range(1, 4):
        out += spread(permute(block, ACROSS[k]))
    return out


def gathered_order(chip, core):
    inner = jnp.where(core == 0, jnp.array([0, 2, 1, 3]), jnp.array([0, 1, 2, 3]))
    return (chip ^ (jnp.arange(4)[:, None] * 4) ^ inner[None, :]).reshape(16)


def scatter_order(chip, core):
    z = chip // 4
    rows = jnp.array([[3, 2, 1, 0], [3, 2, 0, 1], [0, 1, 3, 2], [0, 1, 2, 3]])
    z_order = jnp.sum(jnp.where(jnp.arange(4)[:, None] == z, rows, 0), 0)
    inner = jnp.where(core == 0, jnp.array([3, 1, 2, 0]), jnp.array([3, 2, 1, 0]))
    return (z_order[:, None] * 4 + ((chip & 3) ^ inner)[None, :]).reshape(16)


def reduce_blocks(send, keep):
    part = []
    for k in range(4):
        rows = keep[k].shape[0] // 2
        come = permute(send[k], THIRD)
        passing = keep[k][:rows] + come[:rows]
        part.append(keep[k][rows:] + come[rows:] + permute(passing, SECOND))
    first = permute(part[0], INWARD)
    second = permute(part[1], INWARD)
    third = permute(part[2], INWARD)
    passed = permute(part[0] + first, MIDDLE)
    later = permute(part[1] + second, MIDDLE)
    last = permute(part[2] + passed, OUTWARD)
    return part[3] + third + later + last


def two_terms(x):
    upper = x.astype(jnp.bfloat16)
    return upper, (x - upper.astype(jnp.float32)).astype(jnp.bfloat16)


def dot(a, b, dims):
    return lax.dot_general(a, b, (dims, ((), ())), preferred_element_type=jnp.float32)


def dot_terms(a, b, dims=((1,), (0,))):
    return dot(a[0], b[0], dims) + (dot(a[0], b[1], dims) + dot(a[1], b[0], dims))


def dot_rows(a, b):
    dims = ((1,), (1,))
    return dot(jnp.concatenate(a, 1), jnp.concatenate([b[0], b[0]], 1), dims) + dot(a[0], b[1], dims)


def three_terms(x):
    first = x.astype(jnp.bfloat16)
    rest = x - first.astype(jnp.float32)
    second = rest.astype(jnp.bfloat16)
    return first, second, (rest - second.astype(jnp.float32)).astype(jnp.bfloat16)


def dot_rows_exact(a, b):
    a, b = three_terms(a), three_terms(b)
    dims = ((1,), (1,))
    pair = jnp.concatenate(a[:2], 1)
    small = dot(jnp.concatenate([a[2], a[0]], 1), jnp.concatenate([b[0], b[2]], 1), dims)
    small = small + dot(pair, jnp.concatenate([b[1], b[1]], 1), dims)
    return dot(pair, jnp.concatenate([b[0], b[0]], 1), dims) + small


VMEM_LIMIT = 56 << 20


def call(kernel, name, grid, in_specs, out_specs, out_shape, scalars=0, scratch=()):
    return pl.pallas_call(
        kernel,
        out_shape=[jax.ShapeDtypeStruct(*shape) for shape in out_shape],
        grid_spec=pltpu.PrefetchScalarGridSpec(
            num_scalar_prefetch=scalars,
            grid=grid,
            in_specs=in_specs,
            out_specs=out_specs,
            scratch_shapes=scratch,
        ),
        compiler_params=pltpu.CompilerParams(vmem_limit_bytes=VMEM_LIMIT),
        name=name,
    )


def whole(x):
    return pl.BlockSpec(x.shape, lambda *_: (0,) * x.ndim)


def turn_kernel(core, x, out):
    t = x[...].T
    count, half, _ = out.shape
    for c in range(count):
        own = t[2 * c * half : 2 * (c + 1) * half]
        out[c] = jnp.where(core[0] == 0, own[:half], own[half:])


def turn(core, hidden, chips):
    rows, model = hidden.shape
    half = model // chips // 2
    (out,) = call(
        turn_kernel,
        "turn",
        (chips // 2,),
        [pl.BlockSpec((rows, model // chips * 2), lambda i, *_: (0, i))],
        [pl.BlockSpec((2, half, rows), lambda i, *_: (i, 0, 0))],
        [((chips, half, rows), jnp.float32)],
        scalars=1,
    )(core, hidden)
    return out


def turn_back_kernel(core, own, other, out):
    first = core[0] == 0
    parts = []
    for c in range(own.shape[0]):
        x, y = own[c], other[c]
        parts += [jnp.where(first, x, y), jnp.where(first, y, x)]
    out[...] = jnp.concatenate(parts, 0).T


def turn_back(core, back, come):
    chips, half, rows = back.shape
    steps = chips // 4
    (out,) = call(
        turn_back_kernel,
        "turn_back",
        (steps,),
        [
            pl.BlockSpec((2, half, rows), lambda i, core: (core[0] * steps + i, 0, 0)),
            pl.BlockSpec((2, half, rows), lambda i, core: (i, 0, 0)),
        ],
        [pl.BlockSpec((rows, 4 * half), lambda i, *_: (0, i))],
        [((rows, chips * half), jnp.float32)],
        scalars=1,
    )(core, back, come)
    return out


def split_kernel(core, key, value, upper, lower):
    half = key.shape[0] // 2
    first = core[0] == 0
    for start, ref in ((0, key), (key.shape[1], value)):
        x, y = ref[:half], ref[half:]
        for row, part in ((0, jnp.where(first, x, y)), (half, jnp.where(first, y, x))):
            terms = two_terms(part)
            for out, term in ((upper, terms[0]), (lower, terms[1])):
                out[row : row + half, start : start + key.shape[1]] = term


def split_weights(core, key, value):
    shape = ((key.shape[0], 2 * key.shape[1]), jnp.bfloat16)
    out = pl.BlockSpec(shape[0], lambda *_: (0, 0))
    return call(
        split_kernel, "split_weights", (1,), [whole(key), whole(value)], [out] * 2, [shape] * 2, scalars=1
    )(core, key, value)


def project_kernel(index, *refs):
    own, other, (upper, lower), outs = refs[:4], refs[4:8], refs[8:10], refs[10:]
    x = jnp.concatenate(
        [
            jnp.concatenate([ref[0] for ref in own], 1),
            jnp.concatenate([ref[0] for ref in other], 1),
        ],
        0,
    )
    terms = dot_terms(two_terms(x), (upper[...], lower[...]), ((0,), (0,)))
    count = outs[0].shape[0]
    outs[0][...] = terms[:count]
    outs[1][...] = terms[count:]


def project(index, own, other, weight_terms):
    _, half, plen = own.shape
    columns = weight_terms[0].shape[1]
    picked = [
        pl.BlockSpec((1, half, plen), lambda i, index, q=q: (index[q], 0, 0)) for q in range(4)
    ]
    shape = ((2 * plen, columns), jnp.float32)
    return call(
        project_kernel,
        "project",
        (1,),
        picked * 2 + [whole(weight_terms[0])] * 2,
        [pl.BlockSpec(shape[0], lambda *_: (0, 0))] * 2,
        [shape] * 2,
        scalars=1,
    )(index, *([own] * 4), *([other] * 4), *weight_terms)


def hidden_grad_kernel(listed, *refs):
    blocks, (upper, lower), (keep, give) = refs[:-4], refs[-4:-2], refs[-2:]
    half, plen = keep.shape[1:]
    weights = upper[...], lower[...]
    for q in range(0, len(blocks), 2):
        x = two_terms(jnp.concatenate([blocks[q][...], blocks[q + 1][...]], 0))
        terms = dot_terms(weights, x, ((1,), (1,)))
        for i in range(2):
            part = terms[:, i * plen : (i + 1) * plen]
            keep[listed[q + i]] = part[:half]
            give[listed[q + i]] = part[half:]


def hidden_grad(listed, blocks, weight_terms):
    plen, columns = blocks[0].shape
    count, half = len(blocks), weight_terms[0].shape[0] // 2
    shape = ((count, half, plen), jnp.float32)
    return call(
        hidden_grad_kernel,
        "hidden_grad",
        (1,),
        [whole(blocks[0])] * count + [whole(weight_terms[0])] * 2,
        [pl.BlockSpec(shape[0], lambda *_: (0, 0, 0))] * 2,
        [shape] * 2,
        scalars=1,
    )(listed, *blocks, *weight_terms)


def weight_grad_kernel(listed, core, own, other, *refs):
    blocks, outs = refs[:-2], refs[-2:]
    half = own.shape[1]
    width = outs[0].shape[1]
    total = None
    for q in range(0, len(blocks), 4):
        x = jnp.concatenate(
            [jnp.concatenate([ref[listed[q + i]] for i in range(4)], 1) for ref in (own, other)], 0
        )
        g = jnp.concatenate([ref[...] for ref in blocks[q : q + 4]], 0)
        term = dot_terms(two_terms(x), two_terms(g))
        total = term if total is None else total + term
    x, y = total[:half], total[half:]
    first = core[0] == 0
    for row, part in ((0, jnp.where(first, x, y)), (half, jnp.where(first, y, x))):
        for out, start in zip(outs, (0, width)):
            out[row : row + half] = part[:, start : start + width]


def weight_grad(listed, core, own, other, blocks):
    plen, columns = blocks[0].shape
    shape = ((2 * own.shape[1], columns // 2), jnp.float32)
    return call(
        weight_grad_kernel,
        "weight_grad",
        (1,),
        [whole(own)] * 2 + [whole(blocks[0])] * len(blocks),
        [pl.BlockSpec(shape[0], lambda *_: (0, 0))] * 2,
        [shape] * 2,
        scalars=2,
    )(listed, core, own, other, *blocks)


SCALE = 1.0 / math.sqrt(HEAD_SIZE)
PER_GROUP = QUERY_HEADS // KEY_VALUE_HEADS


def stack(ref):
    size = ref.shape[1] // PER_GROUP
    return jnp.concatenate([ref[:, h * size : (h + 1) * size] for h in range(PER_GROUP)], 0)


def unstack(ref, x):
    rows, size = ref.shape[0], ref.shape[1] // PER_GROUP
    for h in range(PER_GROUP):
        ref[:, h * size : (h + 1) * size] = x[h * rows : (h + 1) * rows]


def save_columns(ref, first, second):
    rows = ref.shape[0]
    lane = lax.broadcasted_iota(jnp.int32, ref.shape, 1)
    out = jnp.zeros(ref.shape, jnp.float32)
    for start, column in ((0, first), (8, second)):
        for h in range(PER_GROUP):
            out = jnp.where(lane == start + h, column[h * rows : (h + 1) * rows], out)
    ref[...] = out


def load_column(ref, start):
    return jnp.concatenate([ref[:, start + h : start + h + 1] for h in range(PER_GROUP)], 0)


def row_number(shape, rows):
    return lax.broadcasted_iota(jnp.int32, shape, 0) % rows


def own_scores(length, query, keys, rows):
    scores = dot_rows_exact(query, keys) * SCALE
    j = lax.broadcasted_iota(jnp.int32, scores.shape, 1)
    return jnp.where((j <= row_number(scores.shape, rows)) & (j < length), scores, masked_value)


def open_kernel(length, q, k, v, total, stats):
    scores = own_scores(length[0], stack(q), k[...], q.shape[0])
    top = jnp.max(scores, -1, keepdims=True)
    expo = jnp.exp(scores - top)
    unstack(total, dot_terms(two_terms(expo), two_terms(v[...])))
    save_columns(stats, top, jnp.sum(expo, -1, keepdims=True))


def close_kernel(length, q, g, kp, vp, total, stats, out, grad_scores, stats_out, gk, gv):
    query, keys, values = stack(q), kp[...], vp[...]
    scores = dot_rows_exact(query, keys) * SCALE
    before = load_column(stats, 0)
    top = jnp.maximum(before, jnp.max(scores, -1, keepdims=True))
    weight = jnp.exp(before - top)
    expo = jnp.exp(scores - top)
    denominator = weight * load_column(stats, 8) + jnp.sum(expo, -1, keepdims=True)
    inverse = 1.0 / denominator
    prob = expo * inverse
    prob_terms, value_terms = two_terms(prob), two_terms(values)
    result = (weight * inverse) * stack(total) + dot_terms(prob_terms, value_terms)
    valid = row_number(result.shape, q.shape[0]) < length[0]
    result = jnp.where(valid, result, 0.0)
    upstream = jnp.where(valid, stack(g), 0.0)
    upstream_terms = two_terms(upstream)
    inner = jnp.sum(upstream * result, -1, keepdims=True)
    grad = prob * (dot_rows(upstream_terms, value_terms) - inner) * SCALE
    unstack(out, result)
    unstack(grad_scores, grad)
    save_columns(stats_out, top + jnp.log(denominator), inner)
    gk[...] = dot_terms(two_terms(grad), two_terms(query), ((0,), (0,)))
    gv[...] = dot_terms(prob_terms, upstream_terms, ((0,), (0,)))


def finish_kernel(length, q, g, k, v, kp, grad_scores, stats, gq, gk, gv):
    query, keys = stack(q), k[...]
    rows = q.shape[0]
    prob = jnp.exp(own_scores(length[0], query, keys, rows) - load_column(stats, 0))
    upstream = stack(g)
    upstream = jnp.where(row_number(upstream.shape, rows) < length[0], upstream, 0.0)
    upstream_terms = two_terms(upstream)
    grad = prob * (dot_rows(upstream_terms, two_terms(v[...])) - load_column(stats, 8)) * SCALE
    grad_terms = two_terms(grad)
    prompt_part = dot_terms(two_terms(stack(grad_scores)), two_terms(kp[...]))
    unstack(gq, prompt_part + dot_terms(grad_terms, two_terms(keys)))
    gk[...] = dot_terms(grad_terms, two_terms(query), ((0,), (0,)))
    gv[...] = dot_terms(two_terms(prob), upstream_terms, ((0,), (0,)))


def attention(kernel, name, groups, length, ins, outs):
    return call(
        kernel,
        name,
        (groups,),
        [
            pl.BlockSpec((x.shape[0], size), lambda i, *_, skip=skip: (0, skip + i))
            for x, size, skip in ins
        ],
        [pl.BlockSpec(shape, lambda i, *_: (0, i)) for shape in outs],
        [((rows, groups * size), jnp.float32) for rows, size in outs],
        scalars=1,
    )(length, *(x for x, _, _ in ins))


def take_blocks(x, index):
    return jnp.stack(
        [lax.dynamic_index_in_dim(x, index[j], keepdims=False) for j in range(index.shape[0])]
    )


def take_small(table, index):
    hit = index[..., None] == jnp.arange(table.shape[0])
    return jnp.sum(jnp.where(hit, table, 0), -1)


def per_device(
    short,
    prompt_hidden,
    key_weight,
    value_weight,
    queries,
    keys_resp,
    response_value_rows,
    grad_out,
    resp_prompt,
    resp_len,
):
    chips = lax.axis_size("dp")
    chip, core = lax.axis_index("dp"), lax.axis_index("mp")
    rows_own, model = prompt_hidden.shape
    slice_width = model // chips
    width = key_weight.shape[1]
    groups = width // HEAD_SIZE
    plen = rows_own * chips // PROMPT_COUNT
    tokens = queries.shape[0]
    responses = tokens * chips // RESPONSE_LENGTH
    assert tokens == RESPONSE_LENGTH
    short = short and responses == PROMPT_COUNT
    here = core.astype(jnp.int32)[None]
    wide = PER_GROUP * HEAD_SIZE

    if short:
        all_prompts = jnp.where(jnp.arange(chips) == chip, resp_prompt, 0)
        for pairs in (ACROSS[1], ACROSS[2], SECOND, THIRD):
            all_prompts = all_prompts + permute(all_prompts, pairs)
        mine = lax.all_to_all(turn(here, prompt_hidden, chips), "dp", 0, 0)
        weight_terms = split_weights(here, key_weight, value_weight)
    else:
        all_prompts = lax.all_gather(resp_prompt, "dp", axis=0, tiled=True)
        hidden = lax.all_to_all(
            prompt_hidden.reshape(rows_own, chips, slice_width).transpose(1, 0, 2), "dp", 0, 0
        )
        hidden = hidden.reshape(PROMPT_COUNT, plen, slice_width)
        weights = jnp.concatenate([key_weight, value_weight], 1)

    q = (queries, wide, 0)
    total, stats = attention(
        open_kernel,
        "open",
        groups,
        resp_len,
        [q, (keys_resp, HEAD_SIZE, 0), (response_value_rows, HEAD_SIZE, 0)],
        [(tokens, wide), (tokens, HEAD_SIZE)],
    )

    if short:
        mine, weight_terms, total, stats, all_prompts = lax.optimization_barrier(
            (mine, weight_terms, total, stats, all_prompts)
        )
        other = lax.ppermute(mine, "mp", SWAP)
        listed = take_small(all_prompts, scatter_order(chip, core))
        pairs = [project(listed[4 * k : 4 * k + 4], mine, other, weight_terms) for k in range(4)]
        prompt_rows = reduce_blocks([pair[0] for pair in pairs], [pair[1] for pair in pairs])
    else:
        terms = jnp.einsum("rtc,ck->rtk", take_blocks(hidden, all_prompts), weights, precision=HIGH)
        prompt_rows = lax.psum_scatter(
            terms.reshape(responses * plen, 2 * width), "dp", scatter_dimension=0, tiled=True
        )

    g = (grad_out, wide, 0)
    prompt_keys = (prompt_rows, HEAD_SIZE, 0)
    result, grad_scores, stats, own_k, own_v = attention(
        close_kernel,
        "close",
        groups,
        resp_len,
        [q, g, prompt_keys, (prompt_rows, HEAD_SIZE, groups), (total, wide, 0), (stats, HEAD_SIZE, 0)],
        [(tokens, wide), (tokens, PER_GROUP * plen), (tokens, HEAD_SIZE)] + [(plen, HEAD_SIZE)] * 2,
    )
    grad_query, grad_keys, grad_values = attention(
        finish_kernel,
        "finish",
        groups,
        resp_len,
        [q, g, (keys_resp, HEAD_SIZE, 0), (response_value_rows, HEAD_SIZE, 0), prompt_keys]
        + [(grad_scores, PER_GROUP * plen, 0), (stats, HEAD_SIZE, 0)],
        [(tokens, wide)] + [(tokens, HEAD_SIZE)] * 2,
    )

    own = jnp.concatenate([own_k, own_v], 1)
    if short:
        gathered = gather_blocks(own)
        gathered, grad_query, grad_keys, grad_values = lax.optimization_barrier(
            (gathered, grad_query, grad_keys, grad_values)
        )
        listed = take_small(all_prompts, gathered_order(chip, core))
        keep, give = hidden_grad(listed, gathered, weight_terms)
        back = lax.all_to_all(keep + lax.ppermute(give, "mp", SWAP), "dp", 0, 0)
        grad_w_key, grad_w_value = weight_grad(listed, here, mine, other, gathered)
        back, grad_w_key, grad_w_value = lax.optimization_barrier((back, grad_w_key, grad_w_value))
        leave = jnp.where(core == 0, back[chips // 2 :], back[: chips // 2])
        grad_hidden = turn_back(here, back, lax.ppermute(leave, "mp", SWAP))
    else:
        gathered = lax.all_gather(own, "dp", axis=0, tiled=True).reshape(responses, plen, 2 * width)
        summed = jnp.einsum(
            "rtc,rtk->ck", take_blocks(hidden, all_prompts), gathered, precision=HIGH
        )
        grad_w_key, grad_w_value = summed[:, :width], summed[:, width:]
        terms = jnp.einsum("rtk,ck->rtc", gathered, weights, precision=HIGH)
        numbers = jnp.arange(responses)
        same = all_prompts[:, None] == all_prompts[None, :]
        earlier = jnp.sum(same & (numbers[None, :] < numbers[:, None]), 1)
        hidden_terms = 0.0
        for i in range(responses // PROMPT_COUNT):
            hit = (all_prompts[None, :] == jnp.arange(PROMPT_COUNT)[:, None]) & (earlier[None, :] == i)
            place = jnp.sum(jnp.where(hit, numbers[None, :], 0), -1)
            hidden_terms = hidden_terms + take_blocks(terms, place)
        back = lax.all_to_all(hidden_terms.reshape(chips, rows_own, slice_width), "dp", 0, 0)
        back = back.transpose(1, 0, 2).reshape(rows_own, model)
        grad_hidden = lax.psum_scatter(back, "mp", scatter_dimension=1, tiled=True)
    return (
        result,
        grad_query,
        grad_keys,
        grad_values,
        grad_hidden,
        grad_w_key,
        grad_w_value,
    )


def solution(mesh):
    short = mesh.shape["dp"] == 16 and mesh.shape["mp"] == 2
    in_specs = (P("dp", None),) + (P("dp", "mp"),) * 6 + (P("dp"),) * 2
    out_specs = (P("dp", "mp"),) * 7
    return jax.shard_map(
        functools.partial(per_device, short),
        mesh=mesh,
        in_specs=in_specs,
        out_specs=out_specs,
        check_vma=False,
    )
```

time: 1210 us -> 334 us (0.28)
  waiting for transfers between devices: 975 us -> 166 us
  matrix products: 124 us -> 0 us
  Pallas kernels: 0 us -> 103 us
  local copies, waits for them, and re-layouts: 78 us -> 4.76 us
  starting transfers between devices: 0.32 us -> 51.5 us
  between operations: 16.1 us -> 2.36 us
    all_gather x4 -> x0, waiting for transfers between devices: 387 us -> none  [the longest x1 133 us: per_device(): lax.all_gather(value_weight, 'dp', axis=0, tiled=True)]
    unnamed x9 -> x0, waiting for transfers between devices: 384 us -> none
    reduce_scatter x3 -> x0, waiting for transfers between devices: 204 us -> none  [the longest x1 96.8 us: per_device(): lax.psum_scatter(key_terms, 'dp', scatter_dimension=0, tiled=True)]
    ppermute x0 -> x36, waiting for transfers between devices: none -> 145 us  [the longest x33 139 us: permute(): return lax.ppermute(x, BOTH, pairs)]
    dot_general x11 -> x0, matrix products: 124 us -> none  [the longest x1 20.6 us: per_device(): jnp.einsum('tc,tk->ck', prompt_hidden, joined, precision=highest_precisio...]
    pallas_call x0 -> x12, Pallas kernels: none -> 103 us  [the longest x3 48.9 us: attention(): call(kernel, name, (groups,), [pl.BlockSpec((x.shape[0], size), lambda i,...]
    unnamed x41 -> x55, local copies, waits for them, and re-layouts: 47 us -> 3 us
    ppermute x0 -> x36, starting transfers between devices: none -> 40.6 us  [the longest x33 36 us: permute(): return lax.ppermute(x, BOTH, pairs)]
  transfers between devices with their start and end apart: 8 -> 38, of which waited for: 8 -> 22; matrix products, arithmetic and copies ran while one was open for 8% -> 1% of each run, Pallas kernels for 0% -> 16%
where the time goes in v1:
time: 334 us; the launch traced here: 333 us
  waiting for transfers between devices  166 us (50%)
  Pallas kernels  103 us (31%)
  starting transfers between devices  51.5 us (15%)
  other arithmetic  5.45 us (2%)
  local copies, waits for them, and re-layouts  4.76 us (1%)
    ppermute x33, waiting for transfers between devices, permute(): return lax.ppermute(x, BOTH, pairs)  139 us
    pallas_call x3, Pallas kernels, attention(): call(kernel, name, (groups,), [pl.BlockSpec((x.shape[0], size), lambda i,...  48.9 us
    ppermute x33, starting transfers between devices, permute(): return lax.ppermute(x, BOTH, pairs)  36 us
    pallas_call x4, Pallas kernels, project(): call(project_kernel, 'project', (1,), picked * 2 + [whole(weight_terms[0]...  21.7 us
    all_to_all x1, waiting for transfers between devices, per_device(): back = lax.all_to_all(keep + lax.ppermute(give, 'mp', SWAP), 'dp', 0, 0)  20.1 us
    pallas_call x1, Pallas kernels, hidden_grad(): call(hidden_grad_kernel, 'hidden_grad', (1,), [whole(blocks[0])] * count...  10.2 us
    pallas_call x1, Pallas kernels, weight_grad(): call(weight_grad_kernel, 'weight_grad', (1,), [whole(own)] * 2 + [whole(b...  9.91 us
    all_to_all x1, starting transfers between devices, per_device(): mine = lax.all_to_all(turn(here, prompt_hidden, chips), 'dp', 0, 0)  6.8 us
  transfers between devices with their start and end apart: 38, of which 22 were waited for; matrix products, arithmetic and copies ran while one was open for 1% of the time, Pallas kernels for 16%

profile of v1, /device:TPU:9, one launch (start us, length us, event | category | flops | bytes accessed | tf_op | source)
XLA Modules:
  0.0 332.9 jit_solution(1458540519840660654)
XLA Ops:
  0.6 6.1 %turn.1 = f32[16,160,128]{2,1,0:T(8,128)} custom-call(s32[1]{0:T(128)} %bitcast.core, f32[128,5120]{1,0:T(8,128)} %x.1), custom_call_target="tpu_custom_call" | custom-call | tf_op jit(solution)/shard_map/turn/pallas_call | solution.py:157
  6.8 6.8 %all-to-all-start = ((f32[16,160,128]{2,1,0:T(8,128)}), f32[16,160,128]{2,1,0:T(8,128)S(1)}, u32[]{:S(2)}, u32[]{:S(2)}) async-start(f32[16,160,128]{2,1,0:T(8,128)} %turn.1), calls=%async_computation | async-start | bytes 2621440 | tf_op jit(solution)/shard_map/all_to_all | solution.py:452
  14.5 20.5 %collective-permute-done = s32[16]{0:T(128)S(1)} collective-permute-done((s32[16]{0:T(128)S(1)}, s32[16]{0:T(128)S(1)}, u32[]{:S(2)}, u32[]{:S(2)}) %collective-permute-start) | collective-permute-done | bytes 96 | tf_op jit(solution)/shard_map/ppermute | solution.py:45
  37.0 4.2 %collective-permute-done.1 = s32[16]{0:T(128)S(1)} collective-permute-done((s32[16]{0:T(128)S(1)}, s32[16]{0:T(128)S(1)}, u32[]{:S(2)}, u32[]{:S(2)}) %collective-permute-start.1) | collective-permute-done | bytes 96 | tf_op jit(solution)/shard_map/ppermute | solution.py:45
  42.3 2.6 split_weights.1
  44.8 1.9 collective-permute-start.3
  46.7 10.9 %open.1 = (f32[256,2560]{1,0:T(8,128)}, f32[256,512]{1,0:T(8,128)}) custom-call(s32[1]{0:T(128)S(6)} %copy.23.length, f32[256,2560]{1,0:T(8,128)} %q.5, f32[256,512]{1,0:T(8,128)} %k.3, f32[256,512]{1,0:T(8,128)} %v.3), custom_call_target="tpu_custom_call" | custom-call | tf_op jit(solution)/shard_map/open/pallas_call | solution.py:397
  57.6 2.0 collective-permute-start.4
  63.4 5.4 %project.7 = (f32[256,1024]{1,0:T(8,128)}, f32[256,1024]{1,0:T(8,128)}) custom-call(s32[4]{0:T(128)} %get-tuple-element.116.index, f32[16,160,128]{2,1,0:T(8,128)} %copy-done, f32[16,160,128]{2,1,0:T(8,128)} %copy-done, f32[16,160,128]{2,1,0:T(8,128)} %copy-done, f32[16,160,128]{2,1,0:T(8,128)} %copy-done, f32[16,160,128]{2,1,0:T(8,128)} %copy-done.1, ...), custom_call_target="tpu_custom_call" | custom-call | tf_op jit(solution)/shard_map/project/pallas_call | solution.py:237
  69.4 5.4 %project.6 = (f32[256,1024]{1,0:T(8,128)}, f32[256,1024]{1,0:T(8,128)}) custom-call(s32[4]{0:T(128)} %get-tuple-element.117.index, f32[16,160,128]{2,1,0:T(8,128)} %copy-done, f32[16,160,128]{2,1,0:T(8,128)} %copy-done, f32[16,160,128]{2,1,0:T(8,128)} %copy-done, f32[16,160,128]{2,1,0:T(8,128)} %copy-done, f32[16,160,128]{2,1,0:T(8,128)} %copy-done.1, ...), custom_call_target="tpu_custom_call" | custom-call | tf_op jit(solution)/shard_map/project/pallas_call | solution.py:237
  75.6 5.5 %project.5 = (f32[256,1024]{1,0:T(8,128)}, f32[256,1024]{1,0:T(8,128)}) custom-call(s32[4]{0:T(128)} %get-tuple-element.118.index, f32[16,160,128]{2,1,0:T(8,128)} %copy-done, f32[16,160,128]{2,1,0:T(8,128)} %copy-done, f32[16,160,128]{2,1,0:T(8,128)} %copy-done, f32[16,160,128]{2,1,0:T(8,128)} %copy-done, f32[16,160,128]{2,1,0:T(8,128)} %copy-done.1, ...), custom_call_target="tpu_custom_call" | custom-call | tf_op jit(solution)/shard_map/project/pallas_call | solution.py:237
  83.4 5.5 %project.4 = (f32[256,1024]{1,0:T(8,128)}, f32[256,1024]{1,0:T(8,128)}) custom-call(s32[4]{0:T(128)} %get-tuple-element.115.index, f32[16,160,128]{2,1,0:T(8,128)} %copy-done, f32[16,160,128]{2,1,0:T(8,128)} %copy-done, f32[16,160,128]{2,1,0:T(8,128)} %copy-done, f32[16,160,128]{2,1,0:T(8,128)} %copy-done, f32[16,160,128]{2,1,0:T(8,128)} %copy-done.1, ...), custom_call_target="tpu_custom_call" | custom-call | tf_op jit(solution)/shard_map/project/pallas_call | solution.py:237
  89.5 10.3 %collective-permute-done.10 = f32[256,1024]{1,0:T(8,128)S(1)} collective-permute-done((f32[256,1024]{1,0:T(8,128)}, f32[256,1024]{1,0:T(8,128)S(1)}, u32[]{:S(2)}, u32[]{:S(2)}) %collective-permute-start.10) | collective-permute-done | bytes 1048608 | tf_op jit(solution)/shard_map/ppermute | solution.py:45
  101.6 15.0 %collective-permute-done.7 = f32[256,1024]{1,0:T(8,128)S(1)} collective-permute-done((f32[256,1024]{1,0:T(8,128)}, f32[256,1024]{1,0:T(8,128)S(1)}, u32[]{:S(2)}, u32[]{:S(2)}) %collective-permute-start.7) | collective-permute-done | bytes 1048608 | tf_op jit(solution)/shard_map/ppermute | solution.py:45
  116.8 1.4 collective-permute-start.12
  118.7 3.7 %collective-permute-start.17 = (f32[128,1024]{1,0:T(8,128)S(1)}, f32[128,1024]{1,0:T(8,128)S(1)}, u32[]{:S(2)}, u32[]{:S(2)}) collective-permute-start(f32[128,1024]{1,0:T(8,128)S(1)} %add.113), channel_id=1, source_target_pairs={{8,16},{9,17},{10,18},{11,19},{12,20},{13,21},{14,22},{15,23},{16,... | collective-permute-start | bytes 1572872 | tf_op jit(solution)/shard_map/ppermute | solution.py:45
  122.3 10.6 %collective-permute-done.5 = f32[256,1024]{1,0:T(8,128)S(1)} collective-permute-done((f32[256,1024]{1,0:T(8,128)}, f32[256,1024]{1,0:T(8,128)S(1)}, u32[]{:S(2)}, u32[]{:S(2)}) %collective-permute-start.5) | collective-permute-done | bytes 1048608 | tf_op jit(solution)/shard_map/ppermute | solution.py:45
  133.5 3.6 %collective-permute-start.13 = (f32[128,1024]{1,0:T(8,128)S(1)}, f32[128,1024]{1,0:T(8,128)S(1)}, u32[]{:S(2)}, u32[]{:S(2)}) collective-permute-start(f32[128,1024]{1,0:T(8,128)S(1)} %add.108), channel_id=1, source_target_pairs={{8,16},{9,17},{10,18},{11,19},{12,20},{13,21},{14,22},{15,23},{16,... | collective-permute-start | bytes 1572872 | tf_op jit(solution)/shard_map/ppermute | solution.py:45
  137.3 2.5 collective-permute-start.18
  141.4 5.6 %collective-permute-done.13 = f32[128,1024]{1,0:T(8,128)S(1)} collective-permute-done((f32[128,1024]{1,0:T(8,128)S(1)}, f32[128,1024]{1,0:T(8,128)S(1)}, u32[]{:S(2)}, u32[]{:S(2)}) %collective-permute-start.13) | collective-permute-done | bytes 524320 | tf_op jit(solution)/shard_map/ppermute | solution.py:45
  147.0 1.7 collective-permute-done.18
  148.7 3.9 %collective-permute-done.9 = f32[128,1024]{1,0:T(8,128)S(1)} collective-permute-done((f32[128,1024]{1,0:T(8,128)S(1)}, f32[128,1024]{1,0:T(8,128)S(1)}, u32[]{:S(2)}, u32[]{:S(2)}) %collective-permute-start.9) | collective-permute-done | bytes 524320 | tf_op jit(solution)/shard_map/ppermute | solution.py:45
  153.6 23.5 %close.1 = (f32[256,2560]{1,0:T(8,128)}, f32[256,2560]{1,0:T(8,128)}, f32[256,512]{1,0:T(8,128)}, f32[128,512]{1,0:T(8,128)}, f32[128,512]{1,0:T(8,128)}) custom-call(s32[1]{0:T(128)S(6)} %copy.23.length, f32[256,2560]{1,0:T(8,128)} %q.5, f32[256,2560]{1,0:T(8,128)} %g.3, f32[128,1024]{1,0:T(8,128)} %fusion.6.kp.vp, f32[128,1024]{1,0:T(8,128)} %fusion.6.kp.vp, ...), custom_call_target="tpu_custom_call" | custom-call | tf_op jit(solution)/shard_map/close/pallas_call | solution.py:397
  179.2 2.6 collective-permute-start.30
  181.8 1.8 collective-permute-start.19
  183.9 12.2 %collective-permute-done.22.refs_4_ = f32[128,1024]{1,0:T(8,128)S(1)} collective-permute-done((f32[128,1024]{1,0:T(8,128)S(1)}, f32[128,1024]{1,0:T(8,128)S(1)}, u32[]{:S(2)}, u32[]{:S(2)}) %collective-permute-start.22) | collective-permute-done | bytes 524320 | tf_op jit(solution)/shard_map/ppermute | solution.py:45
  196.1 2.0 collective-permute-start.23
  198.1 2.2 collective-permute-start.27
  200.2 24.3 %collective-permute-done.30.refs_12_ = f32[128,1024]{1,0:T(8,128)S(1)} collective-permute-done((f32[128,1024]{1,0:T(8,128)S(1)}, f32[128,1024]{1,0:T(8,128)S(1)}, u32[]{:S(2)}, u32[]{:S(2)}) %collective-permute-start.30) | collective-permute-done | bytes 524320 | tf_op jit(solution)/shard_map/ppermute | solution.py:45
  224.5 1.7 collective-permute-start.31
  226.3 1.4 collective-permute-start.24
  227.8 1.4 collective-permute-start.32
  229.2 4.7 %collective-permute-done.31.refs_13_ = f32[128,1024]{1,0:T(8,128)S(1)} collective-permute-done((f32[128,1024]{1,0:T(8,128)S(1)}, f32[128,1024]{1,0:T(8,128)S(1)}, u32[]{:S(2)}, u32[]{:S(2)}) %collective-permute-start.31) | collective-permute-done | bytes 524320 | tf_op jit(solution)/shard_map/ppermute | solution.py:45
  233.9 3.6 %collective-permute-done.21.refs_3_ = f32[128,1024]{1,0:T(8,128)S(1)} collective-permute-done((f32[128,1024]{1,0:T(8,128)S(1)}, f32[128,1024]{1,0:T(8,128)S(1)}, u32[]{:S(2)}, u32[]{:S(2)}) %collective-permute-start.21) | collective-permute-done | bytes 524320 | tf_op jit(solution)/shard_map/ppermute | solution.py:45
  237.4 8.3 %collective-permute-done.24.refs_6_ = f32[128,1024]{1,0:T(8,128)S(1)} collective-permute-done((f32[128,1024]{1,0:T(8,128)S(1)}, f32[128,1024]{1,0:T(8,128)S(1)}, u32[]{:S(2)}, u32[]{:S(2)}) %collective-permute-start.24) | collective-permute-done | bytes 524320 | tf_op jit(solution)/shard_map/ppermute | solution.py:45
  245.9 14.6 %finish.1 = (f32[256,2560]{1,0:T(8,128)}, f32[256,512]{1,0:T(8,128)}, f32[256,512]{1,0:T(8,128)}) custom-call(s32[1]{0:T(128)S(6)} %copy.23.length, f32[256,2560]{1,0:T(8,128)} %q.5, f32[256,2560]{1,0:T(8,128)} %g.3, f32[256,512]{1,0:T(8,128)} %k.3, f32[256,512]{1,0:T(8,128)} %v.3, f32[128,1024]{1,0:T(8,128)} %fusion.6.kp.vp, ...), custom_call_target="tpu_custom_call" | custom-call | tf_op jit(solution)/shard_map/finish/pallas_call | solution.py:397
  260.6 2.0 collective-permute-done.25.refs_7_
  262.6 5.7 %collective-permute-done.29.refs_11_ = f32[128,1024]{1,0:T(8,128)S(1)} collective-permute-done((f32[128,1024]{1,0:T(8,128)S(1)}, f32[128,1024]{1,0:T(8,128)S(1)}, u32[]{:S(2)}, u32[]{:S(2)}) %collective-permute-start.29) | collective-permute-done | bytes 524320 | tf_op jit(solution)/shard_map/ppermute | solution.py:45
  268.4 5.3 %collective-permute-done.33.refs_15_ = f32[128,1024]{1,0:T(8,128)} collective-permute-done((f32[128,1024]{1,0:T(8,128)S(1)}, f32[128,1024]{1,0:T(8,128)}, u32[]{:S(2)}, u32[]{:S(2)}) %collective-permute-start.33) | collective-permute-done | bytes 524320 | tf_op jit(solution)/shard_map/ppermute | solution.py:45
  273.7 10.2 %hidden_grad.1 = (f32[16,160,128]{2,1,0:T(8,128)}, f32[16,160,128]{2,1,0:T(8,128)}) custom-call(s32[16]{0:T(128)} %get-tuple-element.111.listed, f32[128,1024]{1,0:T(8,128)} %copy-done.3, f32[128,1024]{1,0:T(8,128)} %copy-done.7, f32[128,1024]{1,0:T(8,128)} %copy-done.8, f32[128,1024]{1,0:T(8,128)} %copy-done.12, f32[128,1024]{1,0:T(8,128)} %copy-done.4, ...), custom_call_target="tpu_custom_call" | custom-call | tf_op jit(solution)/shard_map/hidden_grad/pallas_call | solution.py:265
  283.9 3.2 collective-permute-done.34
  287.2 2.6 add.116
  289.8 4.1 %all-to-all-start.1 = ((f32[16,160,128]{2,1,0:T(8,128)}), f32[16,160,128]{2,1,0:T(8,128)S(1)}, u32[]{:S(2)}, u32[]{:S(2)}) async-start(f32[16,160,128]{2,1,0:T(8,128)} %add.116), calls=%async_computation.1 | async-start | bytes 2621440 | tf_op jit(solution)/shard_map/all_to_all | solution.py:514
  293.9 9.9 %weight_grad.1 = (f32[320,512]{1,0:T(8,128)}, f32[320,512]{1,0:T(8,128)}) custom-call(s32[16]{0:T(128)} %get-tuple-element.111.listed, s32[1]{0:T(128)} %bitcast.core, f32[16,160,128]{2,1,0:T(8,128)} %copy-done, f32[16,160,128]{2,1,0:T(8,128)} %copy-done.1, f32[128,1024]{1,0:T(8,128)} %copy-done.3, f32[128,1024]{1,0:T(8,128)} %copy-done.7, ...), custom_call_target="tpu_custom_call" | custom-call | tf_op jit(solution)/shard_map/weight_grad/pallas_call | solution.py:298
  303.8 20.1 %all-to-all-done.1.own = f32[16,160,128]{2,1,0:T(8,128)S(1)} async-done(((f32[16,160,128]{2,1,0:T(8,128)}), f32[16,160,128]{2,1,0:T(8,128)S(1)}, u32[]{:S(2)}, u32[]{:S(2)}) %all-to-all-start.1) | async-done | bytes 1310752 | tf_op jit(solution)/shard_map/all_to_all | solution.py:514
  324.0 2.5 collective-permute-start.35
  326.5 1.7 collective-permute-done.35.other
  329.1 3.8 %turn_back.1 = f32[128,2560]{1,0:T(8,128)} custom-call(s32[1]{0:T(128)} %bitcast.core, f32[16,160,128]{2,1,0:T(8,128)} %copy-done.2, f32[8,160,128]{2,1,0:T(8,128)} %copy-done.22), custom_call_target="tpu_custom_call" | custom-call | tf_op jit(solution)/shard_map/turn_back/pallas_call | solution.py:181
  (125 shorter events, 20.3 us)
Async XLA Ops:
  6.8 50.8 %all-to-all-start = ((f32[16,160,128]{2,1,0:T(8,128)}), f32[16,160,128]{2,1,0:T(8,128)S(1)}, u32[]{:S(2)}, u32[]{:S(2)}) async-start(f32[16,160,128]{2,1,0:T(8,128)} %turn.1), calls=%async_computation | async-start | bytes 2621440 | tf_op jit(solution)/shard_map/all_to_all | solution.py:452
  14.2 20.8 %collective-permute-start = (s32[16]{0:T(128)S(1)}, s32[16]{0:T(128)S(1)}, u32[]{:S(2)}, u32[]{:S(2)}) collective-permute-start(s32[16]{0:T(128)S(1)} %compare_select_fusion), channel_id=1, source_target_pairs={{0,8},{1,9},{2,10},{3,11},{4,12},{5,13},{6,14},{7,15},{8,0},{9,1},... | collective-permute-start | bytes 200 | tf_op jit(solution)/shard_map/ppermute | solution.py:45
  35.0 6.1 %collective-permute-start.1 = (s32[16]{0:T(128)S(1)}, s32[16]{0:T(128)S(1)}, u32[]{:S(2)}, u32[]{:S(2)}) collective-permute-start(s32[16]{0:T(128)S(1)} %fusion.11), channel_id=1, source_target_pairs={{0,16},{1,17},{2,18},{3,19},{4,20},{5,21},{6,22},{7,23},{8,24},{9,... | collective-permute-start | bytes 200 | tf_op jit(solution)/shard_map/ppermute | solution.py:45
  41.1 3.7 %collective-permute-start.2 = (s32[16]{0:T(128)S(1)}, s32[16]{0:T(128)S(1)}, u32[]{:S(2)}, u32[]{:S(2)}) collective-permute-start(s32[16]{0:T(128)S(1)} %fusion.12), channel_id=1, source_target_pairs={{0,4},{1,3},{2,6},{3,1},{4,0},{5,7},{6,2},{7,5},{8,12},{9,11},{10,... | collective-permute-start | bytes 200 | tf_op jit(solution)/shard_map/ppermute | solution.py:45
  44.8 12.8 %collective-permute-start.3 = (s32[16]{0:T(128)S(1)}, s32[16]{0:T(128)S(1)}, u32[]{:S(2)}, u32[]{:S(2)}) collective-permute-start(s32[16]{0:T(128)S(1)} %add.96), channel_id=1, source_target_pairs={{0,2},{1,5},{2,0},{3,7},{4,6},{5,1},{6,4},{7,3},{8,10},{9,13},{10,... | collective-permute-start | bytes 200 | tf_op jit(solution)/shard_map/ppermute | solution.py:45
  57.6 4.7 %collective-permute-start.4 = (f32[16,160,128]{2,1,0:T(8,128)S(1)}, f32[16,160,128]{2,1,0:T(8,128)S(1)}, u32[]{:S(2)}, u32[]{:S(2)}) collective-permute-start(f32[16,160,128]{2,1,0:T(8,128)S(1)} %all-to-all-done.refs_0_.refs_1_.refs_2_.refs_3_.own), channel_id=1, source_target_pairs={{0,1},{1,0},{2,3},{3,2},{4,5},{5,4},{6,7},{7,6},{8,9},{9,8},{10,11... | collective-permute-start | bytes 3932168 | tf_op jit(solution)/shard_map/ppermute | solution.py:476
  68.8 14.2 %collective-permute-start.14 = (f32[256,1024]{1,0:T(8,128)}, f32[256,1024]{1,0:T(8,128)S(1)}, u32[]{:S(2)}, u32[]{:S(2)}) collective-permute-start(f32[256,1024]{1,0:T(8,128)} %get-tuple-element.74), channel_id=1, source_target_pairs={{0,2},{1,5},{2,0},{3,7},{4,6},{5,1},{6,4},{7,3},{8,10},{9,13},{10,... | collective-permute-start | bytes 3145736 | tf_op jit(solution)/shard_map/ppermute | solution.py:45
  74.7 25.0 %collective-permute-start.10 = (f32[256,1024]{1,0:T(8,128)}, f32[256,1024]{1,0:T(8,128)S(1)}, u32[]{:S(2)}, u32[]{:S(2)}) collective-permute-start(f32[256,1024]{1,0:T(8,128)} %get-tuple-element.72), channel_id=1, source_target_pairs={{0,2},{1,5},{2,0},{3,7},{4,6},{5,1},{6,4},{7,3},{8,10},{9,13},{10,... | collective-permute-start | bytes 3145736 | tf_op jit(solution)/shard_map/ppermute | solution.py:45
  81.1 35.6 %collective-permute-start.7 = (f32[256,1024]{1,0:T(8,128)}, f32[256,1024]{1,0:T(8,128)S(1)}, u32[]{:S(2)}, u32[]{:S(2)}) collective-permute-start(f32[256,1024]{1,0:T(8,128)} %get-tuple-element.70), channel_id=1, source_target_pairs={{0,2},{1,5},{2,0},{3,7},{4,6},{5,1},{6,4},{7,3},{8,10},{9,13},{10,... | collective-permute-start | bytes 3145736 | tf_op jit(solution)/shard_map/ppermute | solution.py:45
  83.0 17.2 %collective-permute-start.15 = (f32[128,1024]{1,0:T(8,128)S(1)}, f32[128,1024]{1,0:T(8,128)S(1)}, u32[]{:S(2)}, u32[]{:S(2)}) collective-permute-start(f32[128,1024]{1,0:T(8,128)S(1)} %slice_add_fusion), channel_id=1, source_target_pairs={{0,4},{1,3},{2,6},{3,1},{4,0},{5,7},{6,2},{7,5},{8,12},{9,11},{10,... | collective-permute-start | bytes 1572872 | tf_op jit(solution)/shard_map/ppermute | solution.py:45
  88.9 44.1 %collective-permute-start.5 = (f32[256,1024]{1,0:T(8,128)}, f32[256,1024]{1,0:T(8,128)S(1)}, u32[]{:S(2)}, u32[]{:S(2)}) collective-permute-start(f32[256,1024]{1,0:T(8,128)} %get-tuple-element.68), channel_id=1, source_target_pairs={{0,2},{1,5},{2,0},{3,7},{4,6},{5,1},{6,4},{7,3},{8,10},{9,13},{10,... | collective-permute-start | bytes 3145736 | tf_op jit(solution)/shard_map/ppermute | solution.py:45
  99.9 16.8 %collective-permute-start.11 = (f32[128,1024]{1,0:T(8,128)S(1)}, f32[128,1024]{1,0:T(8,128)S(1)}, u32[]{:S(2)}, u32[]{:S(2)}) collective-permute-start(f32[128,1024]{1,0:T(8,128)S(1)} %slice_add_fusion.2), channel_id=1, source_target_pairs={{0,4},{1,3},{2,6},{3,1},{4,0},{5,7},{6,2},{7,5},{8,12},{9,11},{10,... | collective-permute-start | bytes 1572872 | tf_op jit(solution)/shard_map/ppermute | solution.py:45
  100.3 18.3 %collective-permute-start.16 = (f32[128,1024]{1,0:T(8,128)S(1)}, f32[128,1024]{1,0:T(8,128)S(1)}, u32[]{:S(2)}, u32[]{:S(2)}) collective-permute-start(f32[128,1024]{1,0:T(8,128)S(1)} %fusion), channel_id=1, source_target_pairs={{0,8},{1,9},{2,10},{3,11},{4,12},{5,13},{6,14},{7,15},{24,16},{25,... | collective-permute-start | bytes 1572872 | tf_op jit(solution)/shard_map/ppermute | solution.py:45
  116.8 16.6 %collective-permute-start.12 = (f32[128,1024]{1,0:T(8,128)S(1)}, f32[128,1024]{1,0:T(8,128)S(1)}, u32[]{:S(2)}, u32[]{:S(2)}) collective-permute-start(f32[128,1024]{1,0:T(8,128)S(1)} %fusion.1), channel_id=1, source_target_pairs={{0,8},{1,9},{2,10},{3,11},{4,12},{5,13},{6,14},{7,15},{24,16},{25,... | collective-permute-start | bytes 1572872 | tf_op jit(solution)/shard_map/ppermute | solution.py:45
  118.3 18.9 %collective-permute-start.8 = (f32[128,1024]{1,0:T(8,128)S(1)}, f32[128,1024]{1,0:T(8,128)S(1)}, u32[]{:S(2)}, u32[]{:S(2)}) collective-permute-start(f32[128,1024]{1,0:T(8,128)S(1)} %slice_add_fusion.4), channel_id=1, source_target_pairs={{0,4},{1,3},{2,6},{3,1},{4,0},{5,7},{6,2},{7,5},{8,12},{9,11},{10,... | collective-permute-start | bytes 1572872 | tf_op jit(solution)/shard_map/ppermute | solution.py:45
  118.7 18.4 %collective-permute-start.17 = (f32[128,1024]{1,0:T(8,128)S(1)}, f32[128,1024]{1,0:T(8,128)S(1)}, u32[]{:S(2)}, u32[]{:S(2)}) collective-permute-start(f32[128,1024]{1,0:T(8,128)S(1)} %add.113), channel_id=1, source_target_pairs={{8,16},{9,17},{10,18},{11,19},{12,20},{13,21},{14,22},{15,23},{16,... | collective-permute-start | bytes 1572872 | tf_op jit(solution)/shard_map/ppermute | solution.py:45
  133.0 8.4 %collective-permute-start.6 = (f32[128,1024]{1,0:T(8,128)S(1)}, f32[128,1024]{1,0:T(8,128)S(1)}, u32[]{:S(2)}, u32[]{:S(2)}) collective-permute-start(f32[128,1024]{1,0:T(8,128)S(1)} %slice_add_fusion.6), channel_id=1, source_target_pairs={{0,4},{1,3},{2,6},{3,1},{4,0},{5,7},{6,2},{7,5},{8,12},{9,11},{10,... | collective-permute-start | bytes 1572872 | tf_op jit(solution)/shard_map/ppermute | solution.py:45
  133.5 13.5 %collective-permute-start.13 = (f32[128,1024]{1,0:T(8,128)S(1)}, f32[128,1024]{1,0:T(8,128)S(1)}, u32[]{:S(2)}, u32[]{:S(2)}) collective-permute-start(f32[128,1024]{1,0:T(8,128)S(1)} %add.108), channel_id=1, source_target_pairs={{8,16},{9,17},{10,18},{11,19},{12,20},{13,21},{14,22},{15,23},{16,... | collective-permute-start | bytes 1572872 | tf_op jit(solution)/shard_map/ppermute | solution.py:45
  137.3 11.4 %collective-permute-start.18 = (f32[128,1024]{1,0:T(8,128)S(1)}, f32[128,1024]{1,0:T(8,128)S(1)}, u32[]{:S(2)}, u32[]{:S(2)}) collective-permute-start(f32[128,1024]{1,0:T(8,128)S(1)} %get-tuple-element.113), channel_id=1, source_target_pairs={{8,0},{9,1},{10,2},{11,3},{12,4},{13,5},{14,6},{15,7},{16,24},{17,... | collective-permute-start | bytes 1572872 | tf_op jit(solution)/shard_map/ppermute | solution.py:45
  139.8 12.7 %collective-permute-start.9 = (f32[128,1024]{1,0:T(8,128)S(1)}, f32[128,1024]{1,0:T(8,128)S(1)}, u32[]{:S(2)}, u32[]{:S(2)}) collective-permute-start(f32[128,1024]{1,0:T(8,128)S(1)} %get-tuple-element.114), channel_id=1, source_target_pairs={{0,8},{1,9},{2,10},{3,11},{4,12},{5,13},{6,14},{7,15},{24,16},{25,... | collective-permute-start | bytes 1572872 | tf_op jit(solution)/shard_map/ppermute | solution.py:45
  179.1 81.4 %copy-start.3 = (f32[128,1024]{1,0:T(8,128)}, f32[128,1024]{1,0:T(8,128)S(1)}, u32[]{:S(2)}) copy-start(f32[128,1024]{1,0:T(8,128)S(1)} %constant_dynamic-update-slice_fusion.refs_0_) | copy-start | bytes 1572868
  179.1 17.0 %collective-permute-start.22 = (f32[128,1024]{1,0:T(8,128)S(1)}, f32[128,1024]{1,0:T(8,128)S(1)}, u32[]{:S(2)}, u32[]{:S(2)}) collective-permute-start(f32[128,1024]{1,0:T(8,128)S(1)} %constant_dynamic-update-slice_fusion.refs_0_), channel_id=1, source_target_pairs={{0,8},{1,9},{2,10},{3,11},{4,12},{5,13},{6,14},{7,15},{8,0},{9,1},... | collective-permute-start | bytes 1572872 | tf_op jit(solution)/shard_map/ppermute | solution.py:45
  179.1 18.9 %collective-permute-start.26 = (f32[128,1024]{1,0:T(8,128)S(1)}, f32[128,1024]{1,0:T(8,128)S(1)}, u32[]{:S(2)}, u32[]{:S(2)}) collective-permute-start(f32[128,1024]{1,0:T(8,128)S(1)} %constant_dynamic-update-slice_fusion.refs_0_), channel_id=1, source_target_pairs={{0,16},{1,17},{2,18},{3,19},{4,20},{5,21},{6,22},{7,23},{8,24},{9,... | collective-permute-start | bytes 1572872 | tf_op jit(solution)/shard_map/ppermute | solution.py:45
  179.2 45.3 %collective-permute-start.30 = (f32[128,1024]{1,0:T(8,128)S(1)}, f32[128,1024]{1,0:T(8,128)S(1)}, u32[]{:S(2)}, u32[]{:S(2)}) collective-permute-start(f32[128,1024]{1,0:T(8,128)S(1)} %constant_dynamic-update-slice_fusion.refs_0_), channel_id=1, source_target_pairs={{0,24},{1,25},{2,26},{3,27},{4,28},{5,29},{6,30},{7,31},{8,16},{9,... | collective-permute-start | bytes 1572872 | tf_op jit(solution)/shard_map/ppermute | solution.py:45
  181.8 44.4 %collective-permute-start.19 = (f32[128,1024]{1,0:T(8,128)S(1)}, f32[128,1024]{1,0:T(8,128)S(1)}, u32[]{:S(2)}, u32[]{:S(2)}) collective-permute-start(f32[128,1024]{1,0:T(8,128)S(1)} %constant_dynamic-update-slice_fusion.refs_0_), channel_id=1, source_target_pairs={{0,4},{1,3},{2,6},{3,1},{4,0},{5,7},{6,2},{7,5},{8,12},{9,11},{10,... | collective-permute-start | bytes 1572872 | tf_op jit(solution)/shard_map/ppermute | solution.py:45
  183.5 42.8 %collective-permute-start.20 = (f32[128,1024]{1,0:T(8,128)S(1)}, f32[128,1024]{1,0:T(8,128)S(1)}, u32[]{:S(2)}, u32[]{:S(2)}) collective-permute-start(f32[128,1024]{1,0:T(8,128)S(1)} %constant_dynamic-update-slice_fusion.refs_0_), channel_id=1, source_target_pairs={{0,2},{1,5},{2,0},{3,7},{4,6},{5,1},{6,4},{7,3},{8,10},{9,13},{10,... | collective-permute-start | bytes 1572872 | tf_op jit(solution)/shard_map/ppermute | solution.py:45
  196.1 64.4 %copy-start.4 = (f32[128,1024]{1,0:T(8,128)}, f32[128,1024]{1,0:T(8,128)S(1)}, u32[]{:S(2)}) copy-start(f32[128,1024]{1,0:T(8,128)S(1)} %collective-permute-done.22.refs_4_) | copy-start | bytes 1572868
  196.1 31.6 %collective-permute-start.23 = (f32[128,1024]{1,0:T(8,128)S(1)}, f32[128,1024]{1,0:T(8,128)S(1)}, u32[]{:S(2)}, u32[]{:S(2)}) collective-permute-start(f32[128,1024]{1,0:T(8,128)S(1)} %collective-permute-done.22.refs_4_), channel_id=1, source_target_pairs={{0,4},{1,3},{2,6},{3,1},{4,0},{5,7},{6,2},{7,5},{8,12},{9,11},{10,... | collective-permute-start | bytes 1572872 | tf_op jit(solution)/shard_map/ppermute | solution.py:45
  198.1 62.4 %copy-start.5 = (f32[128,1024]{1,0:T(8,128)}, f32[128,1024]{1,0:T(8,128)S(1)}, u32[]{:S(2)}) copy-start(f32[128,1024]{1,0:T(8,128)S(1)} %collective-permute-done.26.refs_8_) | copy-start | bytes 1572868
  198.1 29.7 %collective-permute-start.27 = (f32[128,1024]{1,0:T(8,128)S(1)}, f32[128,1024]{1,0:T(8,128)S(1)}, u32[]{:S(2)}, u32[]{:S(2)}) collective-permute-start(f32[128,1024]{1,0:T(8,128)S(1)} %collective-permute-done.26.refs_8_), channel_id=1, source_target_pairs={{0,4},{1,3},{2,6},{3,1},{4,0},{5,7},{6,2},{7,5},{8,12},{9,11},{10,... | collective-permute-start | bytes 1572872 | tf_op jit(solution)/shard_map/ppermute | solution.py:45
  224.5 36.0 %copy-start.6 = (f32[128,1024]{1,0:T(8,128)}, f32[128,1024]{1,0:T(8,128)S(1)}, u32[]{:S(2)}) copy-start(f32[128,1024]{1,0:T(8,128)S(1)} %collective-permute-done.30.refs_12_) | copy-start | bytes 1572868
  224.5 9.3 %collective-permute-start.31 = (f32[128,1024]{1,0:T(8,128)S(1)}, f32[128,1024]{1,0:T(8,128)S(1)}, u32[]{:S(2)}, u32[]{:S(2)}) collective-permute-start(f32[128,1024]{1,0:T(8,128)S(1)} %collective-permute-done.30.refs_12_), channel_id=1, source_target_pairs={{0,4},{1,3},{2,6},{3,1},{4,0},{5,7},{6,2},{7,5},{8,12},{9,11},{10,... | collective-permute-start | bytes 1572872 | tf_op jit(solution)/shard_map/ppermute | solution.py:45
  226.2 34.3 %copy-start.7 = (f32[128,1024]{1,0:T(8,128)}, f32[128,1024]{1,0:T(8,128)S(1)}, u32[]{:S(2)}) copy-start(f32[128,1024]{1,0:T(8,128)S(1)} %collective-permute-done.19.refs_1_) | copy-start | bytes 1572868
  226.2 11.2 %collective-permute-start.21 = (f32[128,1024]{1,0:T(8,128)S(1)}, f32[128,1024]{1,0:T(8,128)S(1)}, u32[]{:S(2)}, u32[]{:S(2)}) collective-permute-start(f32[128,1024]{1,0:T(8,128)S(1)} %collective-permute-done.19.refs_1_), channel_id=1, source_target_pairs={{0,2},{1,5},{2,0},{3,7},{4,6},{5,1},{6,4},{7,3},{8,10},{9,13},{10,... | collective-permute-start | bytes 1572872 | tf_op jit(solution)/shard_map/ppermute | solution.py:45
  226.3 34.2 %copy-start.8 = (f32[128,1024]{1,0:T(8,128)}, f32[128,1024]{1,0:T(8,128)S(1)}, u32[]{:S(2)}) copy-start(f32[128,1024]{1,0:T(8,128)S(1)} %collective-permute-done.20.refs_2_) | copy-start | bytes 1572868
  226.3 19.5 %collective-permute-start.24 = (f32[128,1024]{1,0:T(8,128)S(1)}, f32[128,1024]{1,0:T(8,128)S(1)}, u32[]{:S(2)}, u32[]{:S(2)}) collective-permute-start(f32[128,1024]{1,0:T(8,128)S(1)} %collective-permute-done.22.refs_4_), channel_id=1, source_target_pairs={{0,2},{1,5},{2,0},{3,7},{4,6},{5,1},{6,4},{7,3},{8,10},{9,13},{10,... | collective-permute-start | bytes 1572872 | tf_op jit(solution)/shard_map/ppermute | solution.py:45
  227.7 32.8 %copy-start.9 = (f32[128,1024]{1,0:T(8,128)}, f32[128,1024]{1,0:T(8,128)S(1)}, u32[]{:S(2)}) copy-start(f32[128,1024]{1,0:T(8,128)S(1)} %collective-permute-done.23.refs_5_) | copy-start | bytes 1572868
  227.7 32.9 %collective-permute-start.28 = (f32[128,1024]{1,0:T(8,128)S(1)}, f32[128,1024]{1,0:T(8,128)S(1)}, u32[]{:S(2)}, u32[]{:S(2)}) collective-permute-start(f32[128,1024]{1,0:T(8,128)S(1)} %collective-permute-done.26.refs_8_), channel_id=1, source_target_pairs={{0,2},{1,5},{2,0},{3,7},{4,6},{5,1},{6,4},{7,3},{8,10},{9,13},{10,... | collective-permute-start | bytes 1572872 | tf_op jit(solution)/shard_map/ppermute | solution.py:45
  227.8 32.7 %copy-start.10 = (f32[128,1024]{1,0:T(8,128)}, f32[128,1024]{1,0:T(8,128)S(1)}, u32[]{:S(2)}) copy-start(f32[128,1024]{1,0:T(8,128)S(1)} %collective-permute-done.27.refs_9_) | copy-start | bytes 1572868
  227.8 32.8 %collective-permute-start.32 = (f32[128,1024]{1,0:T(8,128)S(1)}, f32[128,1024]{1,0:T(8,128)S(1)}, u32[]{:S(2)}, u32[]{:S(2)}) collective-permute-start(f32[128,1024]{1,0:T(8,128)S(1)} %collective-permute-done.30.refs_12_), channel_id=1, source_target_pairs={{0,2},{1,5},{2,0},{3,7},{4,6},{5,1},{6,4},{7,3},{8,10},{9,13},{10,... | collective-permute-start | bytes 1572872 | tf_op jit(solution)/shard_map/ppermute | solution.py:45
  233.8 26.7 %copy-start.11 = (f32[128,1024]{1,0:T(8,128)}, f32[128,1024]{1,0:T(8,128)S(1)}, u32[]{:S(2)}) copy-start(f32[128,1024]{1,0:T(8,128)S(1)} %collective-permute-done.31.refs_13_) | copy-start | bytes 1572868
  233.8 28.8 %collective-permute-start.25 = (f32[128,1024]{1,0:T(8,128)S(1)}, f32[128,1024]{1,0:T(8,128)S(1)}, u32[]{:S(2)}, u32[]{:S(2)}) collective-permute-start(f32[128,1024]{1,0:T(8,128)S(1)} %collective-permute-done.23.refs_5_), channel_id=1, source_target_pairs={{0,2},{1,5},{2,0},{3,7},{4,6},{5,1},{6,4},{7,3},{8,10},{9,13},{10,... | collective-permute-start | bytes 1572872 | tf_op jit(solution)/shard_map/ppermute | solution.py:45
  237.4 23.1 %copy-start.12 = (f32[128,1024]{1,0:T(8,128)}, f32[128,1024]{1,0:T(8,128)S(1)}, u32[]{:S(2)}) copy-start(f32[128,1024]{1,0:T(8,128)S(1)} %collective-permute-done.21.refs_3_) | copy-start | bytes 1572868
  237.4 30.9 %collective-permute-start.29 = (f32[128,1024]{1,0:T(8,128)S(1)}, f32[128,1024]{1,0:T(8,128)S(1)}, u32[]{:S(2)}, u32[]{:S(2)}) collective-permute-start(f32[128,1024]{1,0:T(8,128)S(1)} %collective-permute-done.27.refs_9_), channel_id=1, source_target_pairs={{0,2},{1,5},{2,0},{3,7},{4,6},{5,1},{6,4},{7,3},{8,10},{9,13},{10,... | collective-permute-start | bytes 1572872 | tf_op jit(solution)/shard_map/ppermute | solution.py:45
  245.8 27.9 %collective-permute-start.33 = (f32[128,1024]{1,0:T(8,128)S(1)}, f32[128,1024]{1,0:T(8,128)}, u32[]{:S(2)}, u32[]{:S(2)}) collective-permute-start(f32[128,1024]{1,0:T(8,128)S(1)} %collective-permute-done.31.refs_13_), channel_id=1, source_target_pairs={{0,2},{1,5},{2,0},{3,7},{4,6},{5,1},{6,4},{7,3},{8,10},{9,13},{10,... | collective-permute-start | bytes 1572872 | tf_op jit(solution)/shard_map/ppermute | solution.py:45
  283.9 3.2 collective-permute-start.34
  289.8 34.2 %all-to-all-start.1 = ((f32[16,160,128]{2,1,0:T(8,128)}), f32[16,160,128]{2,1,0:T(8,128)S(1)}, u32[]{:S(2)}, u32[]{:S(2)}) async-start(f32[16,160,128]{2,1,0:T(8,128)} %add.116), calls=%async_computation.1 | async-start | bytes 2621440 | tf_op jit(solution)/shard_map/all_to_all | solution.py:514
  324.0 4.2 %collective-permute-start.35 = (f32[8,160,128]{2,1,0:T(8,128)S(1)}, f32[8,160,128]{2,1,0:T(8,128)S(1)}, u32[]{:S(2)}, u32[]{:S(2)}) collective-permute-start(f32[8,160,128]{2,1,0:T(8,128)S(1)} %slice_select_fusion), channel_id=1, source_target_pairs={{0,1},{1,0},{2,3},{3,2},{4,5},{5,4},{6,7},{7,6},{8,9},{9,8},{10,11... | collective-permute-start | bytes 1966088 | tf_op jit(solution)/shard_map/ppermute | solution.py:518
  (17 other events, 162.9 us)

commit v2 on v1

--- a/solution.py
+++ b/solution.py
@@ -43,18 +43,6 @@
 
 def permute(x, pairs):
     return lax.ppermute(x, BOTH, pairs)
-
-
-def spread(block):
-    second = permute(block, SECOND)
-    return [block, second, permute(block, THIRD), permute(second, THIRD)]
-
-
-def gather_blocks(block):
-    out = spread(block)
-    for k in range(1, 4):
-        out += spread(permute(block, ACROSS[k]))
-    return out
 
 
 def gathered_order(chip, core):
@@ -99,9 +87,29 @@
     return dot(a[0], b[0], dims) + (dot(a[0], b[1], dims) + dot(a[1], b[0], dims))
 
 
+def beside(terms):
+    return jnp.concatenate(terms, 1)
+
+
+def halves(x):
+    n = x.shape[1] // 2
+    return x[:, :n] + x[:, n:]
+
+
 def dot_rows(a, b):
-    dims = ((1,), (1,))
-    return dot(jnp.concatenate(a, 1), jnp.concatenate([b[0], b[0]], 1), dims) + dot(a[0], b[1], dims)
+    rows = jnp.concatenate([beside([b[0], b[0]]), beside([b[1], b[1]])], 0)
+    return halves(dot(beside(a), rows, ((1,), (1,))))
+
+
+def dot_columns(a, b):
+    pair = beside(b)
+    return halves(dot(beside(a), jnp.concatenate([pair, pair], 0), ((1,), (0,))))
+
+
+def dot_turned(a, b):
+    n = a[0].shape[1]
+    out = halves(dot(beside(a), beside(b), ((0,), (0,))))
+    return out[:n] + out[n:]
 
 
 def three_terms(x):
@@ -113,17 +121,14 @@
 
 def dot_rows_exact(a, b):
     a, b = three_terms(a), three_terms(b)
-    dims = ((1,), (1,))
-    pair = jnp.concatenate(a[:2], 1)
-    small = dot(jnp.concatenate([a[2], a[0]], 1), jnp.concatenate([b[0], b[2]], 1), dims)
-    small = small + dot(pair, jnp.concatenate([b[1], b[1]], 1), dims)
-    return dot(pair, jnp.concatenate([b[0], b[0]], 1), dims) + small
+    small = dot(beside([a[2], a[0]]), beside([b[0], b[2]]), ((1,), (1,)))
+    return dot_rows(a[:2], b[:2]) + small
 
 
 VMEM_LIMIT = 56 << 20
 
 
-def call(kernel, name, grid, in_specs, out_specs, out_shape, scalars=0, scratch=()):
+def call(kernel, name, grid, in_specs, out_specs, out_shape, scalars=0, scratch=(), aliases={}):
     return pl.pallas_call(
         kernel,
         out_shape=[jax.ShapeDtypeStruct(*shape) for shape in out_shape],
@@ -134,6 +139,7 @@
             out_specs=out_specs,
             scratch_shapes=scratch,
         ),
+        input_output_aliases=aliases,
         compiler_params=pltpu.CompilerParams(vmem_limit_bytes=VMEM_LIMIT),
         name=name,
     )
@@ -143,26 +149,31 @@
     return pl.BlockSpec(x.shape, lambda *_: (0,) * x.ndim)
 
 
-def turn_kernel(core, x, out):
+ID_ROWS = 8
+
+
+def turn_kernel(core, prompt, x, out):
     t = x[...].T
-    count, half, _ = out.shape
+    count, rows, _ = out.shape
+    half = rows - ID_ROWS
     for c in range(count):
         own = t[2 * c * half : 2 * (c + 1) * half]
-        out[c] = jnp.where(core[0] == 0, own[:half], own[half:])
-
-
-def turn(core, hidden, chips):
+        out[c, :half] = jnp.where(core[0] == 0, own[:half], own[half:])
+        out[c, half:] = jnp.full((ID_ROWS, out.shape[2]), prompt[0].astype(jnp.float32))
+
+
+def turn(core, prompt, hidden, chips):
     rows, model = hidden.shape
     half = model // chips // 2
     (out,) = call(
         turn_kernel,
         "turn",
-        (chips // 2,),
-        [pl.BlockSpec((rows, model // chips * 2), lambda i, *_: (0, i))],
-        [pl.BlockSpec((2, half, rows), lambda i, *_: (i, 0, 0))],
-        [((chips, half, rows), jnp.float32)],
-        scalars=1,
-    )(core, hidden)
+        (4,),
+        [pl.BlockSpec((rows, model // 4), lambda i, *_: (0, i))],
+        [pl.BlockSpec((chips // 4, half + ID_ROWS, rows), lambda i, *_: (i, 0, 0))],
+        [((chips, half + ID_ROWS, rows), jnp.float32)],
+        scalars=2,
+    )(core, prompt, hidden)
     return out
 
 
@@ -193,94 +204,154 @@
     return out
 
 
-def split_kernel(core, key, value, upper, lower):
-    half = key.shape[0] // 2
+def split_kernel(core, key, value, out):
+    depth, width = key.shape
+    half = depth // 2
     first = core[0] == 0
-    for start, ref in ((0, key), (key.shape[1], value)):
+    for start, ref in ((0, key), (width, value)):
         x, y = ref[:half], ref[half:]
         for row, part in ((0, jnp.where(first, x, y)), (half, jnp.where(first, y, x))):
-            terms = two_terms(part)
-            for out, term in ((upper, terms[0]), (lower, terms[1])):
-                out[row : row + half, start : start + key.shape[1]] = term
+            upper, lower = two_terms(part)
+            for place, term in enumerate((upper, upper, lower)):
+                top = place * depth + row
+                out[top : top + half, start : start + width] = term
 
 
 def split_weights(core, key, value):
-    shape = ((key.shape[0], 2 * key.shape[1]), jnp.bfloat16)
-    out = pl.BlockSpec(shape[0], lambda *_: (0, 0))
-    return call(
-        split_kernel, "split_weights", (1,), [whole(key), whole(value)], [out] * 2, [shape] * 2, scalars=1
+    shape = ((3 * key.shape[0], 2 * key.shape[1]), jnp.bfloat16)
+    (out,) = call(
+        split_kernel,
+        "split_weights",
+        (1,),
+        [whole(key), whole(value)],
+        [pl.BlockSpec(shape[0], lambda *_: (0, 0))],
+        [shape],
+        scalars=1,
     )(core, key, value)
+    return out
 
 
 def project_kernel(index, *refs):
-    own, other, (upper, lower), outs = refs[:4], refs[4:8], refs[8:10], refs[10:]
-    x = jnp.concatenate(
-        [
-            jnp.concatenate([ref[0] for ref in own], 1),
-            jnp.concatenate([ref[0] for ref in other], 1),
-        ],
-        0,
-    )
-    terms = dot_terms(two_terms(x), (upper[...], lower[...]), ((0,), (0,)))
+    own, other, weights, outs, x = refs[:4], refs[4:8], refs[8], refs[9:11], refs[11]
+
+    @pl.when(pl.program_id(0) == 0)
+    def _():
+        both = jnp.concatenate([beside([ref[0] for ref in own]), beside([ref[0] for ref in other])], 0)
+        upper, lower = two_terms(both)
+        x[...] = jnp.concatenate([upper, lower, upper], 0).T
+
+    terms = dot(x[...], weights[...], ((1,), (0,)))
     count = outs[0].shape[0]
     outs[0][...] = terms[:count]
     outs[1][...] = terms[count:]
 
 
-def project(index, own, other, weight_terms):
-    _, half, plen = own.shape
-    columns = weight_terms[0].shape[1]
+def project(index, own, other, weights):
+    _, rows, plen = own.shape
+    depth, columns = weights.shape
     picked = [
-        pl.BlockSpec((1, half, plen), lambda i, index, q=q: (index[q], 0, 0)) for q in range(4)
+        pl.BlockSpec((1, rows - ID_ROWS, plen), lambda i, index, q=q: (index[q], 0, 0))
+        for q in range(4)
     ]
-    shape = ((2 * plen, columns), jnp.float32)
     return call(
         project_kernel,
         "project",
-        (1,),
-        picked * 2 + [whole(weight_terms[0])] * 2,
-        [pl.BlockSpec(shape[0], lambda *_: (0, 0))] * 2,
-        [shape] * 2,
+        (4,),
+        picked * 2 + [pl.BlockSpec((depth, columns // 4), lambda i, *_: (0, i))],
+        [pl.BlockSpec((2 * plen, columns // 4), lambda i, *_: (0, i))] * 2,
+        [((2 * plen, columns), jnp.float32)] * 2,
         scalars=1,
-    )(index, *([own] * 4), *([other] * 4), *weight_terms)
-
-
-def hidden_grad_kernel(listed, *refs):
-    blocks, (upper, lower), (keep, give) = refs[:-4], refs[-4:-2], refs[-2:]
-    half, plen = keep.shape[1:]
-    weights = upper[...], lower[...]
+        scratch=[pltpu.VMEM((4 * plen, depth), jnp.bfloat16)],
+    )(index, *([own] * 4), *([other] * 4), weights)
+
+
+def weight_times(weights, blocks):
+    depth = weights.shape[0] // 3
+    terms = weights[:depth], weights[2 * depth :]
+    out = []
     for q in range(0, len(blocks), 2):
         x = two_terms(jnp.concatenate([blocks[q][...], blocks[q + 1][...]], 0))
-        terms = dot_terms(weights, x, ((1,), (1,)))
+        out.append(dot_terms(terms, x, ((1,), (1,))))
+    return out
+
+
+def hidden_part_kernel(place, *refs):
+    blocks, weights, (keep, give) = refs[:-3], refs[-3], refs[-2:]
+    half, plen = keep.shape[1:]
+    for q, part in enumerate(weight_times(weights, blocks)):
         for i in range(2):
-            part = terms[:, i * plen : (i + 1) * plen]
-            keep[listed[q + i]] = part[:half]
-            give[listed[q + i]] = part[half:]
-
-
-def hidden_grad(listed, blocks, weight_terms):
-    plen, columns = blocks[0].shape
-    count, half = len(blocks), weight_terms[0].shape[0] // 2
-    shape = ((count, half, plen), jnp.float32)
+            piece = part[:, i * plen : (i + 1) * plen]
+            keep[place[2 * q + i]] = piece[:half]
+            give[place[2 * q + i]] = piece[half:]
+
+
+def hidden_part(place, blocks, weights):
+    shape = ((len(blocks), weights.shape[0] // 6, blocks[0].shape[0]), jnp.float32)
     return call(
-        hidden_grad_kernel,
-        "hidden_grad",
+        hidden_part_kernel,
+        "hidden_part",
         (1,),
-        [whole(blocks[0])] * count + [whole(weight_terms[0])] * 2,
+        [whole(x) for x in blocks] + [whole(weights)],
         [pl.BlockSpec(shape[0], lambda *_: (0, 0, 0))] * 2,
         [shape] * 2,
         scalars=1,
-    )(listed, *blocks, *weight_terms)
+    )(place, *blocks, weights)
+
+
+def hidden_last_kernel(place, keep_in, give_in, *refs):
+    blocks, weights, (keep, give) = refs[:-3], refs[-3], refs[-2:]
+    half, plen = keep.shape[1:]
+    (part,) = weight_times(weights, blocks)
+    for i in range(2):
+        keep[place[i]] = keep_in[i]
+        give[place[i]] = give_in[i]
+        piece = part[:, i * plen : (i + 1) * plen]
+        keep[place[2 + i]] = piece[:half]
+        give[place[2 + i]] = piece[half:]
+
+
+def hidden_last(place, keep, give, blocks, weights):
+    shape = ((4,) + keep.shape[1:], jnp.float32)
+    return call(
+        hidden_last_kernel,
+        "hidden_last",
+        (1,),
+        [whole(keep), whole(give)] + [whole(x) for x in blocks] + [whole(weights)],
+        [pl.BlockSpec(shape[0], lambda *_: (0, 0, 0))] * 2,
+        [shape] * 2,
+        scalars=1,
+    )(place, keep, give, *blocks, weights)
+
+
+def assemble_kernel(listed, *refs):
+    keep, come, out = refs[:4], refs[4:8], refs[8]
+    for k in range(4):
+        for i in range(4):
+            out[listed[4 * k + i]] = keep[k][i] + come[k][i]
+
+
+def assemble(listed, keep, come):
+    shape = ((16,) + keep[0].shape[1:], jnp.float32)
+    (out,) = call(
+        assemble_kernel,
+        "assemble",
+        (1,),
+        [whole(x) for x in keep + come],
+        [pl.BlockSpec(shape[0], lambda *_: (0, 0, 0))],
+        [shape],
+        scalars=1,
+    )(listed, *keep, *come)
+    return out
 
 
 def weight_grad_kernel(listed, core, own, other, *refs):
     blocks, outs = refs[:-2], refs[-2:]
-    half = own.shape[1]
+    half = own.shape[1] - ID_ROWS
     width = outs[0].shape[1]
     total = None
     for q in range(0, len(blocks), 4):
         x = jnp.concatenate(
-            [jnp.concatenate([ref[listed[q + i]] for i in range(4)], 1) for ref in (own, other)], 0
+            [beside([ref[listed[q + i], :half] for i in range(4)]) for ref in (own, other)], 0
         )
         g = jnp.concatenate([ref[...] for ref in blocks[q : q + 4]], 0)
         term = dot_terms(two_terms(x), two_terms(g))
@@ -294,7 +365,7 @@
 
 def weight_grad(listed, core, own, other, blocks):
     plen, columns = blocks[0].shape
-    shape = ((2 * own.shape[1], columns // 2), jnp.float32)
+    shape = ((2 * (own.shape[1] - ID_ROWS), columns // 2), jnp.float32)
     return call(
         weight_grad_kernel,
         "weight_grad",
@@ -349,7 +420,7 @@
     scores = own_scores(length[0], stack(q), k[...], q.shape[0])
     top = jnp.max(scores, -1, keepdims=True)
     expo = jnp.exp(scores - top)
-    unstack(total, dot_terms(two_terms(expo), two_terms(v[...])))
+    unstack(total, dot_columns(two_terms(expo), two_terms(v[...])))
     save_columns(stats, top, jnp.sum(expo, -1, keepdims=True))
 
 
@@ -364,7 +435,7 @@
     inverse = 1.0 / denominator
     prob = expo * inverse
     prob_terms, value_terms = two_terms(prob), two_terms(values)
-    result = (weight * inverse) * stack(total) + dot_terms(prob_terms, value_terms)
+    result = (weight * inverse) * stack(total) + dot_columns(prob_terms, value_terms)
     valid = row_number(result.shape, q.shape[0]) < length[0]
     result = jnp.where(valid, result, 0.0)
     upstream = jnp.where(valid, stack(g), 0.0)
@@ -374,8 +445,8 @@
     unstack(out, result)
     unstack(grad_scores, grad)
     save_columns(stats_out, top + jnp.log(denominator), inner)
-    gk[...] = dot_terms(two_terms(grad), two_terms(query), ((0,), (0,)))
-    gv[...] = dot_terms(prob_terms, upstream_terms, ((0,), (0,)))
+    gk[...] = dot_turned(two_terms(grad), two_terms(query))
+    gv[...] = dot_turned(prob_terms, upstream_terms)
 
 
 def finish_kernel(length, q, g, k, v, kp, grad_scores, stats, gq, gk, gv):
@@ -387,25 +458,30 @@
     upstream_terms = two_terms(upstream)
     grad = prob * (dot_rows(upstream_terms, two_terms(v[...])) - load_column(stats, 8)) * SCALE
     grad_terms = two_terms(grad)
-    prompt_part = dot_terms(two_terms(stack(grad_scores)), two_terms(kp[...]))
-    unstack(gq, prompt_part + dot_terms(grad_terms, two_terms(keys)))
-    gk[...] = dot_terms(grad_terms, two_terms(query), ((0,), (0,)))
-    gv[...] = dot_terms(two_terms(prob), upstream_terms, ((0,), (0,)))
-
-
-def attention(kernel, name, groups, length, ins, outs):
+    prompt_part = dot_columns(two_terms(stack(grad_scores)), two_terms(kp[...]))
+    unstack(gq, prompt_part + dot_columns(grad_terms, two_terms(keys)))
+    gk[...] = dot_turned(grad_terms, two_terms(query))
+    gv[...] = dot_turned(two_terms(prob), upstream_terms)
+
+
+def attention(kernel, name, groups, length, ins, outs, start=0, count=None, into=()):
+    def body(length, *refs):
+        kernel(length, *refs[: len(ins)], *refs[len(ins) + len(into) :])
+
     return call(
-        kernel,
+        body,
         name,
-        (groups,),
+        (groups if count is None else count,),
         [
-            pl.BlockSpec((x.shape[0], size), lambda i, *_, skip=skip: (0, skip + i))
+            pl.BlockSpec((x.shape[0], size), lambda i, *_, skip=skip: (0, skip + start + i))
             for x, size, skip in ins
-        ],
-        [pl.BlockSpec(shape, lambda i, *_: (0, i)) for shape in outs],
+        ]
+        + [pl.BlockSpec(memory_space=pl.ANY)] * len(into),
+        [pl.BlockSpec(shape, lambda i, *_: (0, start + i)) for shape in outs],
         [((rows, groups * size), jnp.float32) for rows, size in outs],
         scalars=1,
-    )(length, *(x for x, _, _ in ins))
+        aliases={1 + len(ins) + i: i for i in range(len(into))},
+    )(length, *(x for x, _, _ in ins), *into)
 
 
 def take_blocks(x, index):
@@ -446,10 +522,7 @@
     wide = PER_GROUP * HEAD_SIZE
 
     if short:
-        all_prompts = jnp.where(jnp.arange(chips) == chip, resp_prompt, 0)
-        for pairs in (ACROSS[1], ACROSS[2], SECOND, THIRD):
-            all_prompts = all_prompts + permute(all_prompts, pairs)
-        mine = lax.all_to_all(turn(here, prompt_hidden, chips), "dp", 0, 0)
+        mine = lax.all_to_all(turn(here, resp_prompt, prompt_hidden, chips), "dp", 0, 0)
         weight_terms = split_weights(here, key_weight, value_weight)
     else:
         all_prompts = lax.all_gather(resp_prompt, "dp", axis=0, tiled=True)
@@ -470,9 +543,10 @@
     )
 
     if short:
-        mine, weight_terms, total, stats, all_prompts = lax.optimization_barrier(
-            (mine, weight_terms, total, stats, all_prompts)
-        )
+        mine, weight_terms, total, stats = lax.optimization_barrier(
+            (mine, weight_terms, total, stats)
+        )
+        all_prompts = mine[:, slice_width // 2, 0].astype(jnp.int32)
         other = lax.ppermute(mine, "mp", SWAP)
         listed = take_small(all_prompts, scatter_order(chip, core))
         pairs = [project(listed[4 * k : 4 * k + 4], mine, other, weight_terms) for k in range(4)]
@@ -493,30 +567,61 @@
         [q, g, prompt_keys, (prompt_rows, HEAD_SIZE, groups), (total, wide, 0), (stats, HEAD_SIZE, 0)],
         [(tokens, wide), (tokens, PER_GROUP * plen), (tokens, HEAD_SIZE)] + [(plen, HEAD_SIZE)] * 2,
     )
-    grad_query, grad_keys, grad_values = attention(
-        finish_kernel,
-        "finish",
-        groups,
-        resp_len,
-        [q, g, (keys_resp, HEAD_SIZE, 0), (response_value_rows, HEAD_SIZE, 0), prompt_keys]
-        + [(grad_scores, PER_GROUP * plen, 0), (stats, HEAD_SIZE, 0)],
-        [(tokens, wide)] + [(tokens, HEAD_SIZE)] * 2,
+    finish_ins = [q, g, (keys_resp, HEAD_SIZE, 0), (response_value_rows, HEAD_SIZE, 0), prompt_keys]
+    finish_ins += [(grad_scores, PER_GROUP * plen, 0), (stats, HEAD_SIZE, 0)]
+    finish_outs = [(tokens, wide)] + [(tokens, HEAD_SIZE)] * 2
+    finish = functools.partial(
+        attention, finish_kernel, "finish", groups, resp_len, finish_ins, finish_outs
     )
 
     own = jnp.concatenate([own_k, own_v], 1)
     if short:
-        gathered = gather_blocks(own)
-        gathered, grad_query, grad_keys, grad_values = lax.optimization_barrier(
-            (gathered, grad_query, grad_keys, grad_values)
-        )
-        listed = take_small(all_prompts, gathered_order(chip, core))
-        keep, give = hidden_grad(listed, gathered, weight_terms)
-        back = lax.all_to_all(keep + lax.ppermute(give, "mp", SWAP), "dp", 0, 0)
-        grad_w_key, grad_w_value = weight_grad(listed, here, mine, other, gathered)
-        back, grad_w_key, grad_w_value = lax.optimization_barrier((back, grad_w_key, grad_w_value))
+        place = gathered_order(chip, core)[:4] ^ chip
+        listed = take_small(all_prompts, chip ^ jnp.arange(chips))
+        far = [own] + [permute(own, ACROSS[k]) for k in range(1, 4)]
+        near, third, both = [permute(own, SECOND)], [permute(own, THIRD)], []
+        keep, give, state = [], [], ()
+
+        def group(k):
+            return [far[k], near[k], third[k], both[k]]
+
+        for k in range(1, 4):
+            done = hidden_part(place, group(0), weight_terms) if k == 3 else None
+            state = finish(start=k - 1, count=1, into=state) if k < 3 else state
+            far[k], near[k - 1], state, done = lax.optimization_barrier(
+                (far[k], near[k - 1], state, done)
+            )
+            both.append(permute(near[k - 1], THIRD))
+            near.append(permute(far[k], SECOND))
+            third.append(permute(far[k], THIRD))
+        parts = [done]
+        near[3], done = lax.optimization_barrier(
+            (near[3], hidden_part(place, group(1), weight_terms))
+        )
+        both.append(permute(near[3], THIRD))
+        parts.append(done)
+        parts.append(hidden_part(place, group(2), weight_terms))
+        come = [lax.ppermute(give, "mp", SWAP) for _, give in parts]
+        pair = hidden_part(jnp.arange(2), [far[3], near[3]], weight_terms)
+        third[3], both[3], parts, come, pair = lax.optimization_barrier(
+            (third[3], both[3], parts, come, pair)
+        )
+        parts.append(hidden_last(place, *pair, [third[3], both[3]], weight_terms))
+        come.append(lax.ppermute(parts[3][1], "mp", SWAP))
+        back = lax.all_to_all(assemble(listed, [x for x, _ in parts], come), "dp", 0, 0)
+
+        order = take_small(all_prompts, gathered_order(chip, core))
+        gathered = [x for k in range(4) for x in group(k)]
+        grad_w_key, grad_w_value = weight_grad(order, here, mine, other, gathered)
+        state = finish(start=2, count=groups - 2, into=state)
+        back, grad_w_key, grad_w_value, state = lax.optimization_barrier(
+            (back, grad_w_key, grad_w_value, state)
+        )
+        grad_query, grad_keys, grad_values = state
         leave = jnp.where(core == 0, back[chips // 2 :], back[: chips // 2])
         grad_hidden = turn_back(here, back, lax.ppermute(leave, "mp", SWAP))
     else:
+        grad_query, grad_keys, grad_values = finish()
         gathered = lax.all_gather(own, "dp", axis=0, tiled=True).reshape(responses, plen, 2 * width)
         summed = jnp.einsum(
             "rtc,rtk->ck", take_blocks(hidden, all_prompts), gathered, precision=HIGH

time: 334 us -> 302 us (0.904)
  waiting for transfers between devices: 166 us -> 109 us
  Pallas kernels: 103 us -> 114 us
  starting transfers between devices: 51.5 us -> 61.7 us
  local copies, waits for them, and re-layouts: 4.76 us -> 9.35 us
    ppermute x33 -> x29, waiting for transfers between devices: 139 us -> 73.6 us  [permute(): return lax.ppermute(x, BOTH, pairs)]
    all_to_all x2, waiting for transfers between devices: 20.2 us -> 31.4 us  [the longest x1 19.2 us: per_device(): lax.all_to_all(turn(here, resp_prompt, prompt_hidden, chips), 'dp', 0, 0)]
    pallas_call x10 -> x17, Pallas kernels: 89.6 us -> 100 us  [the longest x5 44.2 us: attention(): call(body, name, (groups if count is None else count,), [pl.BlockSpec((x....]
    ppermute x1 -> x4, starting transfers between devices: 0.01 us -> 9.05 us  [the longest x3 8.22 us: per_device(): come = [lax.ppermute(give, 'mp', SWAP) for _, give in parts]]
    unnamed x55 -> x69, local copies, waits for them, and re-layouts: 3 us -> 7.1 us
    ppermute x33 -> x29, starting transfers between devices: 36 us -> 35 us  [permute(): return lax.ppermute(x, BOTH, pairs)]
  transfers between devices with their start and end apart: 38 -> 37, of which waited for: 22 -> 17; matrix products, arithmetic and copies ran while one was open for 1% -> 1% of each run, Pallas kernels for 16% -> 25%
where the time goes in v2:
time: 302 us; the launch traced here: 300 us
  Pallas kernels  114 us (38%)
  waiting for transfers between devices  109 us (36%)
  starting transfers between devices  61.7 us (20%)
  local copies, waits for them, and re-layouts  9.35 us (3%)
  other arithmetic  3.91 us (1%)
    ppermute x29, waiting for transfers between devices, permute(): return lax.ppermute(x, BOTH, pairs)  73.6 us
    pallas_call x5, Pallas kernels, attention(): call(body, name, (groups if count is None else count,), [pl.BlockSpec((x....  44.2 us
    ppermute x29, starting transfers between devices, permute(): return lax.ppermute(x, BOTH, pairs)  35 us
    pallas_call x4, Pallas kernels, project(): call(project_kernel, 'project', (4,), picked * 2 + [pl.BlockSpec((depth,...  22.9 us
    all_to_all x1, waiting for transfers between devices, per_device(): lax.all_to_all(turn(here, resp_prompt, prompt_hidden, chips), 'dp', 0, 0)  19.2 us
    pallas_call x4, Pallas kernels, hidden_part(): call(hidden_part_kernel, 'hidden_part', (1,), [whole(x) for x in blocks]...  18.6 us
    all_to_all x1, waiting for transfers between devices, per_device(): lax.all_to_all(assemble(listed, [x for x, _ in parts], come), 'dp', 0, 0)  12.2 us
    pallas_call x1, Pallas kernels, weight_grad(): call(weight_grad_kernel, 'weight_grad', (1,), [whole(own)] * 2 + [whole(b...  9.99 us
  transfers between devices with their start and end apart: 37, of which 17 were waited for; matrix products, arithmetic and copies ran while one was open for 1% of the time, Pallas kernels for 25%

profile of v2, /device:TPU:9, one launch (start us, length us, event | category | flops | bytes accessed | tf_op | source)
XLA Modules:
  0.0 300.4 jit_solution(1167049110709006773)
XLA Ops:
  1.3 4.2 %turn.1 = f32[16,168,128]{2,1,0:T(8,128)} custom-call(s32[1]{0:T(128)} %bitcast.core, s32[1]{0:T(128)S(6)} %copy.36.prompt, f32[128,5120]{1,0:T(8,128)} %x.1), custom_call_target="tpu_custom_call" | custom-call | tf_op jit(solution)/shard_map/turn/pallas_call | solution.py:168
  5.4 6.7 %all-to-all-start = ((f32[16,168,128]{2,1,0:T(8,128)}), f32[16,168,128]{2,1,0:T(8,128)S(1)}, u32[]{:S(2)}, u32[]{:S(2)}) async-start(f32[16,168,128]{2,1,0:T(8,128)} %turn.1), calls=%async_computation | async-start | bytes 2752512 | tf_op jit(solution)/shard_map/all_to_all | solution.py:525
  12.8 2.9 split_weights.1.refs_8_.refs_4_.refs_2_
  15.7 8.6 %open.1 = (f32[256,2560]{1,0:T(8,128)}, f32[256,512]{1,0:T(8,128)}) custom-call(s32[1]{0:T(128)S(6)} %copy.37.length, f32[256,2560]{1,0:T(8,128)} %refs_0_.9, f32[256,512]{1,0:T(8,128)} %refs_2_.7, f32[256,512]{1,0:T(8,128)} %refs_3_.5), custom_call_target="tpu_custom_call" | custom-call | tf_op jit(solution)/shard_map/open/pallas_call | solution.py:471
  24.4 19.2 %all-to-all-done.refs_0_.refs_1_.refs_2_.refs_3_.own = f32[16,168,128]{2,1,0:T(8,128)S(1)} async-done(((f32[16,168,128]{2,1,0:T(8,128)}), f32[16,168,128]{2,1,0:T(8,128)S(1)}, u32[]{:S(2)}, u32[]{:S(2)}) %all-to-all-start) | async-done | bytes 1376288 | tf_op jit(solution)/shard_map/all_to_all | solution.py:525
  43.6 2.7 collective-permute-start
  50.1 5.6 %project.7 = (f32[256,1024]{1,0:T(8,128)}, f32[256,1024]{1,0:T(8,128)}) custom-call(s32[4]{0:T(128)} %get-tuple-element.165.index, f32[16,168,128]{2,1,0:T(8,128)} %copy-done, f32[16,168,128]{2,1,0:T(8,128)} %copy-done, f32[16,168,128]{2,1,0:T(8,128)} %copy-done, f32[16,168,128]{2,1,0:T(8,128)} %copy-done, f32[16,168,128]{2,1,0:T(8,128)} %copy-done.1, ...), custom_call_target="tpu_custom_call" | custom-call | tf_op jit(solution)/shard_map/project/pallas_call | solution.py:256
  56.9 5.7 %project.6 = (f32[256,1024]{1,0:T(8,128)}, f32[256,1024]{1,0:T(8,128)}) custom-call(s32[4]{0:T(128)} %get-tuple-element.166.index, f32[16,168,128]{2,1,0:T(8,128)} %copy-done, f32[16,168,128]{2,1,0:T(8,128)} %copy-done, f32[16,168,128]{2,1,0:T(8,128)} %copy-done, f32[16,168,128]{2,1,0:T(8,128)} %copy-done, f32[16,168,128]{2,1,0:T(8,128)} %copy-done.1, ...), custom_call_target="tpu_custom_call" | custom-call | tf_op jit(solution)/shard_map/project/pallas_call | solution.py:256
  62.9 5.9 %project.5 = (f32[256,1024]{1,0:T(8,128)}, f32[256,1024]{1,0:T(8,128)}) custom-call(s32[4]{0:T(128)} %get-tuple-element.167.index, f32[16,168,128]{2,1,0:T(8,128)} %copy-done, f32[16,168,128]{2,1,0:T(8,128)} %copy-done, f32[16,168,128]{2,1,0:T(8,128)} %copy-done, f32[16,168,128]{2,1,0:T(8,128)} %copy-done, f32[16,168,128]{2,1,0:T(8,128)} %copy-done.1, ...), custom_call_target="tpu_custom_call" | custom-call | tf_op jit(solution)/shard_map/project/pallas_call | solution.py:256
  70.5 5.7 %project.4 = (f32[256,1024]{1,0:T(8,128)}, f32[256,1024]{1,0:T(8,128)}) custom-call(s32[4]{0:T(128)} %get-tuple-element.164.index, f32[16,168,128]{2,1,0:T(8,128)} %copy-done, f32[16,168,128]{2,1,0:T(8,128)} %copy-done, f32[16,168,128]{2,1,0:T(8,128)} %copy-done, f32[16,168,128]{2,1,0:T(8,128)} %copy-done, f32[16,168,128]{2,1,0:T(8,128)} %copy-done.1, ...), custom_call_target="tpu_custom_call" | custom-call | tf_op jit(solution)/shard_map/project/pallas_call | solution.py:256
  77.5 9.3 %collective-permute-done.6 = f32[256,1024]{1,0:T(8,128)S(1)} collective-permute-done((f32[256,1024]{1,0:T(8,128)}, f32[256,1024]{1,0:T(8,128)S(1)}, u32[]{:S(2)}, u32[]{:S(2)}) %collective-permute-start.6) | collective-permute-done | bytes 1048608 | tf_op jit(solution)/shard_map/ppermute | solution.py:45
  88.7 14.9 %collective-permute-done.3 = f32[256,1024]{1,0:T(8,128)S(1)} collective-permute-done((f32[256,1024]{1,0:T(8,128)}, f32[256,1024]{1,0:T(8,128)S(1)}, u32[]{:S(2)}, u32[]{:S(2)}) %collective-permute-start.3) | collective-permute-done | bytes 1048608 | tf_op jit(solution)/shard_map/ppermute | solution.py:45
  105.8 2.5 collective-permute-start.13
  108.3 11.6 %collective-permute-done.1 = f32[256,1024]{1,0:T(8,128)S(1)} collective-permute-done((f32[256,1024]{1,0:T(8,128)}, f32[256,1024]{1,0:T(8,128)S(1)}, u32[]{:S(2)}, u32[]{:S(2)}) %collective-permute-start.1) | collective-permute-done | bytes 1048608 | tf_op jit(solution)/shard_map/ppermute | solution.py:45
  120.6 2.5 collective-permute-start.9
  125.9 2.4 collective-permute-done.2
  128.4 4.8 %collective-permute-done.9 = f32[128,1024]{1,0:T(8,128)S(1)} collective-permute-done((f32[128,1024]{1,0:T(8,128)S(1)}, f32[128,1024]{1,0:T(8,128)S(1)}, u32[]{:S(2)}, u32[]{:S(2)}) %collective-permute-start.9) | collective-permute-done | bytes 524320 | tf_op jit(solution)/shard_map/ppermute | solution.py:45
  133.9 3.9 %collective-permute-done.5 = f32[128,1024]{1,0:T(8,128)S(1)} collective-permute-done((f32[128,1024]{1,0:T(8,128)S(1)}, f32[128,1024]{1,0:T(8,128)S(1)}, u32[]{:S(2)}, u32[]{:S(2)}) %collective-permute-start.5) | collective-permute-done | bytes 524320 | tf_op jit(solution)/shard_map/ppermute | solution.py:45
  138.8 18.0 %close.1 = (f32[256,2560]{1,0:T(8,128)}, f32[256,2560]{1,0:T(8,128)}, f32[256,512]{1,0:T(8,128)}, f32[128,512]{1,0:T(8,128)}, f32[128,512]{1,0:T(8,128)}) custom-call(s32[1]{0:T(128)S(6)} %copy.37.length, f32[256,2560]{1,0:T(8,128)} %refs_0_.9, f32[256,2560]{1,0:T(8,128)} %refs_1_.9, f32[128,1024]{1,0:T(8,128)} %fusion.6.refs_2_.refs_3_.refs_4_, ...), custom_call_target="tpu_custom_call" | custom-call | tf_op jit(solution)/shard_map/close/pallas_call | solution.py:471
  159.3 2.3 collective-permute-start.16
  161.6 4.9 %finish.3 = (f32[256,2560]{1,0:T(8,128)}, f32[256,512]{1,0:T(8,128)}, f32[256,512]{1,0:T(8,128)}) custom-call(s32[1]{0:T(128)S(6)} %copy.37.length, f32[256,2560]{1,0:T(8,128)} %refs_0_.9, f32[256,2560]{1,0:T(8,128)} %refs_1_.9, f32[256,512]{1,0:T(8,128)} %refs_2_.7, f32[256,512]{1,0:T(8,128)} %refs_3_.5, f32[128,1024]{1,0:T(8,128)} %fusion.6.refs_2_.refs_3_.refs_4_, ...), custom_call_target="tpu_custom_call" | custom-call | tf_op jit(solution)/shard_map/finish/pallas_call | solution.py:471
  166.5 10.7 %collective-permute-done.17.refs_0_.refs_4_ = f32[128,1024]{1,0:T(8,128)S(1)} collective-permute-done((f32[128,1024]{1,0:T(8,128)S(1)}, f32[128,1024]{1,0:T(8,128)S(1)}, u32[]{:S(2)}, u32[]{:S(2)}) %collective-permute-start.17) | collective-permute-done | bytes 524320 | tf_op jit(solution)/shard_map/ppermute | solution.py:45
  177.3 3.1 %collective-permute-start.21 = (f32[128,1024]{1,0:T(8,128)S(1)}, f32[128,1024]{1,0:T(8,128)S(1)}, u32[]{:S(2)}, u32[]{:S(2)}) collective-permute-start(f32[128,1024]{1,0:T(8,128)S(1)} %constant_dynamic-update-slice_fusion.refs_0_), channel_id=1, source_target_pairs={{0,2},{1,5},{2,0},{3,7},{4,6},{5,1},{6,4},{7,3},{8,10},{9,13},{10,... | collective-permute-start | bytes 1572872 | tf_op jit(solution)/shard_map/ppermute | solution.py:45
  181.2 4.9 %finish.4 = (f32[256,2560]{1,0:T(8,128)}, f32[256,512]{1,0:T(8,128)}, f32[256,512]{1,0:T(8,128)}) custom-call(s32[1]{0:T(128)S(6)} %copy.37.length, f32[256,2560]{1,0:T(8,128)} %refs_0_.9, f32[256,2560]{1,0:T(8,128)} %refs_1_.9, f32[256,512]{1,0:T(8,128)} %refs_2_.7, ...), custom_call_target="tpu_custom_call", output_to_operand_aliasing={{0}: (8, {}), {1}: (9, {}), {2}: (10, {})} | custom-call | tf_op jit(solution)/shard_map/finish/pallas_call | solution.py:471
  187.0 3.8 %collective-permute-start.25 = (f32[128,1024]{1,0:T(8,128)S(1)}, f32[128,1024]{1,0:T(8,128)S(1)}, u32[]{:S(2)}, u32[]{:S(2)}) collective-permute-start(f32[128,1024]{1,0:T(8,128)S(1)} %collective-permute-done.17.refs_0_.refs_4_), channel_id=1, source_target_pairs={{0,2},{1,5},{2,0},{3,7},{4,6},{5,1},{6,4},{7,3},{8,10},{9,13},{10,... | collective-permute-start | bytes 1572872 | tf_op jit(solution)/shard_map/ppermute | solution.py:45
  192.1 6.4 %collective-permute-done.22.refs_3_ = f32[128,1024]{1,0:T(8,128)S(1)} collective-permute-done((f32[128,1024]{1,0:T(8,128)S(1)}, f32[128,1024]{1,0:T(8,128)S(1)}, u32[]{:S(2)}, u32[]{:S(2)}) %collective-permute-start.22) | collective-permute-done | bytes 524320 | tf_op jit(solution)/shard_map/ppermute | solution.py:45
  199.3 4.9 %hidden_part.4 = (f32[4,160,128]{2,1,0:T(8,128)}, f32[4,160,128]{2,1,0:T(8,128)}) custom-call(s32[4]{0:T(128)} %xor_bitcast_fusion.place, f32[128,1024]{1,0:T(8,128)} %copy-done.3, f32[128,1024]{1,0:T(8,128)} %copy-done.5, f32[128,1024]{1,0:T(8,128)} %copy-done.8, f32[128,1024]{1,0:T(8,128)} %copy-done.10, bf16[960,1024]{1,0:T(8,128)(2,1)} %split_weights.1.refs_8_.refs_4_.refs_2_), custom_call_target="tpu_custom_call" | custom-call | tf_op jit(solution)/shard_map/hidden_part/pallas_call | solution.py:290
  204.2 2.2 collective-permute-done.15.refs_0_.refs_12_
  206.4 1.6 collective-permute-start.24
  208.0 2.0 collective-permute-start.28
  211.5 3.8 %collective-permute-done.26.refs_3_.refs_7_ = f32[128,1024]{1,0:T(8,128)S(1)} collective-permute-done((f32[128,1024]{1,0:T(8,128)S(1)}, f32[128,1024]{1,0:T(8,128)S(1)}, u32[]{:S(2)}, u32[]{:S(2)}) %collective-permute-start.26) | collective-permute-done | bytes 524320 | tf_op jit(solution)/shard_map/ppermute | solution.py:45
  216.2 4.9 %hidden_part.5 = (f32[4,160,128]{2,1,0:T(8,128)}, f32[4,160,128]{2,1,0:T(8,128)}) custom-call(s32[4]{0:T(128)} %xor_bitcast_fusion.place, f32[128,1024]{1,0:T(8,128)} %copy-done.4, f32[128,1024]{1,0:T(8,128)} %copy-done.7, f32[128,1024]{1,0:T(8,128)} %copy-done.12, f32[128,1024]{1,0:T(8,128)} %copy-done.13, ...), custom_call_target="tpu_custom_call" | custom-call | tf_op jit(solution)/shard_map/hidden_part/pallas_call | solution.py:290
  221.1 1.5 collective-permute-start.27
  222.6 6.6 %collective-permute-start.30 = (f32[4,160,128]{2,1,0:T(8,128)S(1)}, f32[4,160,128]{2,1,0:T(8,128)S(1)}, u32[]{:S(2)}, u32[]{:S(2)}) collective-permute-start(f32[4,160,128]{2,1,0:T(8,128)S(1)} %copy-done.32), channel_id=1, source_target_pairs={{0,1},{1,0},{2,3},{3,2},{4,5},{5,4},{6,7},{7,6},{8,9},{9,8},{10,11... | collective-permute-start | bytes 983048 | tf_op jit(solution)/shard_map/ppermute | solution.py:604
  229.3 2.9 collective-permute-done.29.refs_3_.refs_11_
  233.0 4.9 %hidden_part.6 = (f32[4,160,128]{2,1,0:T(8,128)}, f32[4,160,128]{2,1,0:T(8,128)}) custom-call(s32[4]{0:T(128)} %xor_bitcast_fusion.place, f32[128,1024]{1,0:T(8,128)} %copy-done.6, f32[128,1024]{1,0:T(8,128)} %copy-done.11, f32[128,1024]{1,0:T(8,128)} %copy-done.15, f32[128,1024]{1,0:T(8,128)} %copy-done.16, ...), custom_call_target="tpu_custom_call" | custom-call | tf_op jit(solution)/shard_map/hidden_part/pallas_call | solution.py:290
  237.9 1.5 collective-permute-start.32
  240.0 3.9 %hidden_part.7 = (f32[2,160,128]{2,1,0:T(8,128)}, f32[2,160,128]{2,1,0:T(8,128)}) custom-call(s32[2]{0:T(128)} %iota.28.place, f32[128,1024]{1,0:T(8,128)} %copy-done.9, f32[128,1024]{1,0:T(8,128)} %copy-done.14, bf16[960,1024]{1,0:T(8,128)(2,1)} %split_weights.1.refs_8_.refs_4_.refs_2_), custom_call_target="tpu_custom_call" | custom-call | tf_op jit(solution)/shard_map/hidden_part/pallas_call | solution.py:290
  244.9 4.2 %hidden_last.1 = (f32[4,160,128]{2,1,0:T(8,128)}, f32[4,160,128]{2,1,0:T(8,128)}) custom-call(s32[4]{0:T(128)} %xor_bitcast_fusion.place, f32[2,160,128]{2,1,0:T(8,128)} %get-tuple-element.136.keep_in, f32[2,160,128]{2,1,0:T(8,128)} %get-tuple-element.137.give_in, f32[128,1024]{1,0:T(8,128)} %copy-done.17, f32[128,1024]{1,0:T(8,128)} %copy-done.18, ...), custom_call_target="tpu_custom_call" | custom-call | tf_op jit(solution)/shard_map/hidden_last/pallas_call | solution.py:315
  250.0 1.5 collective-permute-done.33.refs_7_
  252.2 3.5 %assemble.1 = f32[16,160,128]{2,1,0:T(8,128)} custom-call(s32[16]{0:T(128)} %get-tuple-element.160.listed, f32[4,160,128]{2,1,0:T(8,128)} %get-tuple-element.133.refs_0_, f32[4,160,128]{2,1,0:T(8,128)} %get-tuple-element.134.refs_1_, f32[4,160,128]{2,1,0:T(8,128)} %get-tuple-element.135.refs_2_, f32[4,160,128]{2,1,0:T(8,128)} %get-tuple-element.140.refs_3_, ...), custom_call_target="tpu_custom_call" | custom-call | tf_op jit(solution)/shard_map/assemble/pallas_call | solution.py:335
  255.7 5.6 %all-to-all-start.1 = ((f32[16,160,128]{2,1,0:T(8,128)}), f32[16,160,128]{2,1,0:T(8,128)S(1)}, u32[]{:S(2)}, u32[]{:S(2)}) async-start(f32[16,160,128]{2,1,0:T(8,128)} %assemble.1), calls=%async_computation.1 | async-start | bytes 2621440 | tf_op jit(solution)/shard_map/all_to_all | solution.py:611
  261.3 7.7 %finish.5 = (f32[256,2560]{1,0:T(8,128)}, f32[256,512]{1,0:T(8,128)}, f32[256,512]{1,0:T(8,128)}) custom-call(s32[1]{0:T(128)S(6)} %copy.37.length, f32[256,2560]{1,0:T(8,128)} %refs_0_.9, f32[256,2560]{1,0:T(8,128)} %refs_1_.9, f32[256,512]{1,0:T(8,128)} %refs_2_.7, ...), custom_call_target="tpu_custom_call", output_to_operand_aliasing={{0}: (8, {}), {1}: (9, {}), {2}: (10, {})} | custom-call | tf_op jit(solution)/shard_map/finish/pallas_call | solution.py:471
  269.0 10.0 %weight_grad.1 = (f32[320,512]{1,0:T(8,128)}, f32[320,512]{1,0:T(8,128)}) custom-call(s32[16]{0:T(128)} %get-tuple-element.159.listed, s32[1]{0:T(128)} %bitcast.core, f32[16,168,128]{2,1,0:T(8,128)} %copy-done, f32[16,168,128]{2,1,0:T(8,128)} %copy-done.1, f32[128,1024]{1,0:T(8,128)} %copy-done.3, f32[128,1024]{1,0:T(8,128)} %copy-done.5, ...), custom_call_target="tpu_custom_call" | custom-call | tf_op jit(solution)/shard_map/weight_grad/pallas_call | solution.py:369
  279.0 12.2 %all-to-all-done.1.own = f32[16,160,128]{2,1,0:T(8,128)S(1)} async-done(((f32[16,160,128]{2,1,0:T(8,128)}), f32[16,160,128]{2,1,0:T(8,128)S(1)}, u32[]{:S(2)}, u32[]{:S(2)}) %all-to-all-start.1) | async-done | bytes 1310752 | tf_op jit(solution)/shard_map/all_to_all | solution.py:611
  291.3 2.6 collective-permute-start.34
  294.0 1.7 collective-permute-done.34.other
  296.5 3.8 %turn_back.1 = f32[128,2560]{1,0:T(8,128)} custom-call(s32[1]{0:T(128)} %bitcast.core, f32[16,160,128]{2,1,0:T(8,128)} %copy-done.2, f32[8,160,128]{2,1,0:T(8,128)} %copy-done.23), custom_call_target="tpu_custom_call" | custom-call | tf_op jit(solution)/shard_map/turn_back/pallas_call | solution.py:192
  (141 shorter events, 31.3 us)
Async XLA Ops:
  5.4 38.1 %all-to-all-start = ((f32[16,168,128]{2,1,0:T(8,128)}), f32[16,168,128]{2,1,0:T(8,128)S(1)}, u32[]{:S(2)}, u32[]{:S(2)}) async-start(f32[16,168,128]{2,1,0:T(8,128)} %turn.1), calls=%async_computation | async-start | bytes 2752512 | tf_op jit(solution)/shard_map/all_to_all | solution.py:525
  15.6 30.6 %copy-start.29 = (s32[4]{0:T(128)S(1)}, s32[4]{0:T(128)}, u32[]{:S(2)}) copy-start(s32[4]{0:T(128)} %constant.39.clone) | copy-start | bytes 52
  15.7 30.6 %copy-start.30 = (s32[4]{0:T(128)S(1)}, s32[4]{0:T(128)}, u32[]{:S(2)}) copy-start(s32[4]{0:T(128)} %constant.40.clone) | copy-start | bytes 52
  15.7 30.6 %copy-start.31 = (s32[4]{0:T(128)S(1)}, s32[4]{0:T(128)}, u32[]{:S(2)}) copy-start(s32[4]{0:T(128)} %constant.41.clone) | copy-start | bytes 52
  43.6 5.4 %collective-permute-start = (f32[16,168,128]{2,1,0:T(8,128)S(1)}, f32[16,168,128]{2,1,0:T(8,128)S(1)}, u32[]{:S(2)}, u32[]{:S(2)}) collective-permute-start(f32[16,168,128]{2,1,0:T(8,128)S(1)} %all-to-all-done.refs_0_.refs_1_.refs_2_.refs_3_.own), channel_id=1, source_target_pairs={{0,1},{1,0},{2,3},{3,2},{4,5},{5,4},{6,7},{7,6},{8,9},{9,8},{10,11... | collective-permute-start | bytes 4128776 | tf_op jit(solution)/shard_map/ppermute | solution.py:550
  55.7 14.2 %collective-permute-start.10 = (f32[256,1024]{1,0:T(8,128)}, f32[256,1024]{1,0:T(8,128)S(1)}, u32[]{:S(2)}, u32[]{:S(2)}) collective-permute-start(f32[256,1024]{1,0:T(8,128)} %get-tuple-element.94), channel_id=1, source_target_pairs={{0,2},{1,5},{2,0},{3,7},{4,6},{5,1},{6,4},{7,3},{8,10},{9,13},{10,... | collective-permute-start | bytes 3145736 | tf_op jit(solution)/shard_map/ppermute | solution.py:45
  62.6 24.1 %collective-permute-start.6 = (f32[256,1024]{1,0:T(8,128)}, f32[256,1024]{1,0:T(8,128)S(1)}, u32[]{:S(2)}, u32[]{:S(2)}) collective-permute-start(f32[256,1024]{1,0:T(8,128)} %get-tuple-element.92), channel_id=1, source_target_pairs={{0,2},{1,5},{2,0},{3,7},{4,6},{5,1},{6,4},{7,3},{8,10},{9,13},{10,... | collective-permute-start | bytes 3145736 | tf_op jit(solution)/shard_map/ppermute | solution.py:45
  68.7 34.8 %collective-permute-start.3 = (f32[256,1024]{1,0:T(8,128)}, f32[256,1024]{1,0:T(8,128)S(1)}, u32[]{:S(2)}, u32[]{:S(2)}) collective-permute-start(f32[256,1024]{1,0:T(8,128)} %get-tuple-element.90), channel_id=1, source_target_pairs={{0,2},{1,5},{2,0},{3,7},{4,6},{5,1},{6,4},{7,3},{8,10},{9,13},{10,... | collective-permute-start | bytes 3145736 | tf_op jit(solution)/shard_map/ppermute | solution.py:45
  70.0 17.3 %collective-permute-start.11 = (f32[128,1024]{1,0:T(8,128)S(1)}, f32[128,1024]{1,0:T(8,128)S(1)}, u32[]{:S(2)}, u32[]{:S(2)}) collective-permute-start(f32[128,1024]{1,0:T(8,128)S(1)} %slice_add_fusion), channel_id=1, source_target_pairs={{0,4},{1,3},{2,6},{3,1},{4,0},{5,7},{6,2},{7,5},{8,12},{9,11},{10,... | collective-permute-start | bytes 1572872 | tf_op jit(solution)/shard_map/ppermute | solution.py:45
  76.3 27.3 %copy-start.20 = (f32[256,1024]{1,0:T(8,128)S(1)}, f32[256,1024]{1,0:T(8,128)}, u32[]{:S(2)}) copy-start(f32[256,1024]{1,0:T(8,128)} %get-tuple-element.89) | copy-start | bytes 3145732
  76.3 43.6 %collective-permute-start.1 = (f32[256,1024]{1,0:T(8,128)}, f32[256,1024]{1,0:T(8,128)S(1)}, u32[]{:S(2)}, u32[]{:S(2)}) collective-permute-start(f32[256,1024]{1,0:T(8,128)} %get-tuple-element.88), channel_id=1, source_target_pairs={{0,2},{1,5},{2,0},{3,7},{4,6},{5,1},{6,4},{7,3},{8,10},{9,13},{10,... | collective-permute-start | bytes 3145736 | tf_op jit(solution)/shard_map/ppermute | solution.py:45
  86.8 16.9 %collective-permute-start.7 = (f32[128,1024]{1,0:T(8,128)S(1)}, f32[128,1024]{1,0:T(8,128)S(1)}, u32[]{:S(2)}, u32[]{:S(2)}) collective-permute-start(f32[128,1024]{1,0:T(8,128)S(1)} %slice_add_fusion.2), channel_id=1, source_target_pairs={{0,4},{1,3},{2,6},{3,1},{4,0},{5,7},{6,2},{7,5},{8,12},{9,11},{10,... | collective-permute-start | bytes 1572872 | tf_op jit(solution)/shard_map/ppermute | solution.py:45
  87.4 18.3 %collective-permute-start.12 = (f32[128,1024]{1,0:T(8,128)S(1)}, f32[128,1024]{1,0:T(8,128)S(1)}, u32[]{:S(2)}, u32[]{:S(2)}) collective-permute-start(f32[128,1024]{1,0:T(8,128)S(1)} %fusion), channel_id=1, source_target_pairs={{0,8},{1,9},{2,10},{3,11},{4,12},{5,13},{6,14},{7,15},{24,16},{25,... | collective-permute-start | bytes 1572872 | tf_op jit(solution)/shard_map/ppermute | solution.py:45
  103.7 16.8 %collective-permute-start.8 = (f32[128,1024]{1,0:T(8,128)S(1)}, f32[128,1024]{1,0:T(8,128)S(1)}, u32[]{:S(2)}, u32[]{:S(2)}) collective-permute-start(f32[128,1024]{1,0:T(8,128)S(1)} %fusion.1), channel_id=1, source_target_pairs={{0,8},{1,9},{2,10},{3,11},{4,12},{5,13},{6,14},{7,15},{24,16},{25,... | collective-permute-start | bytes 1572872 | tf_op jit(solution)/shard_map/ppermute | solution.py:45
  105.2 17.9 %collective-permute-start.4 = (f32[128,1024]{1,0:T(8,128)S(1)}, f32[128,1024]{1,0:T(8,128)S(1)}, u32[]{:S(2)}, u32[]{:S(2)}) collective-permute-start(f32[128,1024]{1,0:T(8,128)S(1)} %slice_add_fusion.4), channel_id=1, source_target_pairs={{0,4},{1,3},{2,6},{3,1},{4,0},{5,7},{6,2},{7,5},{8,12},{9,11},{10,... | collective-permute-start | bytes 1572872 | tf_op jit(solution)/shard_map/ppermute | solution.py:45
  105.8 17.3 %collective-permute-start.13 = (f32[128,1024]{1,0:T(8,128)S(1)}, f32[128,1024]{1,0:T(8,128)S(1)}, u32[]{:S(2)}, u32[]{:S(2)}) collective-permute-start(f32[128,1024]{1,0:T(8,128)S(1)} %add.94), channel_id=1, source_target_pairs={{8,16},{9,17},{10,18},{11,19},{12,20},{13,21},{14,22},{15,23},{16,... | collective-permute-start | bytes 1572872 | tf_op jit(solution)/shard_map/ppermute | solution.py:45
  120.0 8.4 %collective-permute-start.2 = (f32[128,1024]{1,0:T(8,128)S(1)}, f32[128,1024]{1,0:T(8,128)S(1)}, u32[]{:S(2)}, u32[]{:S(2)}) collective-permute-start(f32[128,1024]{1,0:T(8,128)S(1)} %slice_add_fusion.6), channel_id=1, source_target_pairs={{0,4},{1,3},{2,6},{3,1},{4,0},{5,7},{6,2},{7,5},{8,12},{9,11},{10,... | collective-permute-start | bytes 1572872 | tf_op jit(solution)/shard_map/ppermute | solution.py:45
  120.6 12.5 %collective-permute-start.9 = (f32[128,1024]{1,0:T(8,128)S(1)}, f32[128,1024]{1,0:T(8,128)S(1)}, u32[]{:S(2)}, u32[]{:S(2)}) collective-permute-start(f32[128,1024]{1,0:T(8,128)S(1)} %add.89), channel_id=1, source_target_pairs={{8,16},{9,17},{10,18},{11,19},{12,20},{13,21},{14,22},{15,23},{16,... | collective-permute-start | bytes 1572872 | tf_op jit(solution)/shard_map/ppermute | solution.py:45
  123.3 10.6 %collective-permute-start.14 = (f32[128,1024]{1,0:T(8,128)S(1)}, f32[128,1024]{1,0:T(8,128)S(1)}, u32[]{:S(2)}, u32[]{:S(2)}) collective-permute-start(f32[128,1024]{1,0:T(8,128)S(1)} %get-tuple-element.162), channel_id=1, source_target_pairs={{8,0},{9,1},{10,2},{11,3},{12,4},{13,5},{14,6},{15,7},{16,24},{17,... | collective-permute-start | bytes 1572872 | tf_op jit(solution)/shard_map/ppermute | solution.py:45
  124.6 13.1 %collective-permute-start.5 = (f32[128,1024]{1,0:T(8,128)S(1)}, f32[128,1024]{1,0:T(8,128)S(1)}, u32[]{:S(2)}, u32[]{:S(2)}) collective-permute-start(f32[128,1024]{1,0:T(8,128)S(1)} %get-tuple-element.163), channel_id=1, source_target_pairs={{0,8},{1,9},{2,10},{3,11},{4,12},{5,13},{6,14},{7,15},{24,16},{25,... | collective-permute-start | bytes 1572872 | tf_op jit(solution)/shard_map/ppermute | solution.py:45
  158.8 21.6 %copy-start.3 = (f32[128,1024]{1,0:T(8,128)}, f32[128,1024]{1,0:T(8,128)S(1)}, u32[]{:S(2)}) copy-start(f32[128,1024]{1,0:T(8,128)S(1)} %constant_dynamic-update-slice_fusion.refs_0_) | copy-start | bytes 1572868
  158.8 18.4 %collective-permute-start.17 = (f32[128,1024]{1,0:T(8,128)S(1)}, f32[128,1024]{1,0:T(8,128)S(1)}, u32[]{:S(2)}, u32[]{:S(2)}) collective-permute-start(f32[128,1024]{1,0:T(8,128)S(1)} %constant_dynamic-update-slice_fusion.refs_0_), channel_id=1, source_target_pairs={{0,8},{1,9},{2,10},{3,11},{4,12},{5,13},{6,14},{7,15},{8,0},{9,1},... | collective-permute-start | bytes 1572872 | tf_op jit(solution)/shard_map/ppermute | solution.py:45
  158.9 18.3 %collective-permute-start.18 = (f32[128,1024]{1,0:T(8,128)S(1)}, f32[128,1024]{1,0:T(8,128)S(1)}, u32[]{:S(2)}, u32[]{:S(2)}) collective-permute-start(f32[128,1024]{1,0:T(8,128)S(1)} %constant_dynamic-update-slice_fusion.refs_0_), channel_id=1, source_target_pairs={{0,4},{1,3},{2,6},{3,1},{4,0},{5,7},{6,2},{7,5},{8,12},{9,11},{10,... | collective-permute-start | bytes 1572872 | tf_op jit(solution)/shard_map/ppermute | solution.py:45
  159.3 26.8 %collective-permute-start.16 = (f32[128,1024]{1,0:T(8,128)S(1)}, f32[128,1024]{1,0:T(8,128)S(1)}, u32[]{:S(2)}, u32[]{:S(2)}) collective-permute-start(f32[128,1024]{1,0:T(8,128)S(1)} %constant_dynamic-update-slice_fusion.refs_0_), channel_id=1, source_target_pairs={{0,16},{1,17},{2,18},{3,19},{4,20},{5,21},{6,22},{7,23},{8,24},{9,... | collective-permute-start | bytes 1572872 | tf_op jit(solution)/shard_map/ppermute | solution.py:45
  177.2 9.0 %collective-permute-start.19 = (f32[128,1024]{1,0:T(8,128)S(1)}, f32[128,1024]{1,0:T(8,128)S(1)}, u32[]{:S(2)}, u32[]{:S(2)}) collective-permute-start(f32[128,1024]{1,0:T(8,128)S(1)} %collective-permute-done.17.refs_0_.refs_4_), channel_id=1, source_target_pairs={{0,4},{1,3},{2,6},{3,1},{4,0},{5,7},{6,2},{7,5},{8,12},{9,11},{10,... | collective-permute-start | bytes 1572872 | tf_op jit(solution)/shard_map/ppermute | solution.py:45
  177.3 13.5 %collective-permute-start.21 = (f32[128,1024]{1,0:T(8,128)S(1)}, f32[128,1024]{1,0:T(8,128)S(1)}, u32[]{:S(2)}, u32[]{:S(2)}) collective-permute-start(f32[128,1024]{1,0:T(8,128)S(1)} %constant_dynamic-update-slice_fusion.refs_0_), channel_id=1, source_target_pairs={{0,2},{1,5},{2,0},{3,7},{4,6},{5,1},{6,4},{7,3},{8,10},{9,13},{10,... | collective-permute-start | bytes 1572872 | tf_op jit(solution)/shard_map/ppermute | solution.py:45
  180.4 26.0 %collective-permute-start.15 = (f32[128,1024]{1,0:T(8,128)S(1)}, f32[128,1024]{1,0:T(8,128)S(1)}, u32[]{:S(2)}, u32[]{:S(2)}) collective-permute-start(f32[128,1024]{1,0:T(8,128)S(1)} %constant_dynamic-update-slice_fusion.refs_0_), channel_id=1, source_target_pairs={{0,24},{1,25},{2,26},{3,27},{4,28},{5,29},{6,30},{7,31},{8,16},{9,... | collective-permute-start | bytes 1572872 | tf_op jit(solution)/shard_map/ppermute | solution.py:45
  181.1 17.4 %collective-permute-start.22 = (f32[128,1024]{1,0:T(8,128)S(1)}, f32[128,1024]{1,0:T(8,128)S(1)}, u32[]{:S(2)}, u32[]{:S(2)}) collective-permute-start(f32[128,1024]{1,0:T(8,128)S(1)} %collective-permute-done.18.refs_1_), channel_id=1, source_target_pairs={{0,2},{1,5},{2,0},{3,7},{4,6},{5,1},{6,4},{7,3},{8,10},{9,13},{10,... | collective-permute-start | bytes 1572872 | tf_op jit(solution)/shard_map/ppermute | solution.py:45
  186.1 35.0 %copy-start.6 = (f32[128,1024]{1,0:T(8,128)}, f32[128,1024]{1,0:T(8,128)S(1)}, u32[]{:S(2)}) copy-start(f32[128,1024]{1,0:T(8,128)S(1)} %collective-permute-done.16.refs_0_.refs_8_) | copy-start | bytes 1572868
  186.1 29.2 %copy-start.7 = (f32[128,1024]{1,0:T(8,128)}, f32[128,1024]{1,0:T(8,128)S(1)}, u32[]{:S(2)}) copy-start(f32[128,1024]{1,0:T(8,128)S(1)} %collective-permute-done.19.refs_1_.refs_5_) | copy-start | bytes 1572868
  186.2 20.3 %collective-permute-start.20 = (f32[128,1024]{1,0:T(8,128)S(1)}, f32[128,1024]{1,0:T(8,128)S(1)}, u32[]{:S(2)}, u32[]{:S(2)}) collective-permute-start(f32[128,1024]{1,0:T(8,128)S(1)} %collective-permute-done.16.refs_0_.refs_8_), channel_id=1, source_target_pairs={{0,4},{1,3},{2,6},{3,1},{4,0},{5,7},{6,2},{7,5},{8,12},{9,11},{10,... | collective-permute-start | bytes 1572872 | tf_op jit(solution)/shard_map/ppermute | solution.py:45
  187.0 23.1 %collective-permute-start.25 = (f32[128,1024]{1,0:T(8,128)S(1)}, f32[128,1024]{1,0:T(8,128)S(1)}, u32[]{:S(2)}, u32[]{:S(2)}) collective-permute-start(f32[128,1024]{1,0:T(8,128)S(1)} %collective-permute-done.17.refs_0_.refs_4_), channel_id=1, source_target_pairs={{0,2},{1,5},{2,0},{3,7},{4,6},{5,1},{6,4},{7,3},{8,10},{9,13},{10,... | collective-permute-start | bytes 1572872 | tf_op jit(solution)/shard_map/ppermute | solution.py:45
  190.9 24.5 %collective-permute-start.26 = (f32[128,1024]{1,0:T(8,128)S(1)}, f32[128,1024]{1,0:T(8,128)S(1)}, u32[]{:S(2)}, u32[]{:S(2)}) collective-permute-start(f32[128,1024]{1,0:T(8,128)S(1)} %collective-permute-done.19.refs_1_.refs_5_), channel_id=1, source_target_pairs={{0,2},{1,5},{2,0},{3,7},{4,6},{5,1},{6,4},{7,3},{8,10},{9,13},{10,... | collective-permute-start | bytes 1572872 | tf_op jit(solution)/shard_map/ppermute | solution.py:45
  204.2 18.4 %copy-start.32 = (f32[4,160,128]{2,1,0:T(8,128)S(1)}, f32[4,160,128]{2,1,0:T(8,128)}, u32[]{:S(2)}) copy-start(f32[4,160,128]{2,1,0:T(8,128)} %get-tuple-element.125) | copy-start | bytes 983044
  206.4 31.5 %copy-start.9 = (f32[128,1024]{1,0:T(8,128)}, f32[128,1024]{1,0:T(8,128)S(1)}, u32[]{:S(2)}) copy-start(f32[128,1024]{1,0:T(8,128)S(1)} %collective-permute-done.15.refs_0_.refs_12_) | copy-start | bytes 1572868
  206.4 25.8 %copy-start.11 = (f32[128,1024]{1,0:T(8,128)}, f32[128,1024]{1,0:T(8,128)S(1)}, u32[]{:S(2)}) copy-start(f32[128,1024]{1,0:T(8,128)S(1)} %collective-permute-done.20.refs_1_.refs_9_) | copy-start | bytes 1572868
  206.4 14.7 %collective-permute-start.24 = (f32[128,1024]{1,0:T(8,128)S(1)}, f32[128,1024]{1,0:T(8,128)S(1)}, u32[]{:S(2)}, u32[]{:S(2)}) collective-permute-start(f32[128,1024]{1,0:T(8,128)S(1)} %collective-permute-done.15.refs_0_.refs_12_), channel_id=1, source_target_pairs={{0,4},{1,3},{2,6},{3,1},{4,0},{5,7},{6,2},{7,5},{8,12},{9,11},{10,... | collective-permute-start | bytes 1572872 | tf_op jit(solution)/shard_map/ppermute | solution.py:45
  208.0 21.3 %collective-permute-start.28 = (f32[128,1024]{1,0:T(8,128)S(1)}, f32[128,1024]{1,0:T(8,128)S(1)}, u32[]{:S(2)}, u32[]{:S(2)}) collective-permute-start(f32[128,1024]{1,0:T(8,128)S(1)} %collective-permute-done.16.refs_0_.refs_8_), channel_id=1, source_target_pairs={{0,2},{1,5},{2,0},{3,7},{4,6},{5,1},{6,4},{7,3},{8,10},{9,13},{10,... | collective-permute-start | bytes 1572872 | tf_op jit(solution)/shard_map/ppermute | solution.py:45
  210.1 22.2 %collective-permute-start.29 = (f32[128,1024]{1,0:T(8,128)S(1)}, f32[128,1024]{1,0:T(8,128)S(1)}, u32[]{:S(2)}, u32[]{:S(2)}) collective-permute-start(f32[128,1024]{1,0:T(8,128)S(1)} %collective-permute-done.20.refs_1_.refs_9_), channel_id=1, source_target_pairs={{0,2},{1,5},{2,0},{3,7},{4,6},{5,1},{6,4},{7,3},{8,10},{9,13},{10,... | collective-permute-start | bytes 1572872 | tf_op jit(solution)/shard_map/ppermute | solution.py:45
  210.1 33.8 %collective-permute-start.23 = (f32[128,1024]{1,0:T(8,128)S(1)}, f32[128,1024]{1,0:T(8,128)S(1)}, u32[]{:S(2)}, u32[]{:S(2)}) collective-permute-start(f32[128,1024]{1,0:T(8,128)S(1)} %collective-permute-done.15.refs_0_.refs_12_), channel_id=1, source_target_pairs={{0,2},{1,5},{2,0},{3,7},{4,6},{5,1},{6,4},{7,3},{8,10},{9,13},{10,... | collective-permute-start | bytes 1572872 | tf_op jit(solution)/shard_map/ppermute | solution.py:45
  221.1 18.9 %copy-start.14 = (f32[128,1024]{1,0:T(8,128)}, f32[128,1024]{1,0:T(8,128)S(1)}, u32[]{:S(2)}) copy-start(f32[128,1024]{1,0:T(8,128)S(1)} %collective-permute-done.24.refs_1_.refs_13_) | copy-start | bytes 1572868
  221.1 22.9 %collective-permute-start.27 = (f32[128,1024]{1,0:T(8,128)S(1)}, f32[128,1024]{1,0:T(8,128)S(1)}, u32[]{:S(2)}, u32[]{:S(2)}) collective-permute-start(f32[128,1024]{1,0:T(8,128)S(1)} %collective-permute-done.24.refs_1_.refs_13_), channel_id=1, source_target_pairs={{0,2},{1,5},{2,0},{3,7},{4,6},{5,1},{6,4},{7,3},{8,10},{9,13},{10,... | collective-permute-start | bytes 1572872 | tf_op jit(solution)/shard_map/ppermute | solution.py:45
  222.6 21.3 %collective-permute-start.30 = (f32[4,160,128]{2,1,0:T(8,128)S(1)}, f32[4,160,128]{2,1,0:T(8,128)S(1)}, u32[]{:S(2)}, u32[]{:S(2)}) collective-permute-start(f32[4,160,128]{2,1,0:T(8,128)S(1)} %copy-done.32), channel_id=1, source_target_pairs={{0,1},{1,0},{2,3},{3,2},{4,5},{5,4},{6,7},{7,6},{8,9},{9,8},{10,11... | collective-permute-start | bytes 983048 | tf_op jit(solution)/shard_map/ppermute | solution.py:604
  237.9 6.1 %collective-permute-start.32 = (f32[4,160,128]{2,1,0:T(8,128)}, f32[4,160,128]{2,1,0:T(8,128)S(1)}, u32[]{:S(2)}, u32[]{:S(2)}) collective-permute-start(f32[4,160,128]{2,1,0:T(8,128)} %get-tuple-element.130), channel_id=1, source_target_pairs={{0,1},{1,0},{2,3},{3,2},{4,5},{5,4},{6,7},{7,6},{8,9},{9,8},{10,11... | collective-permute-start | bytes 983048 | tf_op jit(solution)/shard_map/ppermute | solution.py:604
  239.4 4.6 %collective-permute-start.31 = (f32[4,160,128]{2,1,0:T(8,128)S(1)}, f32[4,160,128]{2,1,0:T(8,128)S(1)}, u32[]{:S(2)}, u32[]{:S(2)}) collective-permute-start(f32[4,160,128]{2,1,0:T(8,128)S(1)} %copy-done.33), channel_id=1, source_target_pairs={{0,1},{1,0},{2,3},{3,2},{4,5},{5,4},{6,7},{7,6},{8,9},{9,8},{10,11... | collective-permute-start | bytes 983048 | tf_op jit(solution)/shard_map/ppermute | solution.py:604
  249.1 2.3 collective-permute-start.33
  255.7 35.6 %all-to-all-start.1 = ((f32[16,160,128]{2,1,0:T(8,128)}), f32[16,160,128]{2,1,0:T(8,128)S(1)}, u32[]{:S(2)}, u32[]{:S(2)}) async-start(f32[16,160,128]{2,1,0:T(8,128)} %assemble.1), calls=%async_computation.1 | async-start | bytes 2621440 | tf_op jit(solution)/shard_map/all_to_all | solution.py:611
  291.3 4.4 %collective-permute-start.34 = (f32[8,160,128]{2,1,0:T(8,128)S(1)}, f32[8,160,128]{2,1,0:T(8,128)S(1)}, u32[]{:S(2)}, u32[]{:S(2)}) collective-permute-start(f32[8,160,128]{2,1,0:T(8,128)S(1)} %slice_select_fusion), channel_id=1, source_target_pairs={{0,1},{1,0},{2,3},{3,2},{4,5},{5,4},{6,7},{7,6},{8,9},{9,8},{10,11... | collective-permute-start | bytes 1966088 | tf_op jit(solution)/shard_map/ppermute | solution.py:622
  (23 other events, 140.4 us)

commit v3 on v2

--- a/solution.py
+++ b/solution.py
@@ -120,33 +120,37 @@
 
 
 def dot_rows_exact(a, b):
-    a, b = three_terms(a), three_terms(b)
+    b = three_terms(b)
     small = dot(beside([a[2], a[0]]), beside([b[0], b[2]]), ((1,), (1,)))
     return dot_rows(a[:2], b[:2]) + small
 
 
-VMEM_LIMIT = 56 << 20
-
-
-def call(kernel, name, grid, in_specs, out_specs, out_shape, scalars=0, scratch=(), aliases={}):
+VMEM_LIMIT = 40 << 20
+WHOLE_LIMIT = 32 << 20
+
+
+def call(kernel, name, grid, in_specs, out_specs, out_shape, scalars=0, limit=VMEM_LIMIT):
     return pl.pallas_call(
         kernel,
         out_shape=[jax.ShapeDtypeStruct(*shape) for shape in out_shape],
         grid_spec=pltpu.PrefetchScalarGridSpec(
-            num_scalar_prefetch=scalars,
-            grid=grid,
-            in_specs=in_specs,
-            out_specs=out_specs,
-            scratch_shapes=scratch,
+            num_scalar_prefetch=scalars, grid=grid, in_specs=in_specs, out_specs=out_specs
         ),
-        input_output_aliases=aliases,
-        compiler_params=pltpu.CompilerParams(vmem_limit_bytes=VMEM_LIMIT),
+        compiler_params=pltpu.CompilerParams(vmem_limit_bytes=limit),
         name=name,
     )
 
 
-def whole(x):
-    return pl.BlockSpec(x.shape, lambda *_: (0,) * x.ndim)
+def call_whole(kernel, name, ins, out_shape, scalars=0):
+    vmem = pl.BlockSpec(memory_space=pltpu.VMEM)
+    return pl.pallas_call(
+        kernel,
+        out_shape=[jax.ShapeDtypeStruct(*shape) for shape in out_shape],
+        in_specs=[pl.BlockSpec(memory_space=pltpu.SMEM)] * scalars + [vmem] * (len(ins) - scalars),
+        out_specs=[vmem] * len(out_shape),
+        compiler_params=pltpu.CompilerParams(vmem_limit_bytes=WHOLE_LIMIT),
+        name=name,
+    )(*ins)
 
 
 ID_ROWS = 8
@@ -218,51 +222,30 @@
 
 
 def split_weights(core, key, value):
-    shape = ((3 * key.shape[0], 2 * key.shape[1]), jnp.bfloat16)
-    (out,) = call(
-        split_kernel,
-        "split_weights",
-        (1,),
-        [whole(key), whole(value)],
-        [pl.BlockSpec(shape[0], lambda *_: (0, 0))],
-        [shape],
-        scalars=1,
-    )(core, key, value)
+    shape = (3 * key.shape[0], 2 * key.shape[1])
+    (out,) = call_whole(
+        split_kernel, "split_weights", [core, key, value], [(shape, jnp.bfloat16)], scalars=1
+    )
     return out
 
 
-def project_kernel(index, *refs):
-    own, other, weights, outs, x = refs[:4], refs[4:8], refs[8], refs[9:11], refs[11]
-
-    @pl.when(pl.program_id(0) == 0)
-    def _():
-        both = jnp.concatenate([beside([ref[0] for ref in own]), beside([ref[0] for ref in other])], 0)
-        upper, lower = two_terms(both)
-        x[...] = jnp.concatenate([upper, lower, upper], 0).T
-
-    terms = dot(x[...], weights[...], ((1,), (0,)))
-    count = outs[0].shape[0]
-    outs[0][...] = terms[:count]
-    outs[1][...] = terms[count:]
+def project_kernel(index, own, other, weights, send, keep):
+    half = own.shape[1] - ID_ROWS
+    both = jnp.concatenate(
+        [beside([ref[index[q], :half] for q in range(4)]) for ref in (own, other)], 0
+    )
+    upper, lower = two_terms(both)
+    terms = dot(jnp.concatenate([upper, lower, upper], 0).T, weights[...], ((1,), (0,)))
+    count = send.shape[0]
+    send[...] = terms[:count]
+    keep[...] = terms[count:]
 
 
 def project(index, own, other, weights):
-    _, rows, plen = own.shape
-    depth, columns = weights.shape
-    picked = [
-        pl.BlockSpec((1, rows - ID_ROWS, plen), lambda i, index, q=q: (index[q], 0, 0))
-        for q in range(4)
-    ]
-    return call(
-        project_kernel,
-        "project",
-        (4,),
-        picked * 2 + [pl.BlockSpec((depth, columns // 4), lambda i, *_: (0, i))],
-        [pl.BlockSpec((2 * plen, columns // 4), lambda i, *_: (0, i))] * 2,
-        [((2 * plen, columns), jnp.float32)] * 2,
-        scalars=1,
-        scratch=[pltpu.VMEM((4 * plen, depth), jnp.bfloat16)],
-    )(index, *([own] * 4), *([other] * 4), weights)
+    shape = ((2 * own.shape[2], weights.shape[1]), jnp.float32)
+    return call_whole(
+        project_kernel, "project", [index, own, other, weights], [shape] * 2, scalars=1
+    )
 
 
 def weight_times(weights, blocks):
@@ -287,15 +270,9 @@
 
 def hidden_part(place, blocks, weights):
     shape = ((len(blocks), weights.shape[0] // 6, blocks[0].shape[0]), jnp.float32)
-    return call(
-        hidden_part_kernel,
-        "hidden_part",
-        (1,),
-        [whole(x) for x in blocks] + [whole(weights)],
-        [pl.BlockSpec(shape[0], lambda *_: (0, 0, 0))] * 2,
-        [shape] * 2,
-        scalars=1,
-    )(place, *blocks, weights)
+    return call_whole(
+        hidden_part_kernel, "hidden_part", [place, *blocks, weights], [shape] * 2, scalars=1
+    )
 
 
 def hidden_last_kernel(place, keep_in, give_in, *refs):
@@ -312,15 +289,13 @@
 
 def hidden_last(place, keep, give, blocks, weights):
     shape = ((4,) + keep.shape[1:], jnp.float32)
-    return call(
+    return call_whole(
         hidden_last_kernel,
         "hidden_last",
-        (1,),
-        [whole(keep), whole(give)] + [whole(x) for x in blocks] + [whole(weights)],
-        [pl.BlockSpec(shape[0], lambda *_: (0, 0, 0))] * 2,
+        [place, keep, give, *blocks, weights],
         [shape] * 2,
         scalars=1,
-    )(place, keep, give, *blocks, weights)
+    )
 
 
 def assemble_kernel(listed, *refs):
@@ -332,15 +307,7 @@
 
 def assemble(listed, keep, come):
     shape = ((16,) + keep[0].shape[1:], jnp.float32)
-    (out,) = call(
-        assemble_kernel,
-        "assemble",
-        (1,),
-        [whole(x) for x in keep + come],
-        [pl.BlockSpec(shape[0], lambda *_: (0, 0, 0))],
-        [shape],
-        scalars=1,
-    )(listed, *keep, *come)
+    (out,) = call_whole(assemble_kernel, "assemble", [listed, *keep, *come], [shape], scalars=1)
     return out
 
 
@@ -366,15 +333,13 @@
 def weight_grad(listed, core, own, other, blocks):
     plen, columns = blocks[0].shape
     shape = ((2 * (own.shape[1] - ID_ROWS), columns // 2), jnp.float32)
-    return call(
+    return call_whole(
         weight_grad_kernel,
         "weight_grad",
-        (1,),
-        [whole(own)] * 2 + [whole(blocks[0])] * len(blocks),
-        [pl.BlockSpec(shape[0], lambda *_: (0, 0))] * 2,
+        [listed, core, own, other, *blocks],
         [shape] * 2,
         scalars=2,
-    )(listed, core, own, other, *blocks)
+    )
 
 
 SCALE = 1.0 / math.sqrt(HEAD_SIZE)
@@ -416,17 +381,24 @@
     return jnp.where((j <= row_number(scores.shape, rows)) & (j < length), scores, masked_value)
 
 
-def open_kernel(length, q, k, v, total, stats):
-    scores = own_scores(length[0], stack(q), k[...], q.shape[0])
+def open_kernel(length, q, g, k, v, total, stats, q1, q2, q3, g1, g2):
+    query_terms = three_terms(stack(q))
+    for ref, term in zip((q1, q2, q3), query_terms):
+        unstack(ref, term)
+    upstream = stack(g)
+    upstream = jnp.where(row_number(upstream.shape, q.shape[0]) < length[0], upstream, 0.0)
+    for ref, term in zip((g1, g2), two_terms(upstream)):
+        unstack(ref, term)
+    scores = own_scores(length[0], query_terms, k[...], q.shape[0])
     top = jnp.max(scores, -1, keepdims=True)
     expo = jnp.exp(scores - top)
     unstack(total, dot_columns(two_terms(expo), two_terms(v[...])))
     save_columns(stats, top, jnp.sum(expo, -1, keepdims=True))
 
 
-def close_kernel(length, q, g, kp, vp, total, stats, out, grad_scores, stats_out, gk, gv):
-    query, keys, values = stack(q), kp[...], vp[...]
-    scores = dot_rows_exact(query, keys) * SCALE
+def close_kernel(length, q1, q2, q3, g, g1, g2, kp, vp, total, stats, out, grad_scores, stats_out, gk, gv):
+    query_terms = stack(q1), stack(q2), stack(q3)
+    scores = dot_rows_exact(query_terms, kp[...]) * SCALE
     before = load_column(stats, 0)
     top = jnp.maximum(before, jnp.max(scores, -1, keepdims=True))
     weight = jnp.exp(before - top)
@@ -434,54 +406,44 @@
     denominator = weight * load_column(stats, 8) + jnp.sum(expo, -1, keepdims=True)
     inverse = 1.0 / denominator
     prob = expo * inverse
-    prob_terms, value_terms = two_terms(prob), two_terms(values)
+    prob_terms, value_terms = two_terms(prob), two_terms(vp[...])
     result = (weight * inverse) * stack(total) + dot_columns(prob_terms, value_terms)
-    valid = row_number(result.shape, q.shape[0]) < length[0]
-    result = jnp.where(valid, result, 0.0)
-    upstream = jnp.where(valid, stack(g), 0.0)
-    upstream_terms = two_terms(upstream)
-    inner = jnp.sum(upstream * result, -1, keepdims=True)
+    result = jnp.where(row_number(result.shape, g.shape[0]) < length[0], result, 0.0)
+    upstream_terms = stack(g1), stack(g2)
+    inner = jnp.sum(stack(g) * result, -1, keepdims=True)
     grad = prob * (dot_rows(upstream_terms, value_terms) - inner) * SCALE
     unstack(out, result)
     unstack(grad_scores, grad)
     save_columns(stats_out, top + jnp.log(denominator), inner)
-    gk[...] = dot_turned(two_terms(grad), two_terms(query))
+    gk[...] = dot_turned(two_terms(grad), query_terms[:2])
     gv[...] = dot_turned(prob_terms, upstream_terms)
 
 
-def finish_kernel(length, q, g, k, v, kp, grad_scores, stats, gq, gk, gv):
-    query, keys = stack(q), k[...]
-    rows = q.shape[0]
-    prob = jnp.exp(own_scores(length[0], query, keys, rows) - load_column(stats, 0))
-    upstream = stack(g)
-    upstream = jnp.where(row_number(upstream.shape, rows) < length[0], upstream, 0.0)
-    upstream_terms = two_terms(upstream)
+def finish_kernel(length, q1, q2, q3, g1, g2, k, v, kp, grad_scores, stats, gq, gk, gv):
+    query_terms, keys = (stack(q1), stack(q2), stack(q3)), k[...]
+    prob = jnp.exp(own_scores(length[0], query_terms, keys, q1.shape[0]) - load_column(stats, 0))
+    upstream_terms = stack(g1), stack(g2)
     grad = prob * (dot_rows(upstream_terms, two_terms(v[...])) - load_column(stats, 8)) * SCALE
     grad_terms = two_terms(grad)
     prompt_part = dot_columns(two_terms(stack(grad_scores)), two_terms(kp[...]))
     unstack(gq, prompt_part + dot_columns(grad_terms, two_terms(keys)))
-    gk[...] = dot_turned(grad_terms, two_terms(query))
+    gk[...] = dot_turned(grad_terms, query_terms[:2])
     gv[...] = dot_turned(two_terms(prob), upstream_terms)
 
 
-def attention(kernel, name, groups, length, ins, outs, start=0, count=None, into=()):
-    def body(length, *refs):
-        kernel(length, *refs[: len(ins)], *refs[len(ins) + len(into) :])
-
+def attention(kernel, name, groups, length, ins, outs):
     return call(
-        body,
+        kernel,
         name,
-        (groups if count is None else count,),
+        (groups,),
         [
-            pl.BlockSpec((x.shape[0], size), lambda i, *_, skip=skip: (0, skip + start + i))
+            pl.BlockSpec((x.shape[0], size), lambda i, *_, skip=skip: (0, skip + i))
             for x, size, skip in ins
-        ]
-        + [pl.BlockSpec(memory_space=pl.ANY)] * len(into),
-        [pl.BlockSpec(shape, lambda i, *_: (0, start + i)) for shape in outs],
-        [((rows, groups * size), jnp.float32) for rows, size in outs],
+        ],
+        [pl.BlockSpec((rows, size), lambda i, *_: (0, i)) for rows, size, _ in outs],
+        [((rows, groups * size), kind) for rows, size, kind in outs],
         scalars=1,
-        aliases={1 + len(ins) + i: i for i in range(len(into))},
-    )(length, *(x for x, _, _ in ins), *into)
+    )(length, *(x for x, _, _ in ins))
 
 
 def take_blocks(x, index):
@@ -532,19 +494,24 @@
         hidden = hidden.reshape(PROMPT_COUNT, plen, slice_width)
         weights = jnp.concatenate([key_weight, value_weight], 1)
 
-    q = (queries, wide, 0)
-    total, stats = attention(
+    whole_heads, one_head = (tokens, wide, jnp.float32), (tokens, HEAD_SIZE, jnp.float32)
+    total, stats, *kept = attention(
         open_kernel,
         "open",
         groups,
         resp_len,
-        [q, (keys_resp, HEAD_SIZE, 0), (response_value_rows, HEAD_SIZE, 0)],
-        [(tokens, wide), (tokens, HEAD_SIZE)],
+        [
+            (queries, wide, 0),
+            (grad_out, wide, 0),
+            (keys_resp, HEAD_SIZE, 0),
+            (response_value_rows, HEAD_SIZE, 0),
+        ],
+        [whole_heads, one_head] + [(tokens, wide, jnp.bfloat16)] * 5,
     )
 
     if short:
-        mine, weight_terms, total, stats = lax.optimization_barrier(
-            (mine, weight_terms, total, stats)
+        mine, weight_terms, total, stats, kept = lax.optimization_barrier(
+            (mine, weight_terms, total, stats, kept)
         )
         all_prompts = mine[:, slice_width // 2, 0].astype(jnp.int32)
         other = lax.ppermute(mine, "mp", SWAP)
@@ -557,22 +524,33 @@
             terms.reshape(responses * plen, 2 * width), "dp", scatter_dimension=0, tiled=True
         )
 
-    g = (grad_out, wide, 0)
+    query_terms = [(x, wide, 0) for x in kept[:3]]
+    upstream_terms = [(x, wide, 0) for x in kept[3:]]
     prompt_keys = (prompt_rows, HEAD_SIZE, 0)
     result, grad_scores, stats, own_k, own_v = attention(
         close_kernel,
         "close",
         groups,
         resp_len,
-        [q, g, prompt_keys, (prompt_rows, HEAD_SIZE, groups), (total, wide, 0), (stats, HEAD_SIZE, 0)],
-        [(tokens, wide), (tokens, PER_GROUP * plen), (tokens, HEAD_SIZE)] + [(plen, HEAD_SIZE)] * 2,
-    )
-    finish_ins = [q, g, (keys_resp, HEAD_SIZE, 0), (response_value_rows, HEAD_SIZE, 0), prompt_keys]
-    finish_ins += [(grad_scores, PER_GROUP * plen, 0), (stats, HEAD_SIZE, 0)]
-    finish_outs = [(tokens, wide)] + [(tokens, HEAD_SIZE)] * 2
-    finish = functools.partial(
-        attention, finish_kernel, "finish", groups, resp_len, finish_ins, finish_outs
-    )
+        query_terms
+        + [(grad_out, wide, 0)]
+        + upstream_terms
+        + [prompt_keys, (prompt_rows, HEAD_SIZE, groups), (total, wide, 0), (stats, HEAD_SIZE, 0)],
+        [whole_heads, (tokens, PER_GROUP * plen, jnp.float32), one_head]
+        + [(plen, HEAD_SIZE, jnp.float32)] * 2,
+    )
+
+    def finish(stats):
+        own_ins = [(keys_resp, HEAD_SIZE, 0), (response_value_rows, HEAD_SIZE, 0), prompt_keys]
+        kept_ins = [(grad_scores, PER_GROUP * plen, 0), (stats, HEAD_SIZE, 0)]
+        return attention(
+            finish_kernel,
+            "finish",
+            groups,
+            resp_len,
+            query_terms + upstream_terms + own_ins + kept_ins,
+            [whole_heads] + [one_head] * 2,
+        )
 
     own = jnp.concatenate([own_k, own_v], 1)
     if short:
@@ -580,17 +558,13 @@
         listed = take_small(all_prompts, chip ^ jnp.arange(chips))
         far = [own] + [permute(own, ACROSS[k]) for k in range(1, 4)]
         near, third, both = [permute(own, SECOND)], [permute(own, THIRD)], []
-        keep, give, state = [], [], ()
 
         def group(k):
             return [far[k], near[k], third[k], both[k]]
 
         for k in range(1, 4):
             done = hidden_part(place, group(0), weight_terms) if k == 3 else None
-            state = finish(start=k - 1, count=1, into=state) if k < 3 else state
-            far[k], near[k - 1], state, done = lax.optimization_barrier(
-                (far[k], near[k - 1], state, done)
-            )
+            far[k], near[k - 1], done = lax.optimization_barrier((far[k], near[k - 1], done))
             both.append(permute(near[k - 1], THIRD))
             near.append(permute(far[k], SECOND))
             third.append(permute(far[k], THIRD))
@@ -603,8 +577,8 @@
         parts.append(hidden_part(place, group(2), weight_terms))
         come = [lax.ppermute(give, "mp", SWAP) for _, give in parts]
         pair = hidden_part(jnp.arange(2), [far[3], near[3]], weight_terms)
-        third[3], both[3], parts, come, pair = lax.optimization_barrier(
-            (third[3], both[3], parts, come, pair)
+        third[3], both[3], parts, come, pair, stats_late = lax.optimization_barrier(
+            (third[3], both[3], parts, come, pair, stats)
         )
         parts.append(hidden_last(place, *pair, [third[3], both[3]], weight_terms))
         come.append(lax.ppermute(parts[3][1], "mp", SWAP))
@@ -613,15 +587,14 @@
         order = take_small(all_prompts, gathered_order(chip, core))
         gathered = [x for k in range(4) for x in group(k)]
         grad_w_key, grad_w_value = weight_grad(order, here, mine, other, gathered)
-        state = finish(start=2, count=groups - 2, into=state)
         back, grad_w_key, grad_w_value, state = lax.optimization_barrier(
-            (back, grad_w_key, grad_w_value, state)
+            (back, grad_w_key, grad_w_value, finish(stats_late))
         )
         grad_query, grad_keys, grad_values = state
         leave = jnp.where(core == 0, back[chips // 2 :], back[: chips // 2])
         grad_hidden = turn_back(here, back, lax.ppermute(leave, "mp", SWAP))
     else:
-        grad_query, grad_keys, grad_values = finish()
+        grad_query, grad_keys, grad_values = finish(stats)
         gathered = lax.all_gather(own, "dp", axis=0, tiled=True).reshape(responses, plen, 2 * width)
         summed = jnp.einsum(
             "rtc,rtk->ck", take_blocks(hidden, all_prompts), gathered, precision=HIGH

time: 302 us -> 288 us (0.954)
  Pallas kernels: 114 us -> 69.7 us
  local copies, waits for them, and re-layouts: 9.35 us -> 30.4 us
  waiting for transfers between devices: 109 us -> 120 us
    pallas_call x17 -> x15, Pallas kernels: 106 us -> 65.4 us  [the longest x3 39.3 us: attention(): call(kernel, name, (groups,), [pl.BlockSpec((x.shape[0], size), lambda i,...]
    ppermute x29, waiting for transfers between devices: 73.6 us -> 107 us  [permute(): return lax.ppermute(x, BOTH, pairs)]
    unnamed x69 -> x141, local copies, waits for them, and re-layouts: 7.1 us -> 30.1 us
    all_to_all x1, waiting for transfers between devices: 12.2 us -> 0.01 us  [per_device(): lax.all_to_all(assemble(listed, [x for x, _ in parts], come), 'dp', 0, 0)]
    all_to_all x1, waiting for transfers between devices: 19.2 us -> 9.08 us  [per_device(): lax.all_to_all(turn(here, resp_prompt, prompt_hidden, chips), 'dp', 0, 0)]
  transfers between devices with their start and end apart: 37 -> 37, of which waited for: 17 -> 22; matrix products, arithmetic and copies ran while one was open for 1% -> 1% of each run, Pallas kernels for 25% -> 15%
where the time goes in v3:
time: 288 us; the launch traced here: 287 us
  waiting for transfers between devices  120 us (42%)
  Pallas kernels  69.7 us (24%)
  starting transfers between devices  61.7 us (21%)
  local copies, waits for them, and re-layouts  30.4 us (11%)
    ppermute x29, waiting for transfers between devices, permute(): return lax.ppermute(x, BOTH, pairs)  107 us
    pallas_call x3, Pallas kernels, attention(): call(kernel, name, (groups,), [pl.BlockSpec((x.shape[0], size), lambda i,...  39.3 us
    ppermute x29, starting transfers between devices, permute(): return lax.ppermute(x, BOTH, pairs)  36.5 us
    unnamed x141, local copies, waits for them, and re-layouts  30.1 us
    pallas_call x12, Pallas kernels, call_whole(): pl.pallas_call(kernel, out_shape=[jax.ShapeDtypeStruct(*shape) for shape...  26.1 us
    all_to_all x1, waiting for transfers between devices, per_device(): lax.all_to_all(turn(here, resp_prompt, prompt_hidden, chips), 'dp', 0, 0)  9.08 us
    all_to_all x1, starting transfers between devices, per_device(): lax.all_to_all(assemble(listed, [x for x, _ in parts], come), 'dp', 0, 0)  7.17 us
    all_to_all x1, starting transfers between devices, per_device(): lax.all_to_all(turn(here, resp_prompt, prompt_hidden, chips), 'dp', 0, 0)  6.66 us
  transfers between devices with their start and end apart: 37, of which 22 were waited for; matrix products, arithmetic and copies ran while one was open for 1% of the time, Pallas kernels for 15%

profile of v3, /device:TPU:9, one launch (start us, length us, event | category | flops | bytes accessed | tf_op | source)
XLA Modules:
  0.0 287.1 jit_solution(9978211300984168986)
XLA Ops:
  1.3 1.7 copy-done.22
  3.0 2.3 turn.1
  5.4 6.7 %all-to-all-start = ((f32[16,168,128]{2,1,0:T(8,128)}), f32[16,168,128]{2,1,0:T(8,128)S(1)}, u32[]{:S(2)}, u32[]{:S(2)}) async-start(f32[16,168,128]{2,1,0:T(8,128)} %turn.1), calls=%async_computation | async-start | bytes 2752512 | tf_op jit(solution)/shard_map/all_to_all | solution.py:487
  17.7 8.9 %open.1 = (f32[256,2560]{1,0:T(8,128)S(1)}, f32[256,512]{1,0:T(8,128)S(1)}, bf16[256,2560]{1,0:T(8,128)(2,1)S(1)}, bf16[256,2560]{1,0:T(8,128)(2,1)S(1)}, bf16[2...) custom-call(s32[1]{0:T(128)S(6)} %copy.25.length, ...), custom_call_target="tpu_custom_call" | custom-call | tf_op jit(solution)/shard_map/open/pallas_call | solution.py:435
  34.4 9.1 %all-to-all-done.own = f32[16,168,128]{2,1,0:T(8,128)S(1)} async-done(((f32[16,168,128]{2,1,0:T(8,128)}), f32[16,168,128]{2,1,0:T(8,128)S(1)}, u32[]{:S(2)}, u32[]{:S(2)}) %all-to-all-start) | async-done | bytes 1376288 | tf_op jit(solution)/shard_map/all_to_all | solution.py:487
  43.5 2.7 collective-permute-start
  47.2 1.8 collective-permute-done.other
  49.0 2.6 project.7
  52.9 2.6 project.6
  55.9 2.6 project.5
  59.8 5.8 %collective-permute-done.10 = f32[256,1024]{1,0:T(8,128)S(1)} collective-permute-done((f32[256,1024]{1,0:T(8,128)S(1)}, f32[256,1024]{1,0:T(8,128)S(1)}, u32[]{:S(2)}, u32[]{:S(2)}) %collective-permute-start.10) | collective-permute-done | bytes 1048608 | tf_op jit(solution)/shard_map/ppermute | solution.py:45
  66.3 2.6 project.4
  70.2 12.3 %collective-permute-done.6 = f32[256,1024]{1,0:T(8,128)S(1)} collective-permute-done((f32[256,1024]{1,0:T(8,128)S(1)}, f32[256,1024]{1,0:T(8,128)S(1)}, u32[]{:S(2)}, u32[]{:S(2)}) %collective-permute-start.6) | collective-permute-done | bytes 1048608 | tf_op jit(solution)/shard_map/ppermute | solution.py:45
  84.5 14.8 %collective-permute-done.3 = f32[256,1024]{1,0:T(8,128)S(1)} collective-permute-done((f32[256,1024]{1,0:T(8,128)S(1)}, f32[256,1024]{1,0:T(8,128)S(1)}, u32[]{:S(2)}, u32[]{:S(2)}) %collective-permute-start.3) | collective-permute-done | bytes 1048608 | tf_op jit(solution)/shard_map/ppermute | solution.py:45
  101.5 2.5 collective-permute-start.13
  104.0 11.8 %collective-permute-done.1 = f32[256,1024]{1,0:T(8,128)S(1)} collective-permute-done((f32[256,1024]{1,0:T(8,128)S(1)}, f32[256,1024]{1,0:T(8,128)S(1)}, u32[]{:S(2)}, u32[]{:S(2)}) %collective-permute-start.1) | collective-permute-done | bytes 1048608 | tf_op jit(solution)/shard_map/ppermute | solution.py:45
  116.5 2.6 collective-permute-start.9
  121.0 1.7 collective-permute-start.5
  124.3 5.0 %collective-permute-done.9 = f32[128,1024]{1,0:T(8,128)S(1)} collective-permute-done((f32[128,1024]{1,0:T(8,128)S(1)}, f32[128,1024]{1,0:T(8,128)S(1)}, u32[]{:S(2)}, u32[]{:S(2)}) %collective-permute-start.9) | collective-permute-done | bytes 524320 | tf_op jit(solution)/shard_map/ppermute | solution.py:45
  130.3 4.1 %collective-permute-done.5 = f32[128,1024]{1,0:T(8,128)S(1)} collective-permute-done((f32[128,1024]{1,0:T(8,128)S(1)}, f32[128,1024]{1,0:T(8,128)S(1)}, u32[]{:S(2)}, u32[]{:S(2)}) %collective-permute-start.5) | collective-permute-done | bytes 524320 | tf_op jit(solution)/shard_map/ppermute | solution.py:45
  134.9 17.9 %close.1 = (f32[256,2560]{1,0:T(8,128)}, f32[256,2560]{1,0:T(8,128)S(1)}, f32[256,512]{1,0:T(8,128)S(1)}, f32[128,512]{1,0:T(8,128)S(1)}, f32[128,512]{1,0:T(8,128)S(1)}) custom-call(s32[1]{0:T(128)S(6)} %copy.25.length, bf16[256,2560]{1,0:T(8,128)(2,1)S(1)} %copy-done.5, bf16[256,2560]{1,0:T(8,128)(2,1)S(1)} %copy-done.8, bf16[256,2560]{1,0:T(8,128)(2,1)S(1)} %copy-done.11, ...), custom_call_target="tpu_custom_call" | custom-call | tf_op jit(solution)/shard_map/close/pallas_call | solution.py:435
  154.1 2.3 collective-permute-start.16
  156.4 15.5 %collective-permute-done.17.refs_0_.refs_4_ = f32[128,1024]{1,0:T(8,128)S(1)} collective-permute-done((f32[128,1024]{1,0:T(8,128)S(1)}, f32[128,1024]{1,0:T(8,128)S(1)}, u32[]{:S(2)}, u32[]{:S(2)}) %collective-permute-start.17) | collective-permute-done | bytes 524320 | tf_op jit(solution)/shard_map/ppermute | solution.py:45
  172.3 2.3 collective-permute-start.15
  176.1 4.2 %collective-permute-done.19.refs_1_.refs_5_ = f32[128,1024]{1,0:T(8,128)S(1)} collective-permute-done((f32[128,1024]{1,0:T(8,128)S(1)}, f32[128,1024]{1,0:T(8,128)S(1)}, u32[]{:S(2)}, u32[]{:S(2)}) %collective-permute-start.19) | collective-permute-done | bytes 524320 | tf_op jit(solution)/shard_map/ppermute | solution.py:45
  180.6 3.9 %collective-permute-start.25 = (f32[128,1024]{1,0:T(8,128)S(1)}, f32[128,1024]{1,0:T(8,128)S(1)}, u32[]{:S(2)}, u32[]{:S(2)}) collective-permute-start(f32[128,1024]{1,0:T(8,128)S(1)} %collective-permute-done.17.refs_0_.refs_4_), channel_id=1, source_target_pairs={{0,2},{1,5},{2,0},{3,7},{4,6},{5,1},{6,4},{7,3},{8,10},{9,13},{10,... | collective-permute-start | bytes 1572872 | tf_op jit(solution)/shard_map/ppermute | solution.py:45
  184.5 2.9 %collective-permute-done.21.refs_2_ = f32[128,1024]{1,0:T(8,128)S(1)} collective-permute-done((f32[128,1024]{1,0:T(8,128)S(1)}, f32[128,1024]{1,0:T(8,128)S(1)}, u32[]{:S(2)}, u32[]{:S(2)}) %collective-permute-start.21) | collective-permute-done | bytes 524320 | tf_op jit(solution)/shard_map/ppermute | solution.py:45
  188.3 5.8 %collective-permute-done.22.refs_3_ = f32[128,1024]{1,0:T(8,128)S(1)} collective-permute-done((f32[128,1024]{1,0:T(8,128)S(1)}, f32[128,1024]{1,0:T(8,128)S(1)}, u32[]{:S(2)}, u32[]{:S(2)}) %collective-permute-start.22) | collective-permute-done | bytes 524320 | tf_op jit(solution)/shard_map/ppermute | solution.py:45
  194.1 1.8 hidden_part.4
  197.6 3.6 %collective-permute-done.15.refs_0_.refs_12_ = f32[128,1024]{1,0:T(8,128)S(1)} collective-permute-done((f32[128,1024]{1,0:T(8,128)S(1)}, f32[128,1024]{1,0:T(8,128)S(1)}, u32[]{:S(2)}, u32[]{:S(2)}) %collective-permute-start.15) | collective-permute-done | bytes 524320 | tf_op jit(solution)/shard_map/ppermute | solution.py:45
  201.2 1.6 collective-permute-start.24
  202.8 2.0 collective-permute-start.28
  206.3 4.7 %collective-permute-done.26.refs_3_.refs_7_ = f32[128,1024]{1,0:T(8,128)S(1)} collective-permute-done((f32[128,1024]{1,0:T(8,128)S(1)}, f32[128,1024]{1,0:T(8,128)S(1)}, u32[]{:S(2)}, u32[]{:S(2)}) %collective-permute-start.26) | collective-permute-done | bytes 524320 | tf_op jit(solution)/shard_map/ppermute | solution.py:45
  211.0 1.8 hidden_part.5
  213.7 1.7 collective-permute-done.24.refs_1_.refs_13_
  215.4 2.1 collective-permute-start.27
  217.4 6.4 %collective-permute-start.30 = (f32[4,160,128]{2,1,0:T(8,128)S(1)}, f32[4,160,128]{2,1,0:T(8,128)S(1)}, u32[]{:S(2)}, u32[]{:S(2)}) collective-permute-start(f32[4,160,128]{2,1,0:T(8,128)S(1)} %get-tuple-element.117), channel_id=1, source_target_pairs={{0,1},{1,0},{2,3},{3,2},{4,5},{5,4},{6,7},{7,6},{8,9},{9,8},{10,11... | collective-permute-start | bytes 983048 | tf_op jit(solution)/shard_map/ppermute | solution.py:578
  224.0 3.9 %collective-permute-done.29.refs_3_.refs_11_ = f32[128,1024]{1,0:T(8,128)S(1)} collective-permute-done((f32[128,1024]{1,0:T(8,128)S(1)}, f32[128,1024]{1,0:T(8,128)S(1)}, u32[]{:S(2)}, u32[]{:S(2)}) %collective-permute-start.29) | collective-permute-done | bytes 524320 | tf_op jit(solution)/shard_map/ppermute | solution.py:45
  227.9 1.8 hidden_part.6
  231.1 2.4 collective-permute-done.23.refs_0_.refs_14_
  233.5 5.3 %collective-permute-done.27.refs_1_.refs_15_ = f32[128,1024]{1,0:T(8,128)S(1)} collective-permute-done((f32[128,1024]{1,0:T(8,128)S(1)}, f32[128,1024]{1,0:T(8,128)S(1)}, u32[]{:S(2)}, u32[]{:S(2)}) %collective-permute-start.27) | collective-permute-done | bytes 524320 | tf_op jit(solution)/shard_map/ppermute | solution.py:45
  243.6 7.2 %all-to-all-start.1 = ((f32[16,160,128]{2,1,0:T(8,128)}), f32[16,160,128]{2,1,0:T(8,128)S(1)}, u32[]{:S(2)}, u32[]{:S(2)}) async-start(f32[16,160,128]{2,1,0:T(8,128)} %copy-done.3), calls=%async_computation.1 | async-start | bytes 2621440 | tf_op jit(solution)/shard_map/all_to_all | solution.py:585
  257.4 1.7 copy-done.25
  262.4 12.5 %finish.1 = (f32[256,2560]{1,0:T(8,128)}, f32[256,512]{1,0:T(8,128)}, f32[256,512]{1,0:T(8,128)}) custom-call(s32[1]{0:T(128)S(6)} %copy.25.length, bf16[256,2560]{1,0:T(8,128)(2,1)S(1)} %copy-done.6, bf16[256,2560]{1,0:T(8,128)(2,1)S(1)} %copy-done.9, bf16[256,2560]{1,0:T(8,128)(2,1)S(1)} %copy-done.12, bf16[256,2560]{1,0:T(8,128)(2,1)S(1)} %copy-done.15, ...), custom_call_target="tpu_custom_call" | custom-call | tf_op jit(solution)/shard_map/finish/pallas_call | solution.py:435
  275.1 6.6 %weight_grad.1 = (f32[320,512]{1,0:T(8,128)}, f32[320,512]{1,0:T(8,128)}) custom-call(s32[16]{0:T(128)S(1)} %get-tuple-element.151.listed, s32[1]{0:T(128)} %bitcast.core, f32[16,168,128]{2,1,0:T(8,128)S(1)} %all-to-all-done.own, f32[16,168,128]{2,1,0:T(8,128)} %collective-permute-done.other, f32[128,1024]{1,0:T(8,128)S(1)} %copy-done.20, ...), custom_call_target="tpu_custom_call" | custom-call | tf_op jit(solution)/shard_map/weight_grad/pallas_call | solution.py:146
  281.7 1.7 collective-permute-start.34
  283.4 1.7 collective-permute-done.34.other
  285.1 2.0 turn_back.1
  (211 shorter events, 52.6 us)
Async XLA Ops:
  5.4 38.1 %all-to-all-start = ((f32[16,168,128]{2,1,0:T(8,128)}), f32[16,168,128]{2,1,0:T(8,128)S(1)}, u32[]{:S(2)}, u32[]{:S(2)}) async-start(f32[16,168,128]{2,1,0:T(8,128)} %turn.1), calls=%async_computation | async-start | bytes 2752512 | tf_op jit(solution)/shard_map/all_to_all | solution.py:487
  17.7 28.6 %copy-start.66 = (s32[4,4]{1,0:T(4,128)S(1)}, s32[4,4]{1,0:T(4,128)}, u32[]{:S(2)}) copy-start(s32[4,4]{1,0:T(4,128)} %constant.38.clone) | copy-start | bytes 196
  43.5 5.6 %collective-permute-start = (f32[16,168,128]{2,1,0:T(8,128)S(1)}, f32[16,168,128]{2,1,0:T(8,128)}, u32[]{:S(2)}, u32[]{:S(2)}) collective-permute-start(f32[16,168,128]{2,1,0:T(8,128)S(1)} %all-to-all-done.own), channel_id=1, source_target_pairs={{0,1},{1,0},{2,3},{3,2},{4,5},{5,4},{6,7},{7,6},{8,9},{9,8},{10,11... | collective-permute-start | bytes 4128776 | tf_op jit(solution)/shard_map/ppermute | solution.py:517
  51.7 14.0 %collective-permute-start.10 = (f32[256,1024]{1,0:T(8,128)S(1)}, f32[256,1024]{1,0:T(8,128)S(1)}, u32[]{:S(2)}, u32[]{:S(2)}) collective-permute-start(f32[256,1024]{1,0:T(8,128)S(1)} %get-tuple-element.100), channel_id=1, source_target_pairs={{0,2},{1,5},{2,0},{3,7},{4,6},{5,1},{6,4},{7,3},{8,10},{9,13},{10,... | collective-permute-start | bytes 3145736 | tf_op jit(solution)/shard_map/ppermute | solution.py:45
  55.6 26.9 %collective-permute-start.6 = (f32[256,1024]{1,0:T(8,128)S(1)}, f32[256,1024]{1,0:T(8,128)S(1)}, u32[]{:S(2)}, u32[]{:S(2)}) collective-permute-start(f32[256,1024]{1,0:T(8,128)S(1)} %get-tuple-element.98), channel_id=1, source_target_pairs={{0,2},{1,5},{2,0},{3,7},{4,6},{5,1},{6,4},{7,3},{8,10},{9,13},{10,... | collective-permute-start | bytes 3145736 | tf_op jit(solution)/shard_map/ppermute | solution.py:45
  58.5 40.8 %collective-permute-start.3 = (f32[256,1024]{1,0:T(8,128)S(1)}, f32[256,1024]{1,0:T(8,128)S(1)}, u32[]{:S(2)}, u32[]{:S(2)}) collective-permute-start(f32[256,1024]{1,0:T(8,128)S(1)} %get-tuple-element.96), channel_id=1, source_target_pairs={{0,2},{1,5},{2,0},{3,7},{4,6},{5,1},{6,4},{7,3},{8,10},{9,13},{10,... | collective-permute-start | bytes 3145736 | tf_op jit(solution)/shard_map/ppermute | solution.py:45
  65.7 17.4 %collective-permute-start.11 = (f32[128,1024]{1,0:T(8,128)S(1)}, f32[128,1024]{1,0:T(8,128)S(1)}, u32[]{:S(2)}, u32[]{:S(2)}) collective-permute-start(f32[128,1024]{1,0:T(8,128)S(1)} %slice_add_fusion), channel_id=1, source_target_pairs={{0,4},{1,3},{2,6},{3,1},{4,0},{5,7},{6,2},{7,5},{8,12},{9,11},{10,... | collective-permute-start | bytes 1572872 | tf_op jit(solution)/shard_map/ppermute | solution.py:45
  68.9 46.9 %collective-permute-start.1 = (f32[256,1024]{1,0:T(8,128)S(1)}, f32[256,1024]{1,0:T(8,128)S(1)}, u32[]{:S(2)}, u32[]{:S(2)}) collective-permute-start(f32[256,1024]{1,0:T(8,128)S(1)} %get-tuple-element.94), channel_id=1, source_target_pairs={{0,2},{1,5},{2,0},{3,7},{4,6},{5,1},{6,4},{7,3},{8,10},{9,13},{10,... | collective-permute-start | bytes 3145736 | tf_op jit(solution)/shard_map/ppermute | solution.py:45
  82.6 16.9 %collective-permute-start.7 = (f32[128,1024]{1,0:T(8,128)S(1)}, f32[128,1024]{1,0:T(8,128)S(1)}, u32[]{:S(2)}, u32[]{:S(2)}) collective-permute-start(f32[128,1024]{1,0:T(8,128)S(1)} %slice_add_fusion.2), channel_id=1, source_target_pairs={{0,4},{1,3},{2,6},{3,1},{4,0},{5,7},{6,2},{7,5},{8,12},{9,11},{10,... | collective-permute-start | bytes 1572872 | tf_op jit(solution)/shard_map/ppermute | solution.py:45
  83.2 18.2 %collective-permute-start.12 = (f32[128,1024]{1,0:T(8,128)S(1)}, f32[128,1024]{1,0:T(8,128)S(1)}, u32[]{:S(2)}, u32[]{:S(2)}) collective-permute-start(f32[128,1024]{1,0:T(8,128)S(1)} %fusion), channel_id=1, source_target_pairs={{0,8},{1,9},{2,10},{3,11},{4,12},{5,13},{6,14},{7,15},{24,16},{25,... | collective-permute-start | bytes 1572872 | tf_op jit(solution)/shard_map/ppermute | solution.py:45
  99.6 16.8 %collective-permute-start.8 = (f32[128,1024]{1,0:T(8,128)S(1)}, f32[128,1024]{1,0:T(8,128)S(1)}, u32[]{:S(2)}, u32[]{:S(2)}) collective-permute-start(f32[128,1024]{1,0:T(8,128)S(1)} %fusion.1), channel_id=1, source_target_pairs={{0,8},{1,9},{2,10},{3,11},{4,12},{5,13},{6,14},{7,15},{24,16},{25,... | collective-permute-start | bytes 1572872 | tf_op jit(solution)/shard_map/ppermute | solution.py:45
  100.9 18.3 %collective-permute-start.4 = (f32[128,1024]{1,0:T(8,128)S(1)}, f32[128,1024]{1,0:T(8,128)S(1)}, u32[]{:S(2)}, u32[]{:S(2)}) collective-permute-start(f32[128,1024]{1,0:T(8,128)S(1)} %slice_add_fusion.4), channel_id=1, source_target_pairs={{0,4},{1,3},{2,6},{3,1},{4,0},{5,7},{6,2},{7,5},{8,12},{9,11},{10,... | collective-permute-start | bytes 1572872 | tf_op jit(solution)/shard_map/ppermute | solution.py:45
  101.5 17.7 %collective-permute-start.13 = (f32[128,1024]{1,0:T(8,128)S(1)}, f32[128,1024]{1,0:T(8,128)S(1)}, u32[]{:S(2)}, u32[]{:S(2)}) collective-permute-start(f32[128,1024]{1,0:T(8,128)S(1)} %add.94), channel_id=1, source_target_pairs={{8,16},{9,17},{10,18},{11,19},{12,20},{13,21},{14,22},{15,23},{16,... | collective-permute-start | bytes 1572872 | tf_op jit(solution)/shard_map/ppermute | solution.py:45
  115.8 19.0 %copy-start.17 = (bf16[256,2560]{1,0:T(8,128)(2,1)S(1)}, bf16[256,2560]{1,0:T(8,128)(2,1)}, u32[]{:S(2)}) copy-start(bf16[256,2560]{1,0:T(8,128)(2,1)} %copy-done.16) | copy-start | bytes 3932164
  115.9 8.4 %collective-permute-start.2 = (f32[128,1024]{1,0:T(8,128)S(1)}, f32[128,1024]{1,0:T(8,128)S(1)}, u32[]{:S(2)}, u32[]{:S(2)}) collective-permute-start(f32[128,1024]{1,0:T(8,128)S(1)} %slice_add_fusion.6), channel_id=1, source_target_pairs={{0,4},{1,3},{2,6},{3,1},{4,0},{5,7},{6,2},{7,5},{8,12},{9,11},{10,... | collective-permute-start | bytes 1572872 | tf_op jit(solution)/shard_map/ppermute | solution.py:45
  116.4 18.4 %copy-start.14 = (bf16[256,2560]{1,0:T(8,128)(2,1)S(1)}, bf16[256,2560]{1,0:T(8,128)(2,1)}, u32[]{:S(2)}) copy-start(bf16[256,2560]{1,0:T(8,128)(2,1)} %copy-done.13) | copy-start | bytes 3932164
  116.4 18.4 %copy-start.65 = (f32[256,512]{1,0:T(8,128)S(1)}, f32[256,512]{1,0:T(8,128)}, u32[]{:S(2)}) copy-start(f32[256,512]{1,0:T(8,128)} %copy-done.64) | copy-start | bytes 1572868
  116.5 12.7 %collective-permute-start.9 = (f32[128,1024]{1,0:T(8,128)S(1)}, f32[128,1024]{1,0:T(8,128)S(1)}, u32[]{:S(2)}, u32[]{:S(2)}) collective-permute-start(f32[128,1024]{1,0:T(8,128)S(1)} %add.89), channel_id=1, source_target_pairs={{8,16},{9,17},{10,18},{11,19},{12,20},{13,21},{14,22},{15,23},{16,... | collective-permute-start | bytes 1572872 | tf_op jit(solution)/shard_map/ppermute | solution.py:45
  119.4 10.9 %collective-permute-start.14 = (f32[128,1024]{1,0:T(8,128)S(1)}, f32[128,1024]{1,0:T(8,128)S(1)}, u32[]{:S(2)}, u32[]{:S(2)}) collective-permute-start(f32[128,1024]{1,0:T(8,128)S(1)} %get-tuple-element.154), channel_id=1, source_target_pairs={{8,0},{9,1},{10,2},{11,3},{12,4},{13,5},{14,6},{15,7},{16,24},{17,... | collective-permute-start | bytes 1572872 | tf_op jit(solution)/shard_map/ppermute | solution.py:45
  121.0 13.5 %collective-permute-start.5 = (f32[128,1024]{1,0:T(8,128)S(1)}, f32[128,1024]{1,0:T(8,128)S(1)}, u32[]{:S(2)}, u32[]{:S(2)}) collective-permute-start(f32[128,1024]{1,0:T(8,128)S(1)} %get-tuple-element.155), channel_id=1, source_target_pairs={{0,8},{1,9},{2,10},{3,11},{4,12},{5,13},{6,14},{7,15},{24,16},{25,... | collective-permute-start | bytes 1572872 | tf_op jit(solution)/shard_map/ppermute | solution.py:45
  153.5 42.4 %copy-start.24 = (f32[256,2560]{1,0:T(8,128)}, f32[256,2560]{1,0:T(8,128)S(1)}, u32[]{:S(2)}) copy-start(f32[256,2560]{1,0:T(8,128)S(1)} %get-tuple-element.140.grad_scores) | copy-start | bytes 7864324
  153.6 42.4 %copy-start.19 = (f32[128,1024]{1,0:T(8,128)}, f32[128,1024]{1,0:T(8,128)S(1)}, u32[]{:S(2)}) copy-start(f32[128,1024]{1,0:T(8,128)S(1)} %constant_dynamic-update-slice_fusion.refs_0_) | copy-start | bytes 1572868
  153.6 18.3 %collective-permute-start.17 = (f32[128,1024]{1,0:T(8,128)S(1)}, f32[128,1024]{1,0:T(8,128)S(1)}, u32[]{:S(2)}, u32[]{:S(2)}) collective-permute-start(f32[128,1024]{1,0:T(8,128)S(1)} %constant_dynamic-update-slice_fusion.refs_0_), channel_id=1, source_target_pairs={{0,8},{1,9},{2,10},{3,11},{4,12},{5,13},{6,14},{7,15},{8,0},{9,1},... | collective-permute-start | bytes 1572872 | tf_op jit(solution)/shard_map/ppermute | solution.py:45
  153.7 18.2 %collective-permute-start.18 = (f32[128,1024]{1,0:T(8,128)S(1)}, f32[128,1024]{1,0:T(8,128)S(1)}, u32[]{:S(2)}, u32[]{:S(2)}) collective-permute-start(f32[128,1024]{1,0:T(8,128)S(1)} %constant_dynamic-update-slice_fusion.refs_0_), channel_id=1, source_target_pairs={{0,4},{1,3},{2,6},{3,1},{4,0},{5,7},{6,2},{7,5},{8,12},{9,11},{10,... | collective-permute-start | bytes 1572872 | tf_op jit(solution)/shard_map/ppermute | solution.py:45
  154.1 21.9 %collective-permute-start.16 = (f32[128,1024]{1,0:T(8,128)S(1)}, f32[128,1024]{1,0:T(8,128)S(1)}, u32[]{:S(2)}, u32[]{:S(2)}) collective-permute-start(f32[128,1024]{1,0:T(8,128)S(1)} %constant_dynamic-update-slice_fusion.refs_0_), channel_id=1, source_target_pairs={{0,16},{1,17},{2,18},{3,19},{4,20},{5,21},{6,22},{7,23},{8,24},{9,... | collective-permute-start | bytes 1572872 | tf_op jit(solution)/shard_map/ppermute | solution.py:45
  171.9 39.1 %copy-start.30 = (f32[128,1024]{1,0:T(8,128)}, f32[128,1024]{1,0:T(8,128)S(1)}, u32[]{:S(2)}) copy-start(f32[128,1024]{1,0:T(8,128)S(1)} %collective-permute-done.17.refs_0_.refs_4_) | copy-start | bytes 1572868
  171.9 24.0 %copy-start.32 = (f32[128,1024]{1,0:T(8,128)}, f32[128,1024]{1,0:T(8,128)S(1)}, u32[]{:S(2)}) copy-start(f32[128,1024]{1,0:T(8,128)S(1)} %collective-permute-done.18.refs_1_) | copy-start | bytes 1572868
  171.9 8.3 %collective-permute-start.19 = (f32[128,1024]{1,0:T(8,128)S(1)}, f32[128,1024]{1,0:T(8,128)S(1)}, u32[]{:S(2)}, u32[]{:S(2)}) collective-permute-start(f32[128,1024]{1,0:T(8,128)S(1)} %collective-permute-done.17.refs_0_.refs_4_), channel_id=1, source_target_pairs={{0,4},{1,3},{2,6},{3,1},{4,0},{5,7},{6,2},{7,5},{8,12},{9,11},{10,... | collective-permute-start | bytes 1572872 | tf_op jit(solution)/shard_map/ppermute | solution.py:45
  172.3 28.9 %collective-permute-start.15 = (f32[128,1024]{1,0:T(8,128)S(1)}, f32[128,1024]{1,0:T(8,128)S(1)}, u32[]{:S(2)}, u32[]{:S(2)}) collective-permute-start(f32[128,1024]{1,0:T(8,128)S(1)} %constant_dynamic-update-slice_fusion.refs_0_), channel_id=1, source_target_pairs={{0,24},{1,25},{2,26},{3,27},{4,28},{5,29},{6,30},{7,31},{8,16},{9,... | collective-permute-start | bytes 1572872 | tf_op jit(solution)/shard_map/ppermute | solution.py:45
  174.6 12.8 %collective-permute-start.21 = (f32[128,1024]{1,0:T(8,128)S(1)}, f32[128,1024]{1,0:T(8,128)S(1)}, u32[]{:S(2)}, u32[]{:S(2)}) collective-permute-start(f32[128,1024]{1,0:T(8,128)S(1)} %constant_dynamic-update-slice_fusion.refs_0_), channel_id=1, source_target_pairs={{0,2},{1,5},{2,0},{3,7},{4,6},{5,1},{6,4},{7,3},{8,10},{9,13},{10,... | collective-permute-start | bytes 1572872 | tf_op jit(solution)/shard_map/ppermute | solution.py:45
  175.9 18.2 %collective-permute-start.22 = (f32[128,1024]{1,0:T(8,128)S(1)}, f32[128,1024]{1,0:T(8,128)S(1)}, u32[]{:S(2)}, u32[]{:S(2)}) collective-permute-start(f32[128,1024]{1,0:T(8,128)S(1)} %collective-permute-done.18.refs_1_), channel_id=1, source_target_pairs={{0,2},{1,5},{2,0},{3,7},{4,6},{5,1},{6,4},{7,3},{8,10},{9,13},{10,... | collective-permute-start | bytes 1572872 | tf_op jit(solution)/shard_map/ppermute | solution.py:45
  176.0 51.8 %copy-start.34 = (f32[128,1024]{1,0:T(8,128)}, f32[128,1024]{1,0:T(8,128)S(1)}, u32[]{:S(2)}) copy-start(f32[128,1024]{1,0:T(8,128)S(1)} %collective-permute-done.16.refs_0_.refs_8_) | copy-start | bytes 1572868
  180.3 20.9 %collective-permute-start.20 = (f32[128,1024]{1,0:T(8,128)S(1)}, f32[128,1024]{1,0:T(8,128)S(1)}, u32[]{:S(2)}, u32[]{:S(2)}) collective-permute-start(f32[128,1024]{1,0:T(8,128)S(1)} %collective-permute-done.16.refs_0_.refs_8_), channel_id=1, source_target_pairs={{0,4},{1,3},{2,6},{3,1},{4,0},{5,7},{6,2},{7,5},{8,12},{9,11},{10,... | collective-permute-start | bytes 1572872 | tf_op jit(solution)/shard_map/ppermute | solution.py:45
  180.6 24.3 %collective-permute-start.25 = (f32[128,1024]{1,0:T(8,128)S(1)}, f32[128,1024]{1,0:T(8,128)S(1)}, u32[]{:S(2)}, u32[]{:S(2)}) collective-permute-start(f32[128,1024]{1,0:T(8,128)S(1)} %collective-permute-done.17.refs_0_.refs_4_), channel_id=1, source_target_pairs={{0,2},{1,5},{2,0},{3,7},{4,6},{5,1},{6,4},{7,3},{8,10},{9,13},{10,... | collective-permute-start | bytes 1572872 | tf_op jit(solution)/shard_map/ppermute | solution.py:45
  187.4 23.6 %collective-permute-start.26 = (f32[128,1024]{1,0:T(8,128)S(1)}, f32[128,1024]{1,0:T(8,128)S(1)}, u32[]{:S(2)}, u32[]{:S(2)}) collective-permute-start(f32[128,1024]{1,0:T(8,128)S(1)} %collective-permute-done.19.refs_1_.refs_5_), channel_id=1, source_target_pairs={{0,2},{1,5},{2,0},{3,7},{4,6},{5,1},{6,4},{7,3},{8,10},{9,13},{10,... | collective-permute-start | bytes 1572872 | tf_op jit(solution)/shard_map/ppermute | solution.py:45
  201.2 28.6 %copy-start.38 = (f32[128,1024]{1,0:T(8,128)}, f32[128,1024]{1,0:T(8,128)S(1)}, u32[]{:S(2)}) copy-start(f32[128,1024]{1,0:T(8,128)S(1)} %collective-permute-done.15.refs_0_.refs_12_) | copy-start | bytes 1572868
  201.2 26.7 %copy-start.44 = (f32[128,1024]{1,0:T(8,128)}, f32[128,1024]{1,0:T(8,128)S(1)}, u32[]{:S(2)}) copy-start(f32[128,1024]{1,0:T(8,128)S(1)} %collective-permute-done.20.refs_1_.refs_9_) | copy-start | bytes 1572868
  201.2 14.2 %collective-permute-start.24 = (f32[128,1024]{1,0:T(8,128)S(1)}, f32[128,1024]{1,0:T(8,128)S(1)}, u32[]{:S(2)}, u32[]{:S(2)}) collective-permute-start(f32[128,1024]{1,0:T(8,128)S(1)} %collective-permute-done.15.refs_0_.refs_12_), channel_id=1, source_target_pairs={{0,4},{1,3},{2,6},{3,1},{4,0},{5,7},{6,2},{7,5},{8,12},{9,11},{10,... | collective-permute-start | bytes 1572872 | tf_op jit(solution)/shard_map/ppermute | solution.py:45
  202.8 21.1 %collective-permute-start.28 = (f32[128,1024]{1,0:T(8,128)S(1)}, f32[128,1024]{1,0:T(8,128)S(1)}, u32[]{:S(2)}, u32[]{:S(2)}) collective-permute-start(f32[128,1024]{1,0:T(8,128)S(1)} %collective-permute-done.16.refs_0_.refs_8_), channel_id=1, source_target_pairs={{0,2},{1,5},{2,0},{3,7},{4,6},{5,1},{6,4},{7,3},{8,10},{9,13},{10,... | collective-permute-start | bytes 1572872 | tf_op jit(solution)/shard_map/ppermute | solution.py:45
  204.8 23.0 %collective-permute-start.29 = (f32[128,1024]{1,0:T(8,128)S(1)}, f32[128,1024]{1,0:T(8,128)S(1)}, u32[]{:S(2)}, u32[]{:S(2)}) collective-permute-start(f32[128,1024]{1,0:T(8,128)S(1)} %collective-permute-done.20.refs_1_.refs_9_), channel_id=1, source_target_pairs={{0,2},{1,5},{2,0},{3,7},{4,6},{5,1},{6,4},{7,3},{8,10},{9,13},{10,... | collective-permute-start | bytes 1572872 | tf_op jit(solution)/shard_map/ppermute | solution.py:45
  204.9 28.6 %collective-permute-start.23 = (f32[128,1024]{1,0:T(8,128)S(1)}, f32[128,1024]{1,0:T(8,128)S(1)}, u32[]{:S(2)}, u32[]{:S(2)}) collective-permute-start(f32[128,1024]{1,0:T(8,128)S(1)} %collective-permute-done.15.refs_0_.refs_12_), channel_id=1, source_target_pairs={{0,2},{1,5},{2,0},{3,7},{4,6},{5,1},{6,4},{7,3},{8,10},{9,13},{10,... | collective-permute-start | bytes 1572872 | tf_op jit(solution)/shard_map/ppermute | solution.py:45
  215.4 23.4 %collective-permute-start.27 = (f32[128,1024]{1,0:T(8,128)S(1)}, f32[128,1024]{1,0:T(8,128)S(1)}, u32[]{:S(2)}, u32[]{:S(2)}) collective-permute-start(f32[128,1024]{1,0:T(8,128)S(1)} %collective-permute-done.24.refs_1_.refs_13_), channel_id=1, source_target_pairs={{0,2},{1,5},{2,0},{3,7},{4,6},{5,1},{6,4},{7,3},{8,10},{9,13},{10,... | collective-permute-start | bytes 1572872 | tf_op jit(solution)/shard_map/ppermute | solution.py:45
  217.4 13.7 %collective-permute-start.30 = (f32[4,160,128]{2,1,0:T(8,128)S(1)}, f32[4,160,128]{2,1,0:T(8,128)S(1)}, u32[]{:S(2)}, u32[]{:S(2)}) collective-permute-start(f32[4,160,128]{2,1,0:T(8,128)S(1)} %get-tuple-element.117), channel_id=1, source_target_pairs={{0,1},{1,0},{2,3},{3,2},{4,5},{5,4},{6,7},{7,6},{8,9},{9,8},{10,11... | collective-permute-start | bytes 983048 | tf_op jit(solution)/shard_map/ppermute | solution.py:578
  223.9 9.6 %collective-permute-start.31 = (f32[4,160,128]{2,1,0:T(8,128)S(1)}, f32[4,160,128]{2,1,0:T(8,128)S(1)}, u32[]{:S(2)}, u32[]{:S(2)}) collective-permute-start(f32[4,160,128]{2,1,0:T(8,128)S(1)} %get-tuple-element.119), channel_id=1, source_target_pairs={{0,1},{1,0},{2,3},{3,2},{4,5},{5,4},{6,7},{7,6},{8,9},{9,8},{10,11... | collective-permute-start | bytes 983048 | tf_op jit(solution)/shard_map/ppermute | solution.py:578
  229.7 3.8 %collective-permute-start.32 = (f32[4,160,128]{2,1,0:T(8,128)S(1)}, f32[4,160,128]{2,1,0:T(8,128)S(1)}, u32[]{:S(2)}, u32[]{:S(2)}) collective-permute-start(f32[4,160,128]{2,1,0:T(8,128)S(1)} %get-tuple-element.122), channel_id=1, source_target_pairs={{0,1},{1,0},{2,3},{3,2},{4,5},{5,4},{6,7},{7,6},{8,9},{9,8},{10,11... | collective-permute-start | bytes 983048 | tf_op jit(solution)/shard_map/ppermute | solution.py:578
  240.1 1.7 collective-permute-start.33
  243.6 38.0 %all-to-all-start.1 = ((f32[16,160,128]{2,1,0:T(8,128)}), f32[16,160,128]{2,1,0:T(8,128)S(1)}, u32[]{:S(2)}, u32[]{:S(2)}) async-start(f32[16,160,128]{2,1,0:T(8,128)} %copy-done.3), calls=%async_computation.1 | async-start | bytes 2621440 | tf_op jit(solution)/shard_map/all_to_all | solution.py:585
  281.7 3.5 %collective-permute-start.34 = (f32[8,160,128]{2,1,0:T(8,128)S(1)}, f32[8,160,128]{2,1,0:T(8,128)S(1)}, u32[]{:S(2)}, u32[]{:S(2)}) collective-permute-start(f32[8,160,128]{2,1,0:T(8,128)S(1)} %slice_select_fusion), channel_id=1, source_target_pairs={{0,1},{1,0},{2,3},{3,2},{4,5},{5,4},{6,7},{7,6},{8,9},{9,8},{10,11... | collective-permute-start | bytes 1966088 | tf_op jit(solution)/shard_map/ppermute | solution.py:595
  (59 other events, 410.3 us)

commit v4 on v3

--- a/solution.py
+++ b/solution.py
@@ -45,9 +45,14 @@
     return lax.ppermute(x, BOTH, pairs)
 
 
-def gathered_order(chip, core):
-    inner = jnp.where(core == 0, jnp.array([0, 2, 1, 3]), jnp.array([0, 1, 2, 3]))
-    return (chip ^ (jnp.arange(4)[:, None] * 4) ^ inner[None, :]).reshape(16)
+def gathered_inner(core):
+    return jnp.where(core == 0, jnp.array([0, 2, 1, 3]), jnp.array([0, 1, 2, 3]))
+
+
+def gathered_order(chip, inner):
+    middle = (chip // 4 == 1) | (chip // 4 == 2)
+    steps = jnp.where(middle, jnp.array([0, 1, 3, 2]), jnp.array([0, 1, 2, 3]))
+    return (chip ^ (steps[:, None] * 4) ^ inner[None, :]).reshape(16)
 
 
 def scatter_order(chip, core):
@@ -110,6 +115,10 @@
     n = a[0].shape[1]
     out = halves(dot(beside(a), beside(b), ((0,), (0,))))
     return out[:n] + out[n:]
+
+
+def row_sums(x):
+    return dot(beside(two_terms(x)), jnp.ones((2 * x.shape[1], HEAD_SIZE), jnp.bfloat16), ((1,), (0,)))
 
 
 def three_terms(x):
@@ -398,20 +407,22 @@
 
 def close_kernel(length, q1, q2, q3, g, g1, g2, kp, vp, total, stats, out, grad_scores, stats_out, gk, gv):
     query_terms = stack(q1), stack(q2), stack(q3)
+    plen = kp.shape[0]
     scores = dot_rows_exact(query_terms, kp[...]) * SCALE
     before = load_column(stats, 0)
     top = jnp.maximum(before, jnp.max(scores, -1, keepdims=True))
     weight = jnp.exp(before - top)
     expo = jnp.exp(scores - top)
-    denominator = weight * load_column(stats, 8) + jnp.sum(expo, -1, keepdims=True)
+    denominator = weight * load_column(stats, 8) + row_sums(expo)
     inverse = 1.0 / denominator
-    prob = expo * inverse
+    prob = expo * (inverse if plen == HEAD_SIZE else inverse[:, :1])
     prob_terms, value_terms = two_terms(prob), two_terms(vp[...])
     result = (weight * inverse) * stack(total) + dot_columns(prob_terms, value_terms)
     result = jnp.where(row_number(result.shape, g.shape[0]) < length[0], result, 0.0)
     upstream_terms = stack(g1), stack(g2)
-    inner = jnp.sum(stack(g) * result, -1, keepdims=True)
-    grad = prob * (dot_rows(upstream_terms, value_terms) - inner) * SCALE
+    inner = row_sums(stack(g) * result)
+    inner_here = inner if plen == HEAD_SIZE else inner[:, :1]
+    grad = prob * (dot_rows(upstream_terms, value_terms) - inner_here) * SCALE
     unstack(out, result)
     unstack(grad_scores, grad)
     save_columns(stats_out, top + jnp.log(denominator), inner)
@@ -554,20 +565,35 @@
 
     own = jnp.concatenate([own_k, own_v], 1)
     if short:
-        place = gathered_order(chip, core)[:4] ^ chip
-        listed = take_small(all_prompts, chip ^ jnp.arange(chips))
-        far = [own] + [permute(own, ACROSS[k]) for k in range(1, 4)]
+        place = gathered_inner(core)
+        listed = take_small(all_prompts, gathered_order(chip, jnp.arange(4)))
+        far = [own, permute(own, ACROSS[1])]
+        ahead = permute(own, MIDDLE)
         near, third, both = [permute(own, SECOND)], [permute(own, THIRD)], []
 
         def group(k):
             return [far[k], near[k], third[k], both[k]]
 
-        for k in range(1, 4):
-            done = hidden_part(place, group(0), weight_terms) if k == 3 else None
-            far[k], near[k - 1], done = lax.optimization_barrier((far[k], near[k - 1], done))
-            both.append(permute(near[k - 1], THIRD))
-            near.append(permute(far[k], SECOND))
-            third.append(permute(far[k], THIRD))
+        far[1], ahead, near[0], third[0] = lax.optimization_barrier(
+            (far[1], ahead, near[0], third[0])
+        )
+        beyond = permute(far[1], MIDDLE)
+        come = permute(ahead, OUTWARD)
+        near.append(permute(far[1], SECOND))
+        third.append(permute(far[1], THIRD))
+        both.append(permute(near[0], THIRD))
+        beyond, come, near[1] = lax.optimization_barrier((beyond, come, near[1]))
+        far.append(ahead + come)
+        come = permute(beyond, OUTWARD)
+        near.append(permute(far[2], SECOND))
+        third.append(permute(far[2], THIRD))
+        both.append(permute(near[1], THIRD))
+        done = hidden_part(place, group(0), weight_terms)
+        come, near[2], done = lax.optimization_barrier((come, near[2], done))
+        far.append(beyond + come)
+        near.append(permute(far[3], SECOND))
+        third.append(permute(far[3], THIRD))
+        both.append(permute(near[2], THIRD))
         parts = [done]
         near[3], done = lax.optimization_barrier(
             (near[3], hidden_part(place, group(1), weight_terms))
@@ -584,7 +610,7 @@
         come.append(lax.ppermute(parts[3][1], "mp", SWAP))
         back = lax.all_to_all(assemble(listed, [x for x, _ in parts], come), "dp", 0, 0)
 
-        order = take_small(all_prompts, gathered_order(chip, core))
+        order = take_small(all_prompts, gathered_order(chip, place))
         gathered = [x for k in range(4) for x in group(k)]
         grad_w_key, grad_w_value = weight_grad(order, here, mine, other, gathered)
         back, grad_w_key, grad_w_value, state = lax.optimization_barrier(

time: 288 us -> 281 us (0.976)
  waiting for transfers between devices: 120 us -> 107 us
  starting transfers between devices: 61.7 us -> 69.4 us
    ppermute x29 -> x31, waiting for transfers between devices: 107 us -> 94.7 us  [permute(): return lax.ppermute(x, BOTH, pairs)]
    ppermute x29 -> x31, starting transfers between devices: 36.5 us -> 41.5 us  [permute(): return lax.ppermute(x, BOTH, pairs)]
    ppermute x3, starting transfers between devices: 6.6 us -> 10.3 us  [per_device(): come = [lax.ppermute(give, 'mp', SWAP) for _, give in parts]]
    unnamed x141 -> x143, local copies, waits for them, and re-layouts: 30.1 us -> 28.9 us
  transfers between devices with their start and end apart: 37 -> 39, of which waited for: 22 -> 23; matrix products, arithmetic and copies ran while one was open for 1% -> 1% of each run, Pallas kernels for 15% -> 15%
where the time goes in v4:
time: 281 us; the launch traced here: 280 us
  waiting for transfers between devices  107 us (38%)
  starting transfers between devices  69.4 us (25%)
  Pallas kernels  68.8 us (24%)
  local copies, waits for them, and re-layouts  29.3 us (10%)
    ppermute x31, waiting for transfers between devices, permute(): return lax.ppermute(x, BOTH, pairs)  94.7 us
    ppermute x31, starting transfers between devices, permute(): return lax.ppermute(x, BOTH, pairs)  41.5 us
    pallas_call x3, Pallas kernels, attention(): call(kernel, name, (groups,), [pl.BlockSpec((x.shape[0], size), lambda i,...  38.4 us
    unnamed x143, local copies, waits for them, and re-layouts  28.9 us
    pallas_call x12, Pallas kernels, call_whole(): pl.pallas_call(kernel, out_shape=[jax.ShapeDtypeStruct(*shape) for shape...  26.1 us
    ppermute x3, starting transfers between devices, per_device(): come = [lax.ppermute(give, 'mp', SWAP) for _, give in parts]  10.3 us
    all_to_all x1, waiting for transfers between devices, per_device(): lax.all_to_all(turn(here, resp_prompt, prompt_hidden, chips), 'dp', 0, 0)  7.85 us
    all_to_all x1, starting transfers between devices, per_device(): lax.all_to_all(turn(here, resp_prompt, prompt_hidden, chips), 'dp', 0, 0)  6.66 us
  transfers between devices with their start and end apart: 39, of which 23 were waited for; matrix products, arithmetic and copies ran while one was open for 1% of the time, Pallas kernels for 15%

profile of v4, /device:TPU:9, one launch (start us, length us, event | category | flops | bytes accessed | tf_op | source)
XLA Modules:
  0.0 279.8 jit_solution(3719113270920912951)
XLA Ops:
  1.3 1.7 copy-done.26
  3.0 2.3 turn.1
  5.4 6.7 %all-to-all-start = ((f32[16,168,128]{2,1,0:T(8,128)}), f32[16,168,128]{2,1,0:T(8,128)S(1)}, u32[]{:S(2)}, u32[]{:S(2)}) async-start(f32[16,168,128]{2,1,0:T(8,128)} %turn.1), calls=%async_computation | async-start | bytes 2752512 | tf_op jit(solution)/shard_map/all_to_all | solution.py:498
  15.2 1.7 copy-done.25
  19.0 8.9 %open.1 = (f32[256,2560]{1,0:T(8,128)S(1)}, f32[256,512]{1,0:T(8,128)S(1)}, bf16[256,2560]{1,0:T(8,128)(2,1)S(1)}, bf16[256,2560]{1,0:T(8,128)(2,1)S(1)}, bf16[2...) custom-call(s32[1]{0:T(128)S(6)} %copy.27.length, ...), custom_call_target="tpu_custom_call" | custom-call | tf_op jit(solution)/shard_map/open/pallas_call | solution.py:446
  35.6 7.9 %all-to-all-done.own = f32[16,168,128]{2,1,0:T(8,128)S(1)} async-done(((f32[16,168,128]{2,1,0:T(8,128)}), f32[16,168,128]{2,1,0:T(8,128)S(1)}, u32[]{:S(2)}, u32[]{:S(2)}) %all-to-all-start) | async-done | bytes 1376288 | tf_op jit(solution)/shard_map/all_to_all | solution.py:498
  43.5 2.7 collective-permute-start
  49.0 2.6 project.7
  52.9 2.6 project.6
  55.9 2.6 project.5
  59.8 5.8 %collective-permute-done.10 = f32[256,1024]{1,0:T(8,128)S(1)} collective-permute-done((f32[256,1024]{1,0:T(8,128)S(1)}, f32[256,1024]{1,0:T(8,128)S(1)}, u32[]{:S(2)}, u32[]{:S(2)}) %collective-permute-start.10) | collective-permute-done | bytes 1048608 | tf_op jit(solution)/shard_map/ppermute | solution.py:45
  66.3 2.6 project.4
  70.2 12.3 %collective-permute-done.6 = f32[256,1024]{1,0:T(8,128)S(1)} collective-permute-done((f32[256,1024]{1,0:T(8,128)S(1)}, f32[256,1024]{1,0:T(8,128)S(1)}, u32[]{:S(2)}, u32[]{:S(2)}) %collective-permute-start.6) | collective-permute-done | bytes 1048608 | tf_op jit(solution)/shard_map/ppermute | solution.py:45
  84.6 14.8 %collective-permute-done.3 = f32[256,1024]{1,0:T(8,128)S(1)} collective-permute-done((f32[256,1024]{1,0:T(8,128)S(1)}, f32[256,1024]{1,0:T(8,128)S(1)}, u32[]{:S(2)}, u32[]{:S(2)}) %collective-permute-start.3) | collective-permute-done | bytes 1048608 | tf_op jit(solution)/shard_map/ppermute | solution.py:45
  101.5 2.5 collective-permute-start.13
  104.0 11.8 %collective-permute-done.1 = f32[256,1024]{1,0:T(8,128)S(1)} collective-permute-done((f32[256,1024]{1,0:T(8,128)S(1)}, f32[256,1024]{1,0:T(8,128)S(1)}, u32[]{:S(2)}, u32[]{:S(2)}) %collective-permute-start.1) | collective-permute-done | bytes 1048608 | tf_op jit(solution)/shard_map/ppermute | solution.py:45
  116.5 2.6 collective-permute-start.9
  121.0 1.7 collective-permute-start.5
  124.3 5.0 %collective-permute-done.9 = f32[128,1024]{1,0:T(8,128)S(1)} collective-permute-done((f32[128,1024]{1,0:T(8,128)S(1)}, f32[128,1024]{1,0:T(8,128)S(1)}, u32[]{:S(2)}, u32[]{:S(2)}) %collective-permute-start.9) | collective-permute-done | bytes 524320 | tf_op jit(solution)/shard_map/ppermute | solution.py:45
  130.3 4.1 %collective-permute-done.5 = f32[128,1024]{1,0:T(8,128)S(1)} collective-permute-done((f32[128,1024]{1,0:T(8,128)S(1)}, f32[128,1024]{1,0:T(8,128)S(1)}, u32[]{:S(2)}, u32[]{:S(2)}) %collective-permute-start.5) | collective-permute-done | bytes 524320 | tf_op jit(solution)/shard_map/ppermute | solution.py:45
  134.8 17.0 %close.1 = (f32[256,2560]{1,0:T(8,128)}, f32[256,2560]{1,0:T(8,128)S(1)}, f32[256,512]{1,0:T(8,128)S(1)}, f32[128,512]{1,0:T(8,128)S(1)}, f32[128,512]{1,0:T(8,128)S(1)}) custom-call(s32[1]{0:T(128)S(6)} %copy.27.length, bf16[256,2560]{1,0:T(8,128)(2,1)S(1)} %copy-done.5, bf16[256,2560]{1,0:T(8,128)(2,1)S(1)} %copy-done.8, bf16[256,2560]{1,0:T(8,128)(2,1)S(1)} %copy-done.11, ...), custom_call_target="tpu_custom_call" | custom-call | tf_op jit(solution)/shard_map/close/pallas_call | solution.py:446
  152.7 2.0 collective-permute-start.16
  156.3 2.2 collective-permute-start.18
  158.5 4.6 %collective-permute-done.15.refs_0_.refs_4_ = f32[128,1024]{1,0:T(8,128)S(1)} collective-permute-done((f32[128,1024]{1,0:T(8,128)S(1)}, f32[128,1024]{1,0:T(8,128)S(1)}, u32[]{:S(2)}, u32[]{:S(2)}) %collective-permute-start.15) | collective-permute-done | bytes 524320 | tf_op jit(solution)/shard_map/ppermute | solution.py:45
  163.1 1.9 collective-permute-done.16
  165.0 3.5 %collective-permute-done.18.refs_2_ = f32[128,1024]{1,0:T(8,128)S(1)} collective-permute-done((f32[128,1024]{1,0:T(8,128)S(1)}, f32[128,1024]{1,0:T(8,128)S(1)}, u32[]{:S(2)}, u32[]{:S(2)}) %collective-permute-start.18) | collective-permute-done | bytes 524320 | tf_op jit(solution)/shard_map/ppermute | solution.py:45
  168.5 1.9 collective-permute-start.19
  173.6 7.3 %collective-permute-done.19 = f32[128,1024]{1,0:T(8,128)S(1)} collective-permute-done((f32[128,1024]{1,0:T(8,128)S(1)}, f32[128,1024]{1,0:T(8,128)S(1)}, u32[]{:S(2)}, u32[]{:S(2)}) %collective-permute-start.19) | collective-permute-done | bytes 524320 | tf_op jit(solution)/shard_map/ppermute | solution.py:45
  181.0 3.2 %collective-permute-start.22 = (f32[128,1024]{1,0:T(8,128)S(1)}, f32[128,1024]{1,0:T(8,128)S(1)}, u32[]{:S(2)}, u32[]{:S(2)}) collective-permute-start(f32[128,1024]{1,0:T(8,128)S(1)} %collective-permute-done.19), channel_id=1, source_target_pairs={{8,0},{9,1},{10,2},{11,3},{12,4},{13,5},{14,6},{15,7},{16,24},{17,... | collective-permute-start | bytes 1572872 | tf_op jit(solution)/shard_map/ppermute | solution.py:45
  184.4 2.0 collective-permute-start.27
  186.5 1.8 hidden_part.4
  188.4 3.2 %collective-permute-done.22 = f32[128,1024]{1,0:T(8,128)S(1)} collective-permute-done((f32[128,1024]{1,0:T(8,128)S(1)}, f32[128,1024]{1,0:T(8,128)S(1)}, u32[]{:S(2)}, u32[]{:S(2)}) %collective-permute-start.22) | collective-permute-done | bytes 524320 | tf_op jit(solution)/shard_map/ppermute | solution.py:45
  192.8 3.2 %collective-permute-start.30 = (f32[128,1024]{1,0:T(8,128)S(1)}, f32[128,1024]{1,0:T(8,128)S(1)}, u32[]{:S(2)}, u32[]{:S(2)}) collective-permute-start(f32[128,1024]{1,0:T(8,128)S(1)} %add.103.refs_0_.refs_8_), channel_id=1, source_target_pairs={{0,2},{1,5},{2,0},{3,7},{4,6},{5,1},{6,4},{7,3},{8,10},{9,13},{10,... | collective-permute-start | bytes 1572872 | tf_op jit(solution)/shard_map/ppermute | solution.py:45
  197.6 6.9 %collective-permute-done.28.refs_3_.refs_7_ = f32[128,1024]{1,0:T(8,128)S(1)} collective-permute-done((f32[128,1024]{1,0:T(8,128)S(1)}, f32[128,1024]{1,0:T(8,128)S(1)}, u32[]{:S(2)}, u32[]{:S(2)}) %collective-permute-start.28) | collective-permute-done | bytes 524320 | tf_op jit(solution)/shard_map/ppermute | solution.py:45
  204.5 1.8 hidden_part.5
  206.8 3.2 %collective-permute-start.29 = (f32[128,1024]{1,0:T(8,128)S(1)}, f32[128,1024]{1,0:T(8,128)S(1)}, u32[]{:S(2)}, u32[]{:S(2)}) collective-permute-start(f32[128,1024]{1,0:T(8,128)S(1)} %collective-permute-done.26.refs_1_.refs_13_), channel_id=1, source_target_pairs={{0,2},{1,5},{2,0},{3,7},{4,6},{5,1},{6,4},{7,3},{8,10},{9,13},{10,... | collective-permute-start | bytes 1572872 | tf_op jit(solution)/shard_map/ppermute | solution.py:45
  210.0 9.5 %collective-permute-start.32 = (f32[4,160,128]{2,1,0:T(8,128)S(1)}, f32[4,160,128]{2,1,0:T(8,128)S(1)}, u32[]{:S(2)}, u32[]{:S(2)}) collective-permute-start(f32[4,160,128]{2,1,0:T(8,128)S(1)} %get-tuple-element.123), channel_id=1, source_target_pairs={{0,1},{1,0},{2,3},{3,2},{4,5},{5,4},{6,7},{7,6},{8,9},{9,8},{10,11... | collective-permute-start | bytes 983048 | tf_op jit(solution)/shard_map/ppermute | solution.py:604
  219.6 1.8 collective-permute-done.31.refs_3_.refs_11_
  221.4 1.8 hidden_part.6
  225.3 1.7 collective-permute-done.25.refs_0_.refs_14_
  227.0 5.6 %collective-permute-done.29.refs_1_.refs_15_ = f32[128,1024]{1,0:T(8,128)S(1)} collective-permute-done((f32[128,1024]{1,0:T(8,128)S(1)}, f32[128,1024]{1,0:T(8,128)S(1)}, u32[]{:S(2)}, u32[]{:S(2)}) %collective-permute-start.29) | collective-permute-done | bytes 524320 | tf_op jit(solution)/shard_map/ppermute | solution.py:45
  237.8 5.7 %all-to-all-start.1 = ((f32[16,160,128]{2,1,0:T(8,128)}), f32[16,160,128]{2,1,0:T(8,128)S(1)}, u32[]{:S(2)}, u32[]{:S(2)}) async-start(f32[16,160,128]{2,1,0:T(8,128)} %copy-done.3), calls=%async_computation.1 | async-start | bytes 2621440 | tf_op jit(solution)/shard_map/all_to_all | solution.py:611
  250.1 1.7 copy-done.29
  255.1 12.5 %finish.1 = (f32[256,2560]{1,0:T(8,128)}, f32[256,512]{1,0:T(8,128)}, f32[256,512]{1,0:T(8,128)}) custom-call(s32[1]{0:T(128)S(6)} %copy.27.length, bf16[256,2560]{1,0:T(8,128)(2,1)S(1)} %copy-done.6, bf16[256,2560]{1,0:T(8,128)(2,1)S(1)} %copy-done.9, bf16[256,2560]{1,0:T(8,128)(2,1)S(1)} %copy-done.12, bf16[256,2560]{1,0:T(8,128)(2,1)S(1)} %copy-done.15, ...), custom_call_target="tpu_custom_call" | custom-call | tf_op jit(solution)/shard_map/finish/pallas_call | solution.py:446
  267.7 6.6 %weight_grad.1 = (f32[320,512]{1,0:T(8,128)}, f32[320,512]{1,0:T(8,128)}) custom-call(s32[16]{0:T(128)S(1)} %get-tuple-element.157.listed, s32[1]{0:T(128)} %bitcast.core, f32[16,168,128]{2,1,0:T(8,128)S(1)} %all-to-all-done.own, f32[16,168,128]{2,1,0:T(8,128)} %collective-permute-done.other, f32[128,1024]{1,0:T(8,128)S(1)} %copy-done.24, ...), custom_call_target="tpu_custom_call" | custom-call | tf_op jit(solution)/shard_map/weight_grad/pallas_call | solution.py:155
  274.4 1.7 collective-permute-start.36
  276.1 1.7 collective-permute-done.36.other
  277.8 2.0 turn_back.1
  (218 shorter events, 55.6 us)
Async XLA Ops:
  5.4 38.1 %all-to-all-start = ((f32[16,168,128]{2,1,0:T(8,128)}), f32[16,168,128]{2,1,0:T(8,128)S(1)}, u32[]{:S(2)}, u32[]{:S(2)}) async-start(f32[16,168,128]{2,1,0:T(8,128)} %turn.1), calls=%async_computation | async-start | bytes 2752512 | tf_op jit(solution)/shard_map/all_to_all | solution.py:498
  19.0 27.2 %copy-start.70 = (s32[4]{0:T(128)S(1)}, s32[4]{0:T(128)}, u32[]{:S(2)}) copy-start(s32[4]{0:T(128)} %constant.54.clone) | copy-start | bytes 52
  19.0 27.4 %copy-start.66 = (s32[4,4]{1,0:T(4,128)S(1)}, s32[4,4]{1,0:T(4,128)}, u32[]{:S(2)}) copy-start(s32[4,4]{1,0:T(4,128)} %constant.50.clone) | copy-start | bytes 196
  43.5 5.6 %collective-permute-start = (f32[16,168,128]{2,1,0:T(8,128)S(1)}, f32[16,168,128]{2,1,0:T(8,128)}, u32[]{:S(2)}, u32[]{:S(2)}) collective-permute-start(f32[16,168,128]{2,1,0:T(8,128)S(1)} %all-to-all-done.own), channel_id=1, source_target_pairs={{0,1},{1,0},{2,3},{3,2},{4,5},{5,4},{6,7},{7,6},{8,9},{9,8},{10,11... | collective-permute-start | bytes 4128776 | tf_op jit(solution)/shard_map/ppermute | solution.py:528
  51.7 14.0 %collective-permute-start.10 = (f32[256,1024]{1,0:T(8,128)S(1)}, f32[256,1024]{1,0:T(8,128)S(1)}, u32[]{:S(2)}, u32[]{:S(2)}) collective-permute-start(f32[256,1024]{1,0:T(8,128)S(1)} %get-tuple-element.103), channel_id=1, source_target_pairs={{0,2},{1,5},{2,0},{3,7},{4,6},{5,1},{6,4},{7,3},{8,10},{9,13},{10,... | collective-permute-start | bytes 3145736 | tf_op jit(solution)/shard_map/ppermute | solution.py:45
  55.6 26.9 %collective-permute-start.6 = (f32[256,1024]{1,0:T(8,128)S(1)}, f32[256,1024]{1,0:T(8,128)S(1)}, u32[]{:S(2)}, u32[]{:S(2)}) collective-permute-start(f32[256,1024]{1,0:T(8,128)S(1)} %get-tuple-element.101), channel_id=1, source_target_pairs={{0,2},{1,5},{2,0},{3,7},{4,6},{5,1},{6,4},{7,3},{8,10},{9,13},{10,... | collective-permute-start | bytes 3145736 | tf_op jit(solution)/shard_map/ppermute | solution.py:45
  58.5 40.8 %collective-permute-start.3 = (f32[256,1024]{1,0:T(8,128)S(1)}, f32[256,1024]{1,0:T(8,128)S(1)}, u32[]{:S(2)}, u32[]{:S(2)}) collective-permute-start(f32[256,1024]{1,0:T(8,128)S(1)} %get-tuple-element.99), channel_id=1, source_target_pairs={{0,2},{1,5},{2,0},{3,7},{4,6},{5,1},{6,4},{7,3},{8,10},{9,13},{10,... | collective-permute-start | bytes 3145736 | tf_op jit(solution)/shard_map/ppermute | solution.py:45
  65.8 17.4 %collective-permute-start.11 = (f32[128,1024]{1,0:T(8,128)S(1)}, f32[128,1024]{1,0:T(8,128)S(1)}, u32[]{:S(2)}, u32[]{:S(2)}) collective-permute-start(f32[128,1024]{1,0:T(8,128)S(1)} %slice_add_fusion), channel_id=1, source_target_pairs={{0,4},{1,3},{2,6},{3,1},{4,0},{5,7},{6,2},{7,5},{8,12},{9,11},{10,... | collective-permute-start | bytes 1572872 | tf_op jit(solution)/shard_map/ppermute | solution.py:45
  68.9 46.9 %collective-permute-start.1 = (f32[256,1024]{1,0:T(8,128)S(1)}, f32[256,1024]{1,0:T(8,128)S(1)}, u32[]{:S(2)}, u32[]{:S(2)}) collective-permute-start(f32[256,1024]{1,0:T(8,128)S(1)} %get-tuple-element.97), channel_id=1, source_target_pairs={{0,2},{1,5},{2,0},{3,7},{4,6},{5,1},{6,4},{7,3},{8,10},{9,13},{10,... | collective-permute-start | bytes 3145736 | tf_op jit(solution)/shard_map/ppermute | solution.py:45
  82.6 16.9 %collective-permute-start.7 = (f32[128,1024]{1,0:T(8,128)S(1)}, f32[128,1024]{1,0:T(8,128)S(1)}, u32[]{:S(2)}, u32[]{:S(2)}) collective-permute-start(f32[128,1024]{1,0:T(8,128)S(1)} %slice_add_fusion.2), channel_id=1, source_target_pairs={{0,4},{1,3},{2,6},{3,1},{4,0},{5,7},{6,2},{7,5},{8,12},{9,11},{10,... | collective-permute-start | bytes 1572872 | tf_op jit(solution)/shard_map/ppermute | solution.py:45
  83.3 18.2 %collective-permute-start.12 = (f32[128,1024]{1,0:T(8,128)S(1)}, f32[128,1024]{1,0:T(8,128)S(1)}, u32[]{:S(2)}, u32[]{:S(2)}) collective-permute-start(f32[128,1024]{1,0:T(8,128)S(1)} %fusion), channel_id=1, source_target_pairs={{0,8},{1,9},{2,10},{3,11},{4,12},{5,13},{6,14},{7,15},{24,16},{25,... | collective-permute-start | bytes 1572872 | tf_op jit(solution)/shard_map/ppermute | solution.py:45
  99.6 16.8 %collective-permute-start.8 = (f32[128,1024]{1,0:T(8,128)S(1)}, f32[128,1024]{1,0:T(8,128)S(1)}, u32[]{:S(2)}, u32[]{:S(2)}) collective-permute-start(f32[128,1024]{1,0:T(8,128)S(1)} %fusion.1), channel_id=1, source_target_pairs={{0,8},{1,9},{2,10},{3,11},{4,12},{5,13},{6,14},{7,15},{24,16},{25,... | collective-permute-start | bytes 1572872 | tf_op jit(solution)/shard_map/ppermute | solution.py:45
  100.9 18.2 %collective-permute-start.4 = (f32[128,1024]{1,0:T(8,128)S(1)}, f32[128,1024]{1,0:T(8,128)S(1)}, u32[]{:S(2)}, u32[]{:S(2)}) collective-permute-start(f32[128,1024]{1,0:T(8,128)S(1)} %slice_add_fusion.4), channel_id=1, source_target_pairs={{0,4},{1,3},{2,6},{3,1},{4,0},{5,7},{6,2},{7,5},{8,12},{9,11},{10,... | collective-permute-start | bytes 1572872 | tf_op jit(solution)/shard_map/ppermute | solution.py:45
  101.5 17.6 %collective-permute-start.13 = (f32[128,1024]{1,0:T(8,128)S(1)}, f32[128,1024]{1,0:T(8,128)S(1)}, u32[]{:S(2)}, u32[]{:S(2)}) collective-permute-start(f32[128,1024]{1,0:T(8,128)S(1)} %add.100), channel_id=1, source_target_pairs={{8,16},{9,17},{10,18},{11,19},{12,20},{13,21},{14,22},{15,23},{16,... | collective-permute-start | bytes 1572872 | tf_op jit(solution)/shard_map/ppermute | solution.py:45
  115.9 8.4 %collective-permute-start.2 = (f32[128,1024]{1,0:T(8,128)S(1)}, f32[128,1024]{1,0:T(8,128)S(1)}, u32[]{:S(2)}, u32[]{:S(2)}) collective-permute-start(f32[128,1024]{1,0:T(8,128)S(1)} %slice_add_fusion.6), channel_id=1, source_target_pairs={{0,4},{1,3},{2,6},{3,1},{4,0},{5,7},{6,2},{7,5},{8,12},{9,11},{10,... | collective-permute-start | bytes 1572872 | tf_op jit(solution)/shard_map/ppermute | solution.py:45
  116.5 12.8 %collective-permute-start.9 = (f32[128,1024]{1,0:T(8,128)S(1)}, f32[128,1024]{1,0:T(8,128)S(1)}, u32[]{:S(2)}, u32[]{:S(2)}) collective-permute-start(f32[128,1024]{1,0:T(8,128)S(1)} %add.95), channel_id=1, source_target_pairs={{8,16},{9,17},{10,18},{11,19},{12,20},{13,21},{14,22},{15,23},{16,... | collective-permute-start | bytes 1572872 | tf_op jit(solution)/shard_map/ppermute | solution.py:45
  119.3 10.9 %collective-permute-start.14 = (f32[128,1024]{1,0:T(8,128)S(1)}, f32[128,1024]{1,0:T(8,128)S(1)}, u32[]{:S(2)}, u32[]{:S(2)}) collective-permute-start(f32[128,1024]{1,0:T(8,128)S(1)} %get-tuple-element.160), channel_id=1, source_target_pairs={{8,0},{9,1},{10,2},{11,3},{12,4},{13,5},{14,6},{15,7},{16,24},{17,... | collective-permute-start | bytes 1572872 | tf_op jit(solution)/shard_map/ppermute | solution.py:45
  121.0 13.4 %collective-permute-start.5 = (f32[128,1024]{1,0:T(8,128)S(1)}, f32[128,1024]{1,0:T(8,128)S(1)}, u32[]{:S(2)}, u32[]{:S(2)}) collective-permute-start(f32[128,1024]{1,0:T(8,128)S(1)} %get-tuple-element.161), channel_id=1, source_target_pairs={{0,8},{1,9},{2,10},{3,11},{4,12},{5,13},{6,14},{7,15},{24,16},{25,... | collective-permute-start | bytes 1572872 | tf_op jit(solution)/shard_map/ppermute | solution.py:45
  152.6 35.7 %copy-start.28 = (f32[256,2560]{1,0:T(8,128)}, f32[256,2560]{1,0:T(8,128)S(1)}, u32[]{:S(2)}) copy-start(f32[256,2560]{1,0:T(8,128)S(1)} %get-tuple-element.146.grad_scores) | copy-start | bytes 7864324
  152.6 35.7 %copy-start.23 = (f32[128,1024]{1,0:T(8,128)}, f32[128,1024]{1,0:T(8,128)S(1)}, u32[]{:S(2)}) copy-start(f32[128,1024]{1,0:T(8,128)S(1)} %constant_dynamic-update-slice_fusion.refs_0_) | copy-start | bytes 1572868
  152.6 10.4 %collective-permute-start.15 = (f32[128,1024]{1,0:T(8,128)S(1)}, f32[128,1024]{1,0:T(8,128)S(1)}, u32[]{:S(2)}, u32[]{:S(2)}) collective-permute-start(f32[128,1024]{1,0:T(8,128)S(1)} %constant_dynamic-update-slice_fusion.refs_0_), channel_id=1, source_target_pairs={{0,8},{1,9},{2,10},{3,11},{4,12},{5,13},{6,14},{7,15},{8,0},{9,1},... | collective-permute-start | bytes 1572872 | tf_op jit(solution)/shard_map/ppermute | solution.py:45
  152.7 12.3 %collective-permute-start.16 = (f32[128,1024]{1,0:T(8,128)S(1)}, f32[128,1024]{1,0:T(8,128)S(1)}, u32[]{:S(2)}, u32[]{:S(2)}) collective-permute-start(f32[128,1024]{1,0:T(8,128)S(1)} %constant_dynamic-update-slice_fusion.refs_0_), channel_id=1, source_target_pairs={{8,16},{9,17},{10,18},{11,19},{12,20},{13,21},{14,22},{15,23},{16,... | collective-permute-start | bytes 1572872 | tf_op jit(solution)/shard_map/ppermute | solution.py:45
  154.7 10.3 %collective-permute-start.17 = (f32[128,1024]{1,0:T(8,128)S(1)}, f32[128,1024]{1,0:T(8,128)S(1)}, u32[]{:S(2)}, u32[]{:S(2)}) collective-permute-start(f32[128,1024]{1,0:T(8,128)S(1)} %constant_dynamic-update-slice_fusion.refs_0_), channel_id=1, source_target_pairs={{0,4},{1,3},{2,6},{3,1},{4,0},{5,7},{6,2},{7,5},{8,12},{9,11},{10,... | collective-permute-start | bytes 1572872 | tf_op jit(solution)/shard_map/ppermute | solution.py:45
  156.3 12.2 %collective-permute-start.18 = (f32[128,1024]{1,0:T(8,128)S(1)}, f32[128,1024]{1,0:T(8,128)S(1)}, u32[]{:S(2)}, u32[]{:S(2)}) collective-permute-start(f32[128,1024]{1,0:T(8,128)S(1)} %constant_dynamic-update-slice_fusion.refs_0_), channel_id=1, source_target_pairs={{0,2},{1,5},{2,0},{3,7},{4,6},{5,1},{6,4},{7,3},{8,10},{9,13},{10,... | collective-permute-start | bytes 1572872 | tf_op jit(solution)/shard_map/ppermute | solution.py:45
  163.1 41.4 %copy-start.34 = (f32[128,1024]{1,0:T(8,128)}, f32[128,1024]{1,0:T(8,128)S(1)}, u32[]{:S(2)}) copy-start(f32[128,1024]{1,0:T(8,128)S(1)} %collective-permute-done.15.refs_0_.refs_4_) | copy-start | bytes 1572868
  168.5 12.4 %collective-permute-start.19 = (f32[128,1024]{1,0:T(8,128)S(1)}, f32[128,1024]{1,0:T(8,128)S(1)}, u32[]{:S(2)}, u32[]{:S(2)}) collective-permute-start(f32[128,1024]{1,0:T(8,128)S(1)} %collective-permute-done.15.refs_0_.refs_4_), channel_id=1, source_target_pairs={{8,16},{9,17},{10,18},{11,19},{12,20},{13,21},{14,22},{15,23},{16,... | collective-permute-start | bytes 1572872 | tf_op jit(solution)/shard_map/ppermute | solution.py:45
  170.4 10.5 %collective-permute-start.20 = (f32[128,1024]{1,0:T(8,128)S(1)}, f32[128,1024]{1,0:T(8,128)S(1)}, u32[]{:S(2)}, u32[]{:S(2)}) collective-permute-start(f32[128,1024]{1,0:T(8,128)S(1)} %collective-permute-done.16), channel_id=1, source_target_pairs={{8,0},{9,1},{10,2},{11,3},{12,4},{13,5},{14,6},{15,7},{16,24},{17,... | collective-permute-start | bytes 1572872 | tf_op jit(solution)/shard_map/ppermute | solution.py:45
  171.8 9.2 %collective-permute-start.21 = (f32[128,1024]{1,0:T(8,128)S(1)}, f32[128,1024]{1,0:T(8,128)S(1)}, u32[]{:S(2)}, u32[]{:S(2)}) collective-permute-start(f32[128,1024]{1,0:T(8,128)S(1)} %collective-permute-done.15.refs_0_.refs_4_), channel_id=1, source_target_pairs={{0,4},{1,3},{2,6},{3,1},{4,0},{5,7},{6,2},{7,5},{8,12},{9,11},{10,... | collective-permute-start | bytes 1572872 | tf_op jit(solution)/shard_map/ppermute | solution.py:45
  172.0 14.5 %collective-permute-start.24 = (f32[128,1024]{1,0:T(8,128)S(1)}, f32[128,1024]{1,0:T(8,128)S(1)}, u32[]{:S(2)}, u32[]{:S(2)}) collective-permute-start(f32[128,1024]{1,0:T(8,128)S(1)} %collective-permute-done.17.refs_1_), channel_id=1, source_target_pairs={{0,2},{1,5},{2,0},{3,7},{4,6},{5,1},{6,4},{7,3},{8,10},{9,13},{10,... | collective-permute-start | bytes 1572872 | tf_op jit(solution)/shard_map/ppermute | solution.py:45
  181.0 23.6 %copy-start.40 = (f32[128,1024]{1,0:T(8,128)}, f32[128,1024]{1,0:T(8,128)S(1)}, u32[]{:S(2)}) copy-start(f32[128,1024]{1,0:T(8,128)S(1)} %collective-permute-done.21.refs_1_.refs_5_) | copy-start | bytes 1572868
  181.0 10.6 %collective-permute-start.22 = (f32[128,1024]{1,0:T(8,128)S(1)}, f32[128,1024]{1,0:T(8,128)S(1)}, u32[]{:S(2)}, u32[]{:S(2)}) collective-permute-start(f32[128,1024]{1,0:T(8,128)S(1)} %collective-permute-done.19), channel_id=1, source_target_pairs={{8,0},{9,1},{10,2},{11,3},{12,4},{13,5},{14,6},{15,7},{16,24},{17,... | collective-permute-start | bytes 1572872 | tf_op jit(solution)/shard_map/ppermute | solution.py:45
  184.3 37.1 %copy-start.19 = (f32[128,1024]{1,0:T(8,128)}, f32[128,1024]{1,0:T(8,128)S(1)}, u32[]{:S(2)}) copy-start(f32[128,1024]{1,0:T(8,128)S(1)} %add.103.refs_0_.refs_8_) | copy-start | bytes 1572868
  184.3 8.4 %collective-permute-start.23 = (f32[128,1024]{1,0:T(8,128)S(1)}, f32[128,1024]{1,0:T(8,128)S(1)}, u32[]{:S(2)}, u32[]{:S(2)}) collective-permute-start(f32[128,1024]{1,0:T(8,128)S(1)} %add.103.refs_0_.refs_8_), channel_id=1, source_target_pairs={{0,4},{1,3},{2,6},{3,1},{4,0},{5,7},{6,2},{7,5},{8,12},{9,11},{10,... | collective-permute-start | bytes 1572872 | tf_op jit(solution)/shard_map/ppermute | solution.py:45
  184.4 11.8 %collective-permute-start.27 = (f32[128,1024]{1,0:T(8,128)S(1)}, f32[128,1024]{1,0:T(8,128)S(1)}, u32[]{:S(2)}, u32[]{:S(2)}) collective-permute-start(f32[128,1024]{1,0:T(8,128)S(1)} %collective-permute-done.15.refs_0_.refs_4_), channel_id=1, source_target_pairs={{0,2},{1,5},{2,0},{3,7},{4,6},{5,1},{6,4},{7,3},{8,10},{9,13},{10,... | collective-permute-start | bytes 1572872 | tf_op jit(solution)/shard_map/ppermute | solution.py:45
  186.4 18.1 %collective-permute-start.28 = (f32[128,1024]{1,0:T(8,128)S(1)}, f32[128,1024]{1,0:T(8,128)S(1)}, u32[]{:S(2)}, u32[]{:S(2)}) collective-permute-start(f32[128,1024]{1,0:T(8,128)S(1)} %collective-permute-done.21.refs_1_.refs_5_), channel_id=1, source_target_pairs={{0,2},{1,5},{2,0},{3,7},{4,6},{5,1},{6,4},{7,3},{8,10},{9,13},{10,... | collective-permute-start | bytes 1572872 | tf_op jit(solution)/shard_map/ppermute | solution.py:45
  192.7 28.7 %copy-start.44 = (f32[128,1024]{1,0:T(8,128)}, f32[128,1024]{1,0:T(8,128)S(1)}, u32[]{:S(2)}) copy-start(f32[128,1024]{1,0:T(8,128)S(1)} %collective-permute-done.23.refs_1_.refs_9_) | copy-start | bytes 1572868
  192.8 31.2 %copy-start.21 = (f32[128,1024]{1,0:T(8,128)}, f32[128,1024]{1,0:T(8,128)S(1)}, u32[]{:S(2)}) copy-start(f32[128,1024]{1,0:T(8,128)S(1)} %add.104.refs_0_.refs_12_) | copy-start | bytes 1572868
  192.8 14.1 %collective-permute-start.26 = (f32[128,1024]{1,0:T(8,128)S(1)}, f32[128,1024]{1,0:T(8,128)S(1)}, u32[]{:S(2)}, u32[]{:S(2)}) collective-permute-start(f32[128,1024]{1,0:T(8,128)S(1)} %add.104.refs_0_.refs_12_), channel_id=1, source_target_pairs={{0,4},{1,3},{2,6},{3,1},{4,0},{5,7},{6,2},{7,5},{8,12},{9,11},{10,... | collective-permute-start | bytes 1572872 | tf_op jit(solution)/shard_map/ppermute | solution.py:45
  192.8 26.7 %collective-permute-start.30 = (f32[128,1024]{1,0:T(8,128)S(1)}, f32[128,1024]{1,0:T(8,128)S(1)}, u32[]{:S(2)}, u32[]{:S(2)}) collective-permute-start(f32[128,1024]{1,0:T(8,128)S(1)} %add.103.refs_0_.refs_8_), channel_id=1, source_target_pairs={{0,2},{1,5},{2,0},{3,7},{4,6},{5,1},{6,4},{7,3},{8,10},{9,13},{10,... | collective-permute-start | bytes 1572872 | tf_op jit(solution)/shard_map/ppermute | solution.py:45
  196.1 25.3 %collective-permute-start.31 = (f32[128,1024]{1,0:T(8,128)S(1)}, f32[128,1024]{1,0:T(8,128)S(1)}, u32[]{:S(2)}, u32[]{:S(2)}) collective-permute-start(f32[128,1024]{1,0:T(8,128)S(1)} %collective-permute-done.23.refs_1_.refs_9_), channel_id=1, source_target_pairs={{0,2},{1,5},{2,0},{3,7},{4,6},{5,1},{6,4},{7,3},{8,10},{9,13},{10,... | collective-permute-start | bytes 1572872 | tf_op jit(solution)/shard_map/ppermute | solution.py:45
  196.2 30.8 %collective-permute-start.25 = (f32[128,1024]{1,0:T(8,128)S(1)}, f32[128,1024]{1,0:T(8,128)S(1)}, u32[]{:S(2)}, u32[]{:S(2)}) collective-permute-start(f32[128,1024]{1,0:T(8,128)S(1)} %add.104.refs_0_.refs_12_), channel_id=1, source_target_pairs={{0,2},{1,5},{2,0},{3,7},{4,6},{5,1},{6,4},{7,3},{8,10},{9,13},{10,... | collective-permute-start | bytes 1572872 | tf_op jit(solution)/shard_map/ppermute | solution.py:45
  206.8 25.8 %collective-permute-start.29 = (f32[128,1024]{1,0:T(8,128)S(1)}, f32[128,1024]{1,0:T(8,128)S(1)}, u32[]{:S(2)}, u32[]{:S(2)}) collective-permute-start(f32[128,1024]{1,0:T(8,128)S(1)} %collective-permute-done.26.refs_1_.refs_13_), channel_id=1, source_target_pairs={{0,2},{1,5},{2,0},{3,7},{4,6},{5,1},{6,4},{7,3},{8,10},{9,13},{10,... | collective-permute-start | bytes 1572872 | tf_op jit(solution)/shard_map/ppermute | solution.py:45
  210.0 15.3 %collective-permute-start.32 = (f32[4,160,128]{2,1,0:T(8,128)S(1)}, f32[4,160,128]{2,1,0:T(8,128)S(1)}, u32[]{:S(2)}, u32[]{:S(2)}) collective-permute-start(f32[4,160,128]{2,1,0:T(8,128)S(1)} %get-tuple-element.123), channel_id=1, source_target_pairs={{0,1},{1,0},{2,3},{3,2},{4,5},{5,4},{6,7},{7,6},{8,9},{9,8},{10,11... | collective-permute-start | bytes 983048 | tf_op jit(solution)/shard_map/ppermute | solution.py:604
  219.5 7.5 %collective-permute-start.33 = (f32[4,160,128]{2,1,0:T(8,128)S(1)}, f32[4,160,128]{2,1,0:T(8,128)S(1)}, u32[]{:S(2)}, u32[]{:S(2)}) collective-permute-start(f32[4,160,128]{2,1,0:T(8,128)S(1)} %get-tuple-element.125), channel_id=1, source_target_pairs={{0,1},{1,0},{2,3},{3,2},{4,5},{5,4},{6,7},{7,6},{8,9},{9,8},{10,11... | collective-permute-start | bytes 983048 | tf_op jit(solution)/shard_map/ppermute | solution.py:604
  223.2 3.8 %collective-permute-start.34 = (f32[4,160,128]{2,1,0:T(8,128)S(1)}, f32[4,160,128]{2,1,0:T(8,128)S(1)}, u32[]{:S(2)}, u32[]{:S(2)}) collective-permute-start(f32[4,160,128]{2,1,0:T(8,128)S(1)} %get-tuple-element.128), channel_id=1, source_target_pairs={{0,1},{1,0},{2,3},{3,2},{4,5},{5,4},{6,7},{7,6},{8,9},{9,8},{10,11... | collective-permute-start | bytes 983048 | tf_op jit(solution)/shard_map/ppermute | solution.py:604
  233.9 2.0 collective-permute-start.35
  237.8 36.5 %all-to-all-start.1 = ((f32[16,160,128]{2,1,0:T(8,128)}), f32[16,160,128]{2,1,0:T(8,128)S(1)}, u32[]{:S(2)}, u32[]{:S(2)}) async-start(f32[16,160,128]{2,1,0:T(8,128)} %copy-done.3), calls=%async_computation.1 | async-start | bytes 2621440 | tf_op jit(solution)/shard_map/all_to_all | solution.py:611
  274.4 3.5 %collective-permute-start.36 = (f32[8,160,128]{2,1,0:T(8,128)S(1)}, f32[8,160,128]{2,1,0:T(8,128)S(1)}, u32[]{:S(2)}, u32[]{:S(2)}) collective-permute-start(f32[8,160,128]{2,1,0:T(8,128)S(1)} %slice_select_fusion), channel_id=1, source_target_pairs={{0,1},{1,0},{2,3},{3,2},{4,5},{5,4},{6,7},{7,6},{8,9},{9,8},{10,11... | collective-permute-start | bytes 1966088 | tf_op jit(solution)/shard_map/ppermute | solution.py:621
  (62 other events, 508.2 us)

commit v5 on v4

--- a/solution.py
+++ b/solution.py
@@ -559,7 +559,12 @@
             "finish",
             groups,
             resp_len,
-            query_terms + upstream_terms + own_ins + kept_ins,
+            [
+                (pltpu.with_memory_space_constraint(x, pltpu.HBM), size, skip)
+                for x, size, skip in query_terms + upstream_terms
+            ]
+            + own_ins
+            + kept_ins,
             [whole_heads] + [one_head] * 2,
         )
 
@@ -612,9 +617,10 @@
 
         order = take_small(all_prompts, gathered_order(chip, place))
         gathered = [x for k in range(4) for x in group(k)]
+        gathered, state = lax.optimization_barrier((gathered, finish(stats_late)))
         grad_w_key, grad_w_value = weight_grad(order, here, mine, other, gathered)
         back, grad_w_key, grad_w_value, state = lax.optimization_barrier(
-            (back, grad_w_key, grad_w_value, finish(stats_late))
+            (back, grad_w_key, grad_w_value, state)
         )
         grad_query, grad_keys, grad_values = state
         leave = jnp.where(core == 0, back[chips // 2 :], back[: chips // 2])

time: 281 us -> 281 us (level)
  local copies, waits for them, and re-layouts: 29.3 us -> 22.7 us
  waiting for transfers between devices: 107 us -> 112 us
    unnamed x143 -> x133, local copies, waits for them, and re-layouts: 28.9 us -> 22.4 us
    all_to_all x1, waiting for transfers between devices: 0.01 us -> 5.07 us  [per_device(): lax.all_to_all(assemble(listed, [x for x, _ in parts], come), 'dp', 0, 0)]
  transfers between devices with their start and end apart: 39 -> 39, of which waited for: 23 -> 24; matrix products, arithmetic and copies ran while one was open for 1% -> 1% of each run, Pallas kernels for 15% -> 16%
where the time goes in v5:
time: 281 us; the launch traced here: 280 us
  waiting for transfers between devices  112 us (40%)
  starting transfers between devices  70.2 us (25%)
  Pallas kernels  69.5 us (25%)
  local copies, waits for them, and re-layouts  22.7 us (8%)
    ppermute x31, waiting for transfers between devices, permute(): return lax.ppermute(x, BOTH, pairs)  94.7 us
    ppermute x31, starting transfers between devices, permute(): return lax.ppermute(x, BOTH, pairs)  41.6 us
    pallas_call x3, Pallas kernels, attention(): call(kernel, name, (groups,), [pl.BlockSpec((x.shape[0], size), lambda i,...  39.2 us
    pallas_call x12, Pallas kernels, call_whole(): pl.pallas_call(kernel, out_shape=[jax.ShapeDtypeStruct(*shape) for shape...  26.1 us
    unnamed x133, local copies, waits for them, and re-layouts  22.4 us
    ppermute x3, starting transfers between devices, per_device(): come = [lax.ppermute(give, 'mp', SWAP) for _, give in parts]  10.3 us
    all_to_all x1, waiting for transfers between devices, per_device(): lax.all_to_all(turn(here, resp_prompt, prompt_hidden, chips), 'dp', 0, 0)  7.84 us
    all_to_all x1, starting transfers between devices, per_device(): lax.all_to_all(turn(here, resp_prompt, prompt_hidden, chips), 'dp', 0, 0)  6.66 us
  transfers between devices with their start and end apart: 39, of which 24 were waited for; matrix products, arithmetic and copies ran while one was open for 1% of the time, Pallas kernels for 16%

profile of v5, /device:TPU:9, one launch (start us, length us, event | category | flops | bytes accessed | tf_op | source)
XLA Modules:
  0.0 279.8 jit_solution(3585046087593458712)
XLA Ops:
  1.3 1.7 copy-done.21
  3.0 2.3 turn.1
  5.4 6.7 %all-to-all-start = ((f32[16,168,128]{2,1,0:T(8,128)}), f32[16,168,128]{2,1,0:T(8,128)S(1)}, u32[]{:S(2)}, u32[]{:S(2)}) async-start(f32[16,168,128]{2,1,0:T(8,128)} %turn.1), calls=%async_computation | async-start | bytes 2752512 | tf_op jit(solution)/shard_map/all_to_all | solution.py:498
  15.2 1.7 copy-done.20
  19.0 8.9 %open.1 = (f32[256,2560]{1,0:T(8,128)S(1)}, f32[256,512]{1,0:T(8,128)S(1)}, bf16[256,2560]{1,0:T(8,128)(2,1)S(1)}, bf16[256,2560]{1,0:T(8,128)(2,1)S(1)}, bf16[2...) custom-call(s32[1]{0:T(128)S(6)} %copy.27.length, ...), custom_call_target="tpu_custom_call" | custom-call | tf_op jit(solution)/shard_map/open/pallas_call | solution.py:446
  35.6 7.8 %all-to-all-done.own = f32[16,168,128]{2,1,0:T(8,128)S(1)} async-done(((f32[16,168,128]{2,1,0:T(8,128)}), f32[16,168,128]{2,1,0:T(8,128)S(1)}, u32[]{:S(2)}, u32[]{:S(2)}) %all-to-all-start) | async-done | bytes 1376288 | tf_op jit(solution)/shard_map/all_to_all | solution.py:498
  43.5 2.7 collective-permute-start
  49.0 2.6 project.7
  52.9 2.6 project.6
  55.9 2.6 project.5
  59.8 5.9 %collective-permute-done.10 = f32[256,1024]{1,0:T(8,128)S(1)} collective-permute-done((f32[256,1024]{1,0:T(8,128)S(1)}, f32[256,1024]{1,0:T(8,128)S(1)}, u32[]{:S(2)}, u32[]{:S(2)}) %collective-permute-start.10) | collective-permute-done | bytes 1048608 | tf_op jit(solution)/shard_map/ppermute | solution.py:45
  66.3 2.6 project.4
  70.2 12.3 %collective-permute-done.6 = f32[256,1024]{1,0:T(8,128)S(1)} collective-permute-done((f32[256,1024]{1,0:T(8,128)S(1)}, f32[256,1024]{1,0:T(8,128)S(1)}, u32[]{:S(2)}, u32[]{:S(2)}) %collective-permute-start.6) | collective-permute-done | bytes 1048608 | tf_op jit(solution)/shard_map/ppermute | solution.py:45
  84.5 14.8 %collective-permute-done.3 = f32[256,1024]{1,0:T(8,128)S(1)} collective-permute-done((f32[256,1024]{1,0:T(8,128)S(1)}, f32[256,1024]{1,0:T(8,128)S(1)}, u32[]{:S(2)}, u32[]{:S(2)}) %collective-permute-start.3) | collective-permute-done | bytes 1048608 | tf_op jit(solution)/shard_map/ppermute | solution.py:45
  101.5 2.5 collective-permute-start.13
  104.0 11.8 %collective-permute-done.1 = f32[256,1024]{1,0:T(8,128)S(1)} collective-permute-done((f32[256,1024]{1,0:T(8,128)S(1)}, f32[256,1024]{1,0:T(8,128)S(1)}, u32[]{:S(2)}, u32[]{:S(2)}) %collective-permute-start.1) | collective-permute-done | bytes 1048608 | tf_op jit(solution)/shard_map/ppermute | solution.py:45
  116.5 2.6 collective-permute-start.9
  121.0 1.7 collective-permute-start.5
  124.3 5.0 %collective-permute-done.9 = f32[128,1024]{1,0:T(8,128)S(1)} collective-permute-done((f32[128,1024]{1,0:T(8,128)S(1)}, f32[128,1024]{1,0:T(8,128)S(1)}, u32[]{:S(2)}, u32[]{:S(2)}) %collective-permute-start.9) | collective-permute-done | bytes 524320 | tf_op jit(solution)/shard_map/ppermute | solution.py:45
  130.3 4.1 %collective-permute-done.5 = f32[128,1024]{1,0:T(8,128)S(1)} collective-permute-done((f32[128,1024]{1,0:T(8,128)S(1)}, f32[128,1024]{1,0:T(8,128)S(1)}, u32[]{:S(2)}, u32[]{:S(2)}) %collective-permute-start.5) | collective-permute-done | bytes 524320 | tf_op jit(solution)/shard_map/ppermute | solution.py:45
  134.9 17.0 %close.1 = (f32[256,2560]{1,0:T(8,128)}, f32[256,2560]{1,0:T(8,128)S(1)}, f32[256,512]{1,0:T(8,128)S(1)}, f32[128,512]{1,0:T(8,128)S(1)}, f32[128,512]{1,0:T(8,128)S(1)}) custom-call(s32[1]{0:T(128)S(6)} %copy.27.length, bf16[256,2560]{1,0:T(8,128)(2,1)S(1)} %copy-done.5, bf16[256,2560]{1,0:T(8,128)(2,1)S(1)} %copy-done.7, bf16[256,2560]{1,0:T(8,128)(2,1)S(1)} %copy-done.9, ...), custom_call_target="tpu_custom_call" | custom-call | tf_op jit(solution)/shard_map/close/pallas_call | solution.py:446
  152.8 1.9 collective-permute-start.16
  156.3 2.1 collective-permute-start.18
  158.5 4.7 %collective-permute-done.15.refs_0_.refs_4_ = f32[128,1024]{1,0:T(8,128)S(1)} collective-permute-done((f32[128,1024]{1,0:T(8,128)S(1)}, f32[128,1024]{1,0:T(8,128)S(1)}, u32[]{:S(2)}, u32[]{:S(2)}) %collective-permute-start.15) | collective-permute-done | bytes 524320 | tf_op jit(solution)/shard_map/ppermute | solution.py:45
  163.2 1.9 collective-permute-done.16
  165.1 3.4 %collective-permute-done.18.refs_2_ = f32[128,1024]{1,0:T(8,128)S(1)} collective-permute-done((f32[128,1024]{1,0:T(8,128)S(1)}, f32[128,1024]{1,0:T(8,128)S(1)}, u32[]{:S(2)}, u32[]{:S(2)}) %collective-permute-start.18) | collective-permute-done | bytes 524320 | tf_op jit(solution)/shard_map/ppermute | solution.py:45
  168.5 1.9 collective-permute-start.19
  173.6 7.3 %collective-permute-done.19 = f32[128,1024]{1,0:T(8,128)S(1)} collective-permute-done((f32[128,1024]{1,0:T(8,128)S(1)}, f32[128,1024]{1,0:T(8,128)S(1)}, u32[]{:S(2)}, u32[]{:S(2)}) %collective-permute-start.19) | collective-permute-done | bytes 524320 | tf_op jit(solution)/shard_map/ppermute | solution.py:45
  180.9 3.2 %collective-permute-start.22 = (f32[128,1024]{1,0:T(8,128)S(1)}, f32[128,1024]{1,0:T(8,128)S(1)}, u32[]{:S(2)}, u32[]{:S(2)}) collective-permute-start(f32[128,1024]{1,0:T(8,128)S(1)} %collective-permute-done.19), channel_id=1, source_target_pairs={{8,0},{9,1},{10,2},{11,3},{12,4},{13,5},{14,6},{15,7},{16,24},{17,... | collective-permute-start | bytes 1572872 | tf_op jit(solution)/shard_map/ppermute | solution.py:45
  184.4 2.0 collective-permute-start.27
  186.5 1.8 hidden_part.4
  188.3 3.2 %collective-permute-done.22 = f32[128,1024]{1,0:T(8,128)S(1)} collective-permute-done((f32[128,1024]{1,0:T(8,128)S(1)}, f32[128,1024]{1,0:T(8,128)S(1)}, u32[]{:S(2)}, u32[]{:S(2)}) %collective-permute-start.22) | collective-permute-done | bytes 524320 | tf_op jit(solution)/shard_map/ppermute | solution.py:45
  192.9 3.2 %collective-permute-start.30 = (f32[128,1024]{1,0:T(8,128)S(1)}, f32[128,1024]{1,0:T(8,128)S(1)}, u32[]{:S(2)}, u32[]{:S(2)}) collective-permute-start(f32[128,1024]{1,0:T(8,128)S(1)} %add.103.refs_0_.refs_8_), channel_id=1, source_target_pairs={{0,2},{1,5},{2,0},{3,7},{4,6},{5,1},{6,4},{7,3},{8,10},{9,13},{10,... | collective-permute-start | bytes 1572872 | tf_op jit(solution)/shard_map/ppermute | solution.py:45
  197.6 6.9 %collective-permute-done.28.refs_3_.refs_7_ = f32[128,1024]{1,0:T(8,128)S(1)} collective-permute-done((f32[128,1024]{1,0:T(8,128)S(1)}, f32[128,1024]{1,0:T(8,128)S(1)}, u32[]{:S(2)}, u32[]{:S(2)}) %collective-permute-start.28) | collective-permute-done | bytes 524320 | tf_op jit(solution)/shard_map/ppermute | solution.py:45
  204.5 1.8 hidden_part.5
  206.8 3.2 %collective-permute-start.29 = (f32[128,1024]{1,0:T(8,128)S(1)}, f32[128,1024]{1,0:T(8,128)S(1)}, u32[]{:S(2)}, u32[]{:S(2)}) collective-permute-start(f32[128,1024]{1,0:T(8,128)S(1)} %collective-permute-done.26.refs_1_.refs_13_), channel_id=1, source_target_pairs={{0,2},{1,5},{2,0},{3,7},{4,6},{5,1},{6,4},{7,3},{8,10},{9,13},{10,... | collective-permute-start | bytes 1572872 | tf_op jit(solution)/shard_map/ppermute | solution.py:45
  210.0 9.5 %collective-permute-start.32 = (f32[4,160,128]{2,1,0:T(8,128)S(1)}, f32[4,160,128]{2,1,0:T(8,128)S(1)}, u32[]{:S(2)}, u32[]{:S(2)}) collective-permute-start(f32[4,160,128]{2,1,0:T(8,128)S(1)} %get-tuple-element.142), channel_id=1, source_target_pairs={{0,1},{1,0},{2,3},{3,2},{4,5},{5,4},{6,7},{7,6},{8,9},{9,8},{10,11... | collective-permute-start | bytes 983048 | tf_op jit(solution)/shard_map/ppermute | solution.py:609
  219.6 1.8 collective-permute-done.31.refs_3_.refs_11_
  221.4 1.8 hidden_part.6
  227.0 5.6 %collective-permute-done.29.refs_1_.refs_15_ = f32[128,1024]{1,0:T(8,128)S(1)} collective-permute-done((f32[128,1024]{1,0:T(8,128)S(1)}, f32[128,1024]{1,0:T(8,128)S(1)}, u32[]{:S(2)}, u32[]{:S(2)}) %collective-permute-start.29) | collective-permute-done | bytes 524320 | tf_op jit(solution)/shard_map/ppermute | solution.py:45
  237.7 5.7 %all-to-all-start.1 = ((f32[16,160,128]{2,1,0:T(8,128)}), f32[16,160,128]{2,1,0:T(8,128)S(1)}, u32[]{:S(2)}, u32[]{:S(2)}) async-start(f32[16,160,128]{2,1,0:T(8,128)} %copy-done.3), calls=%async_computation.1 | async-start | bytes 2621440 | tf_op jit(solution)/shard_map/all_to_all | solution.py:616
  243.5 1.7 copy-done.24
  248.5 13.3 %finish.1 = (f32[256,2560]{1,0:T(8,128)}, f32[256,512]{1,0:T(8,128)}, f32[256,512]{1,0:T(8,128)}) custom-call(s32[1]{0:T(128)S(6)} %copy.27.length, bf16[256,2560]{1,0:T(8,128)(2,1)} %copy-done.4, bf16[256,2560]{1,0:T(8,128)(2,1)} %copy-done.6, bf16[256,2560]{1,0:T(8,128)(2,1)} %copy-done.8, bf16[256,2560]{1,0:T(8,128)(2,1)} %copy-done.10, ...), custom_call_target="tpu_custom_call" | custom-call | tf_op jit(solution)/shard_map/finish/pallas_call | solution.py:446
  261.9 6.6 %weight_grad.1 = (f32[320,512]{1,0:T(8,128)}, f32[320,512]{1,0:T(8,128)}) custom-call(s32[16]{0:T(128)S(1)} %get-tuple-element.195.listed, s32[1]{0:T(128)} %bitcast.core, f32[16,168,128]{2,1,0:T(8,128)S(1)} %all-to-all-done.own, f32[16,168,128]{2,1,0:T(8,128)} %collective-permute-done.other, f32[128,1024]{1,0:T(8,128)S(1)} %copy-done.19, ...), custom_call_target="tpu_custom_call" | custom-call | tf_op jit(solution)/shard_map/weight_grad/pallas_call | solution.py:155
  268.4 5.1 %all-to-all-done.1.own = f32[16,160,128]{2,1,0:T(8,128)S(1)} async-done(((f32[16,160,128]{2,1,0:T(8,128)}), f32[16,160,128]{2,1,0:T(8,128)S(1)}, u32[]{:S(2)}, u32[]{:S(2)}) %all-to-all-start.1) | async-done | bytes 1310752 | tf_op jit(solution)/shard_map/all_to_all | solution.py:616
  273.6 2.5 collective-permute-start.36
  276.1 1.7 collective-permute-done.36.other
  277.8 2.0 turn_back.1
  (208 shorter events, 50.9 us)
Async XLA Ops:
  5.4 38.1 %all-to-all-start = ((f32[16,168,128]{2,1,0:T(8,128)}), f32[16,168,128]{2,1,0:T(8,128)S(1)}, u32[]{:S(2)}, u32[]{:S(2)}) async-start(f32[16,168,128]{2,1,0:T(8,128)} %turn.1), calls=%async_computation | async-start | bytes 2752512 | tf_op jit(solution)/shard_map/all_to_all | solution.py:498
  19.0 27.2 %copy-start.65 = (s32[4]{0:T(128)S(1)}, s32[4]{0:T(128)}, u32[]{:S(2)}) copy-start(s32[4]{0:T(128)} %constant.54.clone) | copy-start | bytes 52
  19.0 27.4 %copy-start.61 = (s32[4,4]{1,0:T(4,128)S(1)}, s32[4,4]{1,0:T(4,128)}, u32[]{:S(2)}) copy-start(s32[4,4]{1,0:T(4,128)} %constant.50.clone) | copy-start | bytes 196
  43.5 5.6 %collective-permute-start = (f32[16,168,128]{2,1,0:T(8,128)S(1)}, f32[16,168,128]{2,1,0:T(8,128)}, u32[]{:S(2)}, u32[]{:S(2)}) collective-permute-start(f32[16,168,128]{2,1,0:T(8,128)S(1)} %all-to-all-done.own), channel_id=1, source_target_pairs={{0,1},{1,0},{2,3},{3,2},{4,5},{5,4},{6,7},{7,6},{8,9},{9,8},{10,11... | collective-permute-start | bytes 4128776 | tf_op jit(solution)/shard_map/ppermute | solution.py:528
  51.7 14.0 %collective-permute-start.10 = (f32[256,1024]{1,0:T(8,128)S(1)}, f32[256,1024]{1,0:T(8,128)S(1)}, u32[]{:S(2)}, u32[]{:S(2)}) collective-permute-start(f32[256,1024]{1,0:T(8,128)S(1)} %get-tuple-element.122), channel_id=1, source_target_pairs={{0,2},{1,5},{2,0},{3,7},{4,6},{5,1},{6,4},{7,3},{8,10},{9,13},{10,... | collective-permute-start | bytes 3145736 | tf_op jit(solution)/shard_map/ppermute | solution.py:45
  55.6 27.0 %collective-permute-start.6 = (f32[256,1024]{1,0:T(8,128)S(1)}, f32[256,1024]{1,0:T(8,128)S(1)}, u32[]{:S(2)}, u32[]{:S(2)}) collective-permute-start(f32[256,1024]{1,0:T(8,128)S(1)} %get-tuple-element.120), channel_id=1, source_target_pairs={{0,2},{1,5},{2,0},{3,7},{4,6},{5,1},{6,4},{7,3},{8,10},{9,13},{10,... | collective-permute-start | bytes 3145736 | tf_op jit(solution)/shard_map/ppermute | solution.py:45
  58.5 40.8 %collective-permute-start.3 = (f32[256,1024]{1,0:T(8,128)S(1)}, f32[256,1024]{1,0:T(8,128)S(1)}, u32[]{:S(2)}, u32[]{:S(2)}) collective-permute-start(f32[256,1024]{1,0:T(8,128)S(1)} %get-tuple-element.118), channel_id=1, source_target_pairs={{0,2},{1,5},{2,0},{3,7},{4,6},{5,1},{6,4},{7,3},{8,10},{9,13},{10,... | collective-permute-start | bytes 3145736 | tf_op jit(solution)/shard_map/ppermute | solution.py:45
  65.8 17.4 %collective-permute-start.11 = (f32[128,1024]{1,0:T(8,128)S(1)}, f32[128,1024]{1,0:T(8,128)S(1)}, u32[]{:S(2)}, u32[]{:S(2)}) collective-permute-start(f32[128,1024]{1,0:T(8,128)S(1)} %slice_add_fusion), channel_id=1, source_target_pairs={{0,4},{1,3},{2,6},{3,1},{4,0},{5,7},{6,2},{7,5},{8,12},{9,11},{10,... | collective-permute-start | bytes 1572872 | tf_op jit(solution)/shard_map/ppermute | solution.py:45
  68.9 46.9 %collective-permute-start.1 = (f32[256,1024]{1,0:T(8,128)S(1)}, f32[256,1024]{1,0:T(8,128)S(1)}, u32[]{:S(2)}, u32[]{:S(2)}) collective-permute-start(f32[256,1024]{1,0:T(8,128)S(1)} %get-tuple-element.116), channel_id=1, source_target_pairs={{0,2},{1,5},{2,0},{3,7},{4,6},{5,1},{6,4},{7,3},{8,10},{9,13},{10,... | collective-permute-start | bytes 3145736 | tf_op jit(solution)/shard_map/ppermute | solution.py:45
  82.6 16.9 %collective-permute-start.7 = (f32[128,1024]{1,0:T(8,128)S(1)}, f32[128,1024]{1,0:T(8,128)S(1)}, u32[]{:S(2)}, u32[]{:S(2)}) collective-permute-start(f32[128,1024]{1,0:T(8,128)S(1)} %slice_add_fusion.2), channel_id=1, source_target_pairs={{0,4},{1,3},{2,6},{3,1},{4,0},{5,7},{6,2},{7,5},{8,12},{9,11},{10,... | collective-permute-start | bytes 1572872 | tf_op jit(solution)/shard_map/ppermute | solution.py:45
  83.2 18.2 %collective-permute-start.12 = (f32[128,1024]{1,0:T(8,128)S(1)}, f32[128,1024]{1,0:T(8,128)S(1)}, u32[]{:S(2)}, u32[]{:S(2)}) collective-permute-start(f32[128,1024]{1,0:T(8,128)S(1)} %fusion), channel_id=1, source_target_pairs={{0,8},{1,9},{2,10},{3,11},{4,12},{5,13},{6,14},{7,15},{24,16},{25,... | collective-permute-start | bytes 1572872 | tf_op jit(solution)/shard_map/ppermute | solution.py:45
  99.6 16.8 %collective-permute-start.8 = (f32[128,1024]{1,0:T(8,128)S(1)}, f32[128,1024]{1,0:T(8,128)S(1)}, u32[]{:S(2)}, u32[]{:S(2)}) collective-permute-start(f32[128,1024]{1,0:T(8,128)S(1)} %fusion.1), channel_id=1, source_target_pairs={{0,8},{1,9},{2,10},{3,11},{4,12},{5,13},{6,14},{7,15},{24,16},{25,... | collective-permute-start | bytes 1572872 | tf_op jit(solution)/shard_map/ppermute | solution.py:45
  100.9 18.3 %collective-permute-start.4 = (f32[128,1024]{1,0:T(8,128)S(1)}, f32[128,1024]{1,0:T(8,128)S(1)}, u32[]{:S(2)}, u32[]{:S(2)}) collective-permute-start(f32[128,1024]{1,0:T(8,128)S(1)} %slice_add_fusion.4), channel_id=1, source_target_pairs={{0,4},{1,3},{2,6},{3,1},{4,0},{5,7},{6,2},{7,5},{8,12},{9,11},{10,... | collective-permute-start | bytes 1572872 | tf_op jit(solution)/shard_map/ppermute | solution.py:45
  101.5 17.7 %collective-permute-start.13 = (f32[128,1024]{1,0:T(8,128)S(1)}, f32[128,1024]{1,0:T(8,128)S(1)}, u32[]{:S(2)}, u32[]{:S(2)}) collective-permute-start(f32[128,1024]{1,0:T(8,128)S(1)} %add.100), channel_id=1, source_target_pairs={{8,16},{9,17},{10,18},{11,19},{12,20},{13,21},{14,22},{15,23},{16,... | collective-permute-start | bytes 1572872 | tf_op jit(solution)/shard_map/ppermute | solution.py:45
  115.9 8.4 %collective-permute-start.2 = (f32[128,1024]{1,0:T(8,128)S(1)}, f32[128,1024]{1,0:T(8,128)S(1)}, u32[]{:S(2)}, u32[]{:S(2)}) collective-permute-start(f32[128,1024]{1,0:T(8,128)S(1)} %slice_add_fusion.6), channel_id=1, source_target_pairs={{0,4},{1,3},{2,6},{3,1},{4,0},{5,7},{6,2},{7,5},{8,12},{9,11},{10,... | collective-permute-start | bytes 1572872 | tf_op jit(solution)/shard_map/ppermute | solution.py:45
  116.5 12.8 %collective-permute-start.9 = (f32[128,1024]{1,0:T(8,128)S(1)}, f32[128,1024]{1,0:T(8,128)S(1)}, u32[]{:S(2)}, u32[]{:S(2)}) collective-permute-start(f32[128,1024]{1,0:T(8,128)S(1)} %add.95), channel_id=1, source_target_pairs={{8,16},{9,17},{10,18},{11,19},{12,20},{13,21},{14,22},{15,23},{16,... | collective-permute-start | bytes 1572872 | tf_op jit(solution)/shard_map/ppermute | solution.py:45
  119.4 10.9 %collective-permute-start.14 = (f32[128,1024]{1,0:T(8,128)S(1)}, f32[128,1024]{1,0:T(8,128)S(1)}, u32[]{:S(2)}, u32[]{:S(2)}) collective-permute-start(f32[128,1024]{1,0:T(8,128)S(1)} %get-tuple-element.198), channel_id=1, source_target_pairs={{8,0},{9,1},{10,2},{11,3},{12,4},{13,5},{14,6},{15,7},{16,24},{17,... | collective-permute-start | bytes 1572872 | tf_op jit(solution)/shard_map/ppermute | solution.py:45
  121.0 13.5 %collective-permute-start.5 = (f32[128,1024]{1,0:T(8,128)S(1)}, f32[128,1024]{1,0:T(8,128)S(1)}, u32[]{:S(2)}, u32[]{:S(2)}) collective-permute-start(f32[128,1024]{1,0:T(8,128)S(1)} %get-tuple-element.199), channel_id=1, source_target_pairs={{0,8},{1,9},{2,10},{3,11},{4,12},{5,13},{6,14},{7,15},{24,16},{25,... | collective-permute-start | bytes 1572872 | tf_op jit(solution)/shard_map/ppermute | solution.py:45
  152.7 35.6 %copy-start.23 = (f32[256,2560]{1,0:T(8,128)}, f32[256,2560]{1,0:T(8,128)S(1)}, u32[]{:S(2)}) copy-start(f32[256,2560]{1,0:T(8,128)S(1)} %get-tuple-element.163.grad_scores) | copy-start | bytes 7864324
  152.7 35.6 %copy-start.18 = (f32[128,1024]{1,0:T(8,128)}, f32[128,1024]{1,0:T(8,128)S(1)}, u32[]{:S(2)}) copy-start(f32[128,1024]{1,0:T(8,128)S(1)} %constant_dynamic-update-slice_fusion.refs_0_) | copy-start | bytes 1572868
  152.7 10.5 %collective-permute-start.15 = (f32[128,1024]{1,0:T(8,128)S(1)}, f32[128,1024]{1,0:T(8,128)S(1)}, u32[]{:S(2)}, u32[]{:S(2)}) collective-permute-start(f32[128,1024]{1,0:T(8,128)S(1)} %constant_dynamic-update-slice_fusion.refs_0_), channel_id=1, source_target_pairs={{0,8},{1,9},{2,10},{3,11},{4,12},{5,13},{6,14},{7,15},{8,0},{9,1},... | collective-permute-start | bytes 1572872 | tf_op jit(solution)/shard_map/ppermute | solution.py:45
  152.8 12.3 %collective-permute-start.16 = (f32[128,1024]{1,0:T(8,128)S(1)}, f32[128,1024]{1,0:T(8,128)S(1)}, u32[]{:S(2)}, u32[]{:S(2)}) collective-permute-start(f32[128,1024]{1,0:T(8,128)S(1)} %constant_dynamic-update-slice_fusion.refs_0_), channel_id=1, source_target_pairs={{8,16},{9,17},{10,18},{11,19},{12,20},{13,21},{14,22},{15,23},{16,... | collective-permute-start | bytes 1572872 | tf_op jit(solution)/shard_map/ppermute | solution.py:45
  154.7 10.4 %collective-permute-start.17 = (f32[128,1024]{1,0:T(8,128)S(1)}, f32[128,1024]{1,0:T(8,128)S(1)}, u32[]{:S(2)}, u32[]{:S(2)}) collective-permute-start(f32[128,1024]{1,0:T(8,128)S(1)} %constant_dynamic-update-slice_fusion.refs_0_), channel_id=1, source_target_pairs={{0,4},{1,3},{2,6},{3,1},{4,0},{5,7},{6,2},{7,5},{8,12},{9,11},{10,... | collective-permute-start | bytes 1572872 | tf_op jit(solution)/shard_map/ppermute | solution.py:45
  156.3 12.2 %collective-permute-start.18 = (f32[128,1024]{1,0:T(8,128)S(1)}, f32[128,1024]{1,0:T(8,128)S(1)}, u32[]{:S(2)}, u32[]{:S(2)}) collective-permute-start(f32[128,1024]{1,0:T(8,128)S(1)} %constant_dynamic-update-slice_fusion.refs_0_), channel_id=1, source_target_pairs={{0,2},{1,5},{2,0},{3,7},{4,6},{5,1},{6,4},{7,3},{8,10},{9,13},{10,... | collective-permute-start | bytes 1572872 | tf_op jit(solution)/shard_map/ppermute | solution.py:45
  163.2 41.3 %copy-start.29 = (f32[128,1024]{1,0:T(8,128)}, f32[128,1024]{1,0:T(8,128)S(1)}, u32[]{:S(2)}) copy-start(f32[128,1024]{1,0:T(8,128)S(1)} %collective-permute-done.15.refs_0_.refs_4_) | copy-start | bytes 1572868
  168.5 12.4 %collective-permute-start.19 = (f32[128,1024]{1,0:T(8,128)S(1)}, f32[128,1024]{1,0:T(8,128)S(1)}, u32[]{:S(2)}, u32[]{:S(2)}) collective-permute-start(f32[128,1024]{1,0:T(8,128)S(1)} %collective-permute-done.15.refs_0_.refs_4_), channel_id=1, source_target_pairs={{8,16},{9,17},{10,18},{11,19},{12,20},{13,21},{14,22},{15,23},{16,... | collective-permute-start | bytes 1572872 | tf_op jit(solution)/shard_map/ppermute | solution.py:45
  170.4 10.5 %collective-permute-start.20 = (f32[128,1024]{1,0:T(8,128)S(1)}, f32[128,1024]{1,0:T(8,128)S(1)}, u32[]{:S(2)}, u32[]{:S(2)}) collective-permute-start(f32[128,1024]{1,0:T(8,128)S(1)} %collective-permute-done.16), channel_id=1, source_target_pairs={{8,0},{9,1},{10,2},{11,3},{12,4},{13,5},{14,6},{15,7},{16,24},{17,... | collective-permute-start | bytes 1572872 | tf_op jit(solution)/shard_map/ppermute | solution.py:45
  171.7 9.2 %collective-permute-start.21 = (f32[128,1024]{1,0:T(8,128)S(1)}, f32[128,1024]{1,0:T(8,128)S(1)}, u32[]{:S(2)}, u32[]{:S(2)}) collective-permute-start(f32[128,1024]{1,0:T(8,128)S(1)} %collective-permute-done.15.refs_0_.refs_4_), channel_id=1, source_target_pairs={{0,4},{1,3},{2,6},{3,1},{4,0},{5,7},{6,2},{7,5},{8,12},{9,11},{10,... | collective-permute-start | bytes 1572872 | tf_op jit(solution)/shard_map/ppermute | solution.py:45
  172.2 14.3 %collective-permute-start.24 = (f32[128,1024]{1,0:T(8,128)S(1)}, f32[128,1024]{1,0:T(8,128)S(1)}, u32[]{:S(2)}, u32[]{:S(2)}) collective-permute-start(f32[128,1024]{1,0:T(8,128)S(1)} %collective-permute-done.17.refs_1_), channel_id=1, source_target_pairs={{0,2},{1,5},{2,0},{3,7},{4,6},{5,1},{6,4},{7,3},{8,10},{9,13},{10,... | collective-permute-start | bytes 1572872 | tf_op jit(solution)/shard_map/ppermute | solution.py:45
  180.9 23.6 %copy-start.35 = (f32[128,1024]{1,0:T(8,128)}, f32[128,1024]{1,0:T(8,128)S(1)}, u32[]{:S(2)}) copy-start(f32[128,1024]{1,0:T(8,128)S(1)} %collective-permute-done.21.refs_1_.refs_5_) | copy-start | bytes 1572868
  180.9 10.6 %collective-permute-start.22 = (f32[128,1024]{1,0:T(8,128)S(1)}, f32[128,1024]{1,0:T(8,128)S(1)}, u32[]{:S(2)}, u32[]{:S(2)}) collective-permute-start(f32[128,1024]{1,0:T(8,128)S(1)} %collective-permute-done.19), channel_id=1, source_target_pairs={{8,0},{9,1},{10,2},{11,3},{12,4},{13,5},{14,6},{15,7},{16,24},{17,... | collective-permute-start | bytes 1572872 | tf_op jit(solution)/shard_map/ppermute | solution.py:45
  184.3 37.1 %copy-start.14 = (f32[128,1024]{1,0:T(8,128)}, f32[128,1024]{1,0:T(8,128)S(1)}, u32[]{:S(2)}) copy-start(f32[128,1024]{1,0:T(8,128)S(1)} %add.103.refs_0_.refs_8_) | copy-start | bytes 1572868
  184.3 8.4 %collective-permute-start.23 = (f32[128,1024]{1,0:T(8,128)S(1)}, f32[128,1024]{1,0:T(8,128)S(1)}, u32[]{:S(2)}, u32[]{:S(2)}) collective-permute-start(f32[128,1024]{1,0:T(8,128)S(1)} %add.103.refs_0_.refs_8_), channel_id=1, source_target_pairs={{0,4},{1,3},{2,6},{3,1},{4,0},{5,7},{6,2},{7,5},{8,12},{9,11},{10,... | collective-permute-start | bytes 1572872 | tf_op jit(solution)/shard_map/ppermute | solution.py:45
  184.4 11.8 %collective-permute-start.27 = (f32[128,1024]{1,0:T(8,128)S(1)}, f32[128,1024]{1,0:T(8,128)S(1)}, u32[]{:S(2)}, u32[]{:S(2)}) collective-permute-start(f32[128,1024]{1,0:T(8,128)S(1)} %collective-permute-done.15.refs_0_.refs_4_), channel_id=1, source_target_pairs={{0,2},{1,5},{2,0},{3,7},{4,6},{5,1},{6,4},{7,3},{8,10},{9,13},{10,... | collective-permute-start | bytes 1572872 | tf_op jit(solution)/shard_map/ppermute | solution.py:45
  186.4 18.1 %collective-permute-start.28 = (f32[128,1024]{1,0:T(8,128)S(1)}, f32[128,1024]{1,0:T(8,128)S(1)}, u32[]{:S(2)}, u32[]{:S(2)}) collective-permute-start(f32[128,1024]{1,0:T(8,128)S(1)} %collective-permute-done.21.refs_1_.refs_5_), channel_id=1, source_target_pairs={{0,2},{1,5},{2,0},{3,7},{4,6},{5,1},{6,4},{7,3},{8,10},{9,13},{10,... | collective-permute-start | bytes 1572872 | tf_op jit(solution)/shard_map/ppermute | solution.py:45
  192.7 28.7 %copy-start.39 = (f32[128,1024]{1,0:T(8,128)}, f32[128,1024]{1,0:T(8,128)S(1)}, u32[]{:S(2)}) copy-start(f32[128,1024]{1,0:T(8,128)S(1)} %collective-permute-done.23.refs_1_.refs_9_) | copy-start | bytes 1572868
  192.7 31.2 %copy-start.16 = (f32[128,1024]{1,0:T(8,128)}, f32[128,1024]{1,0:T(8,128)S(1)}, u32[]{:S(2)}) copy-start(f32[128,1024]{1,0:T(8,128)S(1)} %add.104.refs_0_.refs_12_) | copy-start | bytes 1572868
  192.8 14.1 %collective-permute-start.26 = (f32[128,1024]{1,0:T(8,128)S(1)}, f32[128,1024]{1,0:T(8,128)S(1)}, u32[]{:S(2)}, u32[]{:S(2)}) collective-permute-start(f32[128,1024]{1,0:T(8,128)S(1)} %add.104.refs_0_.refs_12_), channel_id=1, source_target_pairs={{0,4},{1,3},{2,6},{3,1},{4,0},{5,7},{6,2},{7,5},{8,12},{9,11},{10,... | collective-permute-start | bytes 1572872 | tf_op jit(solution)/shard_map/ppermute | solution.py:45
  192.9 26.6 %collective-permute-start.30 = (f32[128,1024]{1,0:T(8,128)S(1)}, f32[128,1024]{1,0:T(8,128)S(1)}, u32[]{:S(2)}, u32[]{:S(2)}) collective-permute-start(f32[128,1024]{1,0:T(8,128)S(1)} %add.103.refs_0_.refs_8_), channel_id=1, source_target_pairs={{0,2},{1,5},{2,0},{3,7},{4,6},{5,1},{6,4},{7,3},{8,10},{9,13},{10,... | collective-permute-start | bytes 1572872 | tf_op jit(solution)/shard_map/ppermute | solution.py:45
  196.1 25.3 %collective-permute-start.31 = (f32[128,1024]{1,0:T(8,128)S(1)}, f32[128,1024]{1,0:T(8,128)S(1)}, u32[]{:S(2)}, u32[]{:S(2)}) collective-permute-start(f32[128,1024]{1,0:T(8,128)S(1)} %collective-permute-done.23.refs_1_.refs_9_), channel_id=1, source_target_pairs={{0,2},{1,5},{2,0},{3,7},{4,6},{5,1},{6,4},{7,3},{8,10},{9,13},{10,... | collective-permute-start | bytes 1572872 | tf_op jit(solution)/shard_map/ppermute | solution.py:45
  196.2 30.8 %collective-permute-start.25 = (f32[128,1024]{1,0:T(8,128)S(1)}, f32[128,1024]{1,0:T(8,128)S(1)}, u32[]{:S(2)}, u32[]{:S(2)}) collective-permute-start(f32[128,1024]{1,0:T(8,128)S(1)} %add.104.refs_0_.refs_12_), channel_id=1, source_target_pairs={{0,2},{1,5},{2,0},{3,7},{4,6},{5,1},{6,4},{7,3},{8,10},{9,13},{10,... | collective-permute-start | bytes 1572872 | tf_op jit(solution)/shard_map/ppermute | solution.py:45
  206.8 25.8 %collective-permute-start.29 = (f32[128,1024]{1,0:T(8,128)S(1)}, f32[128,1024]{1,0:T(8,128)S(1)}, u32[]{:S(2)}, u32[]{:S(2)}) collective-permute-start(f32[128,1024]{1,0:T(8,128)S(1)} %collective-permute-done.26.refs_1_.refs_13_), channel_id=1, source_target_pairs={{0,2},{1,5},{2,0},{3,7},{4,6},{5,1},{6,4},{7,3},{8,10},{9,13},{10,... | collective-permute-start | bytes 1572872 | tf_op jit(solution)/shard_map/ppermute | solution.py:45
  210.0 15.2 %collective-permute-start.32 = (f32[4,160,128]{2,1,0:T(8,128)S(1)}, f32[4,160,128]{2,1,0:T(8,128)S(1)}, u32[]{:S(2)}, u32[]{:S(2)}) collective-permute-start(f32[4,160,128]{2,1,0:T(8,128)S(1)} %get-tuple-element.142), channel_id=1, source_target_pairs={{0,1},{1,0},{2,3},{3,2},{4,5},{5,4},{6,7},{7,6},{8,9},{9,8},{10,11... | collective-permute-start | bytes 983048 | tf_op jit(solution)/shard_map/ppermute | solution.py:609
  219.5 7.5 %collective-permute-start.33 = (f32[4,160,128]{2,1,0:T(8,128)S(1)}, f32[4,160,128]{2,1,0:T(8,128)S(1)}, u32[]{:S(2)}, u32[]{:S(2)}) collective-permute-start(f32[4,160,128]{2,1,0:T(8,128)S(1)} %get-tuple-element.144), channel_id=1, source_target_pairs={{0,1},{1,0},{2,3},{3,2},{4,5},{5,4},{6,7},{7,6},{8,9},{9,8},{10,11... | collective-permute-start | bytes 983048 | tf_op jit(solution)/shard_map/ppermute | solution.py:609
  223.2 3.8 %collective-permute-start.34 = (f32[4,160,128]{2,1,0:T(8,128)S(1)}, f32[4,160,128]{2,1,0:T(8,128)S(1)}, u32[]{:S(2)}, u32[]{:S(2)}) collective-permute-start(f32[4,160,128]{2,1,0:T(8,128)S(1)} %get-tuple-element.147), channel_id=1, source_target_pairs={{0,1},{1,0},{2,3},{3,2},{4,5},{5,4},{6,7},{7,6},{8,9},{9,8},{10,11... | collective-permute-start | bytes 983048 | tf_op jit(solution)/shard_map/ppermute | solution.py:609
  233.9 2.0 collective-permute-start.35
  237.7 35.8 %all-to-all-start.1 = ((f32[16,160,128]{2,1,0:T(8,128)}), f32[16,160,128]{2,1,0:T(8,128)S(1)}, u32[]{:S(2)}, u32[]{:S(2)}) async-start(f32[16,160,128]{2,1,0:T(8,128)} %copy-done.3), calls=%async_computation.1 | async-start | bytes 2621440 | tf_op jit(solution)/shard_map/all_to_all | solution.py:616
  273.6 4.2 %collective-permute-start.36 = (f32[8,160,128]{2,1,0:T(8,128)S(1)}, f32[8,160,128]{2,1,0:T(8,128)S(1)}, u32[]{:S(2)}, u32[]{:S(2)}) collective-permute-start(f32[8,160,128]{2,1,0:T(8,128)S(1)} %slice_select_fusion), channel_id=1, source_target_pairs={{0,1},{1,0},{2,3},{3,2},{4,5},{5,4},{6,7},{7,6},{8,9},{9,8},{10,11... | collective-permute-start | bytes 1966088 | tf_op jit(solution)/shard_map/ppermute | solution.py:627
  (57 other events, 513.9 us)
